TPU v7x, 32 devices: a whole 2x2x4 slice. The times are simulated.
32 devices in a mesh: row: 8 (over y, x, core), col: 4 (over z).
Axes of the slice: x: 2, y: 2, z: 4, core: 2. Of those that a mesh axis runs over, the one named last changes fastest.
Arguments:
- upper_block: float32 [2, 1024, 1024], P(None, 'row', 'col'), may hold values from -0.1875 to 0.1875
- block_inverse: float32 [2, 1024, 128], P(None, 'row'), may hold values from -0.25 to 0.25
- panel_rhs: float32 [2, 32, 1024], P(None, None, 'row'), may hold values from -6 to 6
- upper_trail: float32 [2, 1024, 65536], P(None, 'row', 'col'), may hold values from -0.125 to 0.125
- trail_rhs: float32 [2, 32, 65536], P(None, None, ('col', 'row')), may hold values from -6 to 6
- currents: float32 [2, 1024], P(None, 'row'), may hold values from -4 to 4
- owner: int32 [1024], P('row'), may hold values from 0 to 127
Outputs:
- panel_adjoint: float32 [2, 32, 1024], P(None, None, 'row')
- trail_updated: float32 [2, 32, 65536], P(None, None, ('col', 'row'))
- patch_gradient: float32 [128], P(('row', 'col'))
Inputs may be any that keep to these rules, and one draw needn't show every extreme that they name: owner names a surface patch for each panel unknown.
All inputs are finite; a program needn't handle non-finite values.
Results may differ from a plain program's by a relative error of at most 0.0003.
Values sent between devices are 32-bit elements; how exact they have to be, the bound alone decides.
No kernel may reach another device: no remote copies, remote signals or barrier semaphores. Data moves between devices by JAX's collectives and lax.ppermute only.
A program may use at most 64 MiB of HBM per device.

v0:
```python
import jax
import jax.numpy as jnp
from jax import lax
from jax.sharding import PartitionSpec as P

PATCH_DEV = 4


highest = lax.Precision.HIGHEST


def shifted(block, axis, distance):
    devices = range(lax.axis_size(axis))
    route = [(i - distance, i) for i in devices if i - distance in devices]
    return lax.ppermute(block, axis, route)


def from_root(value, axis, source):
    kept = jnp.where(lax.axis_index(axis) == source, value, 0).astype(value.dtype)
    return lax.psum(kept, axis)


def product_high(first, second):
    return jnp.dot(first, second, precision=highest, preferred_element_type=jnp.float32)


def conj_product(left, right):
    real_part = product_high(left[0], right[0]) + product_high(left[1], right[1])
    imag_part = product_high(left[1], right[0]) - product_high(left[0], right[1])
    return jnp.stack([real_part, imag_part])


def on_device(upper_block, block_inverse, panel_rhs, upper_trail, trail_rhs, currents, owner):
    rows_count = lax.axis_size("row")
    cols_count = lax.axis_size("col")
    row_index = lax.axis_index("row")
    col_index = lax.axis_index("col")
    width = block_inverse.shape[1]
    quarter = upper_block.shape[2]
    observers = panel_rhs.shape[1]
    offset = row_index * width % quarter
    root_col = row_index * width // quarter

    def advance(index, carry):
        held, solved = carry
        incoming = shifted(held, "row", 1)
        local = lax.dynamic_slice_in_dim(incoming, offset, width, 2)
        candidate = conj_product(panel_rhs - local, block_inverse)
        shared = from_root(candidate, "col", root_col)
        update = conj_product(shared, upper_block)
        active = row_index == index
        held = jnp.where(active, incoming + update, held)
        solved = jnp.where(active, shared, solved)
        return (held, solved)

    held_start = jnp.zeros((2, observers, quarter), jnp.float32)
    solved_start = jnp.zeros((2, observers, width), jnp.float32)
    solved = lax.fori_loop(0, rows_count, advance, (held_start, solved_start))[1]
    term = conj_product(solved, upper_trail)
    reduced = lax.psum_scatter(term, "row", scatter_dimension=2, tiled=True)
    updated = trail_rhs - reduced
    share = width // cols_count
    start = col_index * share
    mine = lax.dynamic_slice_in_dim(solved, start, share, 2)
    total = jnp.sum(mine, axis=1)
    current_part = lax.dynamic_slice_in_dim(currents, start, share, 1)
    owner_part = lax.dynamic_slice_in_dim(owner, start, share, 0)
    partial_value = current_part[0] * total[0] - current_part[1] * total[1]
    patch_count = PATCH_DEV * rows_count * cols_count
    patch_ids = lax.broadcasted_iota(jnp.int32, (share, patch_count), 1)
    selector = (owner_part[:, None] == patch_ids).astype(jnp.float32)
    spread = product_high(partial_value[None, :], selector)[0]
    gradient = lax.psum_scatter(spread, ("row", "col"), scatter_dimension=0, tiled=True)
    return (solved, updated, gradient)


def solution(mesh):
    in_specs = (
        P(None, "row", "col"),
        P(None, "row", None),
        P(None, None, "row"),
        P(None, "row", "col"),
        P(None, None, ("col", "row")),
        P(None, "row"),
        P("row"),
    )
    out_specs = (P(None, None, "row"), P(None, None, ("col", "row")), P(("row", "col")))
    return jax.shard_map(
        on_device, mesh=mesh, in_specs=in_specs, out_specs=out_specs, check_vma=False
    )
```

profile of v0, /device:TPU:0, one launch (start us, length us, event | category | flops | bytes accessed | tf_op | source)
XLA Modules:
  0.0 354.7 jit_solution(6087188050505130230)
XLA Ops:
  7.3 249.4 %while.18 = (s32[]{:T(128)}, f32[2,32,256]{2,1,0:T(8,128)S(1)}, f32[2,32,128]{2,1,0:T(8,128)S(1)}, s32[]{:T(128)}, s32[]{:T(128)}, /*index=5*/s32[]{:T(128)}, f3...) while((s32[]{:T(128)}, f32[2,32,256]{2,1,0:T(8,128)S(1)}, ...), condition=%wide.region_2.3_spmd.clone, body=%wide.region_0.2_spmd.clone.sunk | while | flops 75653120 | bytes 2195678 | solution.py:58
  7.3 2.4 collective-permute-start
  15.5 20.1 %psum.16 = f32[2,32,128]{2,1,0:T(8,128)S(1)} all-reduce(f32[2,32,128]{2,1,0:T(8,128)S(1)} %maximum_select_fusion.2), channel_id=1, replica_groups=mesh['row'=8,'col'=4] {'col'}, use_global_device_ids=true, to_apply=%region_1.1 | all-reduce | flops 8192 | bytes 65536 | tf_op jit(solution)/shard_map/while/body/eval_jaxpr/psum | solution.py:20
  35.6 1.1 fusion.83
  37.8 1.1 fusion.84
  38.9 1.1 fusion.82
  40.0 1.3 collective-permute-start
  47.1 15.8 %psum.16 = f32[2,32,128]{2,1,0:T(8,128)S(1)} all-reduce(f32[2,32,128]{2,1,0:T(8,128)S(1)} %maximum_select_fusion.2), channel_id=1, replica_groups=mesh['row'=8,'col'=4] {'col'}, use_global_device_ids=true, to_apply=%region_1.1 | all-reduce | flops 8192 | bytes 65536 | tf_op jit(solution)/shard_map/while/body/eval_jaxpr/psum | solution.py:20
  63.0 1.1 fusion.83
  65.2 1.1 fusion.84
  66.2 1.1 fusion.82
  67.4 4.1 %collective-permute-start = (f32[2,32,256]{2,1,0:T(8,128)S(1)}, f32[2,32,256]{2,1,0:T(8,128)S(1)}, u32[]{:S(2)}, u32[]{:S(2)}) collective-permute-start(f32[2,32,256]{2,1,0:T(8,128)S(1)} %broadcast_select_fusion.2), channel_id=1, source_target_pairs={{0,4},{4,8},{8,12},{12,16},{16,20},{20,24},{24,28},{1,5},{5,9},{9,... | collective-permute-start | bytes 196616 | tf_op jit(solution)/shard_map/while/body/eval_jaxpr/ppermute | solution.py:15
  77.3 17.4 %psum.16 = f32[2,32,128]{2,1,0:T(8,128)S(1)} all-reduce(f32[2,32,128]{2,1,0:T(8,128)S(1)} %maximum_select_fusion.2), channel_id=1, replica_groups=mesh['row'=8,'col'=4] {'col'}, use_global_device_ids=true, to_apply=%region_1.1 | all-reduce | flops 8192 | bytes 65536 | tf_op jit(solution)/shard_map/while/body/eval_jaxpr/psum | solution.py:20
  96.9 1.1 fusion.84
  98.0 1.1 fusion.82
  99.2 4.4 %collective-permute-start = (f32[2,32,256]{2,1,0:T(8,128)S(1)}, f32[2,32,256]{2,1,0:T(8,128)S(1)}, u32[]{:S(2)}, u32[]{:S(2)}) collective-permute-start(f32[2,32,256]{2,1,0:T(8,128)S(1)} %broadcast_select_fusion.2), channel_id=1, source_target_pairs={{0,4},{4,8},{8,12},{12,16},{16,20},{20,24},{24,28},{1,5},{5,9},{9,... | collective-permute-start | bytes 196616 | tf_op jit(solution)/shard_map/while/body/eval_jaxpr/ppermute | solution.py:15
  109.4 16.2 %psum.16 = f32[2,32,128]{2,1,0:T(8,128)S(1)} all-reduce(f32[2,32,128]{2,1,0:T(8,128)S(1)} %maximum_select_fusion.2), channel_id=1, replica_groups=mesh['row'=8,'col'=4] {'col'}, use_global_device_ids=true, to_apply=%region_1.1 | all-reduce | flops 8192 | bytes 65536 | tf_op jit(solution)/shard_map/while/body/eval_jaxpr/psum | solution.py:20
  125.5 1.1 fusion.83
  127.7 1.1 fusion.84
  128.8 1.1 fusion.82
  130.0 4.6 %collective-permute-start = (f32[2,32,256]{2,1,0:T(8,128)S(1)}, f32[2,32,256]{2,1,0:T(8,128)S(1)}, u32[]{:S(2)}, u32[]{:S(2)}) collective-permute-start(f32[2,32,256]{2,1,0:T(8,128)S(1)} %broadcast_select_fusion.2), channel_id=1, source_target_pairs={{0,4},{4,8},{8,12},{12,16},{16,20},{20,24},{24,28},{1,5},{5,9},{9,... | collective-permute-start | bytes 196616 | tf_op jit(solution)/shard_map/while/body/eval_jaxpr/ppermute | solution.py:15
  140.4 17.7 %psum.16 = f32[2,32,128]{2,1,0:T(8,128)S(1)} all-reduce(f32[2,32,128]{2,1,0:T(8,128)S(1)} %maximum_select_fusion.2), channel_id=1, replica_groups=mesh['row'=8,'col'=4] {'col'}, use_global_device_ids=true, to_apply=%region_1.1 | all-reduce | flops 8192 | bytes 65536 | tf_op jit(solution)/shard_map/while/body/eval_jaxpr/psum | solution.py:20
  158.0 1.1 fusion.83
  160.2 1.1 fusion.84
  161.3 1.1 fusion.82
  162.5 4.3 %collective-permute-start = (f32[2,32,256]{2,1,0:T(8,128)S(1)}, f32[2,32,256]{2,1,0:T(8,128)S(1)}, u32[]{:S(2)}, u32[]{:S(2)}) collective-permute-start(f32[2,32,256]{2,1,0:T(8,128)S(1)} %broadcast_select_fusion.2), channel_id=1, source_target_pairs={{0,4},{4,8},{8,12},{12,16},{16,20},{20,24},{24,28},{1,5},{5,9},{9,... | collective-permute-start | bytes 196616 | tf_op jit(solution)/shard_map/while/body/eval_jaxpr/ppermute | solution.py:15
  172.5 16.6 %psum.16 = f32[2,32,128]{2,1,0:T(8,128)S(1)} all-reduce(f32[2,32,128]{2,1,0:T(8,128)S(1)} %maximum_select_fusion.2), channel_id=1, replica_groups=mesh['row'=8,'col'=4] {'col'}, use_global_device_ids=true, to_apply=%region_1.1 | all-reduce | flops 8192 | bytes 65536 | tf_op jit(solution)/shard_map/while/body/eval_jaxpr/psum | solution.py:20
  189.1 1.1 fusion.83
  191.3 1.1 fusion.84
  192.4 1.1 fusion.82
  193.6 4.2 %collective-permute-start = (f32[2,32,256]{2,1,0:T(8,128)S(1)}, f32[2,32,256]{2,1,0:T(8,128)S(1)}, u32[]{:S(2)}, u32[]{:S(2)}) collective-permute-start(f32[2,32,256]{2,1,0:T(8,128)S(1)} %broadcast_select_fusion.2), channel_id=1, source_target_pairs={{0,4},{4,8},{8,12},{12,16},{16,20},{20,24},{24,28},{1,5},{5,9},{9,... | collective-permute-start | bytes 196616 | tf_op jit(solution)/shard_map/while/body/eval_jaxpr/ppermute | solution.py:15
  203.5 17.5 %psum.16 = f32[2,32,128]{2,1,0:T(8,128)S(1)} all-reduce(f32[2,32,128]{2,1,0:T(8,128)S(1)} %maximum_select_fusion.2), channel_id=1, replica_groups=mesh['row'=8,'col'=4] {'col'}, use_global_device_ids=true, to_apply=%region_1.1 | all-reduce | flops 8192 | bytes 65536 | tf_op jit(solution)/shard_map/while/body/eval_jaxpr/psum | solution.py:20
  221.1 1.1 fusion.83
  223.3 1.1 fusion.84
  224.3 1.1 fusion.82
  225.5 4.4 %collective-permute-start = (f32[2,32,256]{2,1,0:T(8,128)S(1)}, f32[2,32,256]{2,1,0:T(8,128)S(1)}, u32[]{:S(2)}, u32[]{:S(2)}) collective-permute-start(f32[2,32,256]{2,1,0:T(8,128)S(1)} %broadcast_select_fusion.2), channel_id=1, source_target_pairs={{0,4},{4,8},{8,12},{12,16},{16,20},{20,24},{24,28},{1,5},{5,9},{9,... | collective-permute-start | bytes 196616 | tf_op jit(solution)/shard_map/while/body/eval_jaxpr/ppermute | solution.py:15
  235.7 16.6 %psum.16 = f32[2,32,128]{2,1,0:T(8,128)S(1)} all-reduce(f32[2,32,128]{2,1,0:T(8,128)S(1)} %maximum_select_fusion.2), channel_id=1, replica_groups=mesh['row'=8,'col'=4] {'col'}, use_global_device_ids=true, to_apply=%region_1.1 | all-reduce | flops 8192 | bytes 65536 | tf_op jit(solution)/shard_map/while/body/eval_jaxpr/psum | solution.py:20
  252.3 1.1 fusion.83
  254.5 1.1 fusion.84
  255.6 1.1 fusion.82
  256.8 6.9 %fusion.29 = f32[32,16384]{1,0:T(8,128)S(1)} fusion(f32[2,128,16384]{2,1,0:T(8,128)} %param.12, f32[2,32,128]{2,1,0:T(8,128)S(1)} %get-tuple-element.224), kind=kOutput, calls=%fused_computation.44 | convolution fusion | flops 805306368 | bytes 10502144 | tf_op jit(solution)/shard_map/dot_general | solution.py:24
  263.6 7.2 %fusion.31 = f32[32,16384]{1,0:T(8,128)S(1)} fusion(f32[2,128,16384]{2,1,0:T(8,128)} %param.12, f32[2,32,128]{2,1,0:T(8,128)S(1)} %get-tuple-element.224), kind=kOutput, calls=%fused_computation.46 | convolution fusion | flops 805306368 | bytes 10502144 | tf_op jit(solution)/shard_map/dot_general | solution.py:24
  270.9 4.4 %fusion.25 = f32[1,32,16384]{2,1,0:T(8,128)S(1)} fusion(f32[32,16384]{1,0:T(8,128)S(1)} %fusion.29, f32[2,128,16384]{2,1,0:T(8,128)S(1)} %copy-done.1, f32[2,32,128]{2,1,0:T(8,128)S(1)} %get-tuple-element.224), kind=kOutput, calls=%fused_computation.39 | convolution fusion | flops 805830656 | bytes 12599296 | tf_op jit(solution)/shard_map/dot_general | solution.py:24
  275.3 4.4 %fusion.26 = f32[1,32,16384]{2,1,0:T(8,128)S(1)} fusion(f32[32,16384]{1,0:T(8,128)S(1)} %fusion.31, f32[2,128,16384]{2,1,0:T(8,128)S(1)} %copy-done.1, f32[2,32,128]{2,1,0:T(8,128)S(1)} %get-tuple-element.224), kind=kOutput, calls=%fused_computation.41 | convolution fusion | flops 805830656 | bytes 12599296 | tf_op jit(solution)/shard_map/dot_general | solution.py:24
  279.8 2.2 pad_maximum_fusion
  283.1 51.4 %all-reduce = f32[128]{0:T(128)S(1)} all-reduce(f32[128]{0:T(128)S(1)} %convolution_bitcast_fusion), channel_id=3, replica_groups=mesh['row'=8,'col'=4] {'row','col'}, use_global_device_ids=true, to_apply=%region_5.6.clone | all-reduce | flops 128 | bytes 1024
  335.0 10.9 %reduce-scatter.2.cloned.1.call-done = f32[2,32,2048]{2,1,0:T(8,128)} async-done(((f32[2,32,16384]{2,1,0:T(8,128)}), f32[2,32,2048]{2,1,0:T(8,128)}) %reduce-scatter.2.cloned.1.call-update) | async-done | bytes 524304 | tf_op jit(solution)/shard_map/reduce_scatter | solution.py:60
  345.9 1.9 sub.46
  (108 shorter events, 57.6 us)
Async XLA Ops:
  7.2 275.6 %copy-start = (f32[2,128]{1,0:T(2,128)S(1)}, f32[2,128]{1,0:T(2,128)}, u32[]{:S(2)}) copy-start(f32[2,128]{1,0:T(2,128)} %param.14) | copy-start | bytes 3076
  7.2 338.7 %reduce-scatter.2.cloned.1.call-start = ((), (), s32[]{:S(2)}) async-start(), calls=%async_computation.1 | async-start | bytes 4718592 | tf_op jit(solution)/shard_map/reduce_scatter | solution.py:60
  7.3 3.3 collective-permute-start
  40.0 2.2 collective-permute-start
  67.4 4.9 %collective-permute-start = (f32[2,32,256]{2,1,0:T(8,128)S(1)}, f32[2,32,256]{2,1,0:T(8,128)S(1)}, u32[]{:S(2)}, u32[]{:S(2)}) collective-permute-start(f32[2,32,256]{2,1,0:T(8,128)S(1)} %broadcast_select_fusion.2), channel_id=1, source_target_pairs={{0,4},{4,8},{8,12},{12,16},{16,20},{20,24},{24,28},{1,5},{5,9},{9,... | collective-permute-start | bytes 196616 | tf_op jit(solution)/shard_map/while/body/eval_jaxpr/ppermute | solution.py:15
  99.2 5.3 %collective-permute-start = (f32[2,32,256]{2,1,0:T(8,128)S(1)}, f32[2,32,256]{2,1,0:T(8,128)S(1)}, u32[]{:S(2)}, u32[]{:S(2)}) collective-permute-start(f32[2,32,256]{2,1,0:T(8,128)S(1)} %broadcast_select_fusion.2), channel_id=1, source_target_pairs={{0,4},{4,8},{8,12},{12,16},{16,20},{20,24},{24,28},{1,5},{5,9},{9,... | collective-permute-start | bytes 196616 | tf_op jit(solution)/shard_map/while/body/eval_jaxpr/ppermute | solution.py:15
  130.0 5.5 %collective-permute-start = (f32[2,32,256]{2,1,0:T(8,128)S(1)}, f32[2,32,256]{2,1,0:T(8,128)S(1)}, u32[]{:S(2)}, u32[]{:S(2)}) collective-permute-start(f32[2,32,256]{2,1,0:T(8,128)S(1)} %broadcast_select_fusion.2), channel_id=1, source_target_pairs={{0,4},{4,8},{8,12},{12,16},{16,20},{20,24},{24,28},{1,5},{5,9},{9,... | collective-permute-start | bytes 196616 | tf_op jit(solution)/shard_map/while/body/eval_jaxpr/ppermute | solution.py:15
  162.5 5.2 %collective-permute-start = (f32[2,32,256]{2,1,0:T(8,128)S(1)}, f32[2,32,256]{2,1,0:T(8,128)S(1)}, u32[]{:S(2)}, u32[]{:S(2)}) collective-permute-start(f32[2,32,256]{2,1,0:T(8,128)S(1)} %broadcast_select_fusion.2), channel_id=1, source_target_pairs={{0,4},{4,8},{8,12},{12,16},{16,20},{20,24},{24,28},{1,5},{5,9},{9,... | collective-permute-start | bytes 196616 | tf_op jit(solution)/shard_map/while/body/eval_jaxpr/ppermute | solution.py:15
  193.6 5.1 %collective-permute-start = (f32[2,32,256]{2,1,0:T(8,128)S(1)}, f32[2,32,256]{2,1,0:T(8,128)S(1)}, u32[]{:S(2)}, u32[]{:S(2)}) collective-permute-start(f32[2,32,256]{2,1,0:T(8,128)S(1)} %broadcast_select_fusion.2), channel_id=1, source_target_pairs={{0,4},{4,8},{8,12},{12,16},{16,20},{20,24},{24,28},{1,5},{5,9},{9,... | collective-permute-start | bytes 196616 | tf_op jit(solution)/shard_map/while/body/eval_jaxpr/ppermute | solution.py:15
  225.5 5.3 %collective-permute-start = (f32[2,32,256]{2,1,0:T(8,128)S(1)}, f32[2,32,256]{2,1,0:T(8,128)S(1)}, u32[]{:S(2)}, u32[]{:S(2)}) collective-permute-start(f32[2,32,256]{2,1,0:T(8,128)S(1)} %broadcast_select_fusion.2), channel_id=1, source_target_pairs={{0,4},{4,8},{8,12},{12,16},{16,20},{20,24},{24,28},{1,5},{5,9},{9,... | collective-permute-start | bytes 196616 | tf_op jit(solution)/shard_map/while/body/eval_jaxpr/ppermute | solution.py:15
  256.7 26.0 %copy-start.2 = (f32[2,32,128]{2,1,0:T(8,128)}, f32[2,32,128]{2,1,0:T(8,128)S(1)}, u32[]{:S(2)}) copy-start(f32[2,32,128]{2,1,0:T(8,128)S(1)} %get-tuple-element.224) | copy-start | bytes 98308
  256.7 14.2 %copy-start.1 = (f32[2,128,16384]{2,1,0:T(8,128)S(1)}, f32[2,128,16384]{2,1,0:T(8,128)}, u32[]{:S(2)}) copy-start(f32[2,128,16384]{2,1,0:T(8,128)} %param.12) | copy-start | bytes 50331652
  282.0 0.7 copy-start.4
  282.0 64.0 %copy-start.3 = (f32[2,32,2048]{2,1,0:T(8,128)S(1)}, f32[2,32,2048]{2,1,0:T(8,128)}, u32[]{:S(2)}) copy-start(f32[2,32,2048]{2,1,0:T(8,128)} %param.13) | copy-start | bytes 1572868
Sparse Core Ops, SparseCore 0:
  282.1 63.7 reduce-scatter.1
where the time goes:
time: 358 us; the launch traced here: 355 us
  blocking collectives  189 us (53%)
  matrix products  89.9 us (25%)
  starting transfers between devices  29.6 us (8%)
  waiting for transfers between devices  17.8 us (5%)
  between operations  14.2 us (4%)
  other arithmetic  11.3 us (3%)
    psum x8, blocking collectives, from_root(): return lax.psum(kept, axis)  138 us
    dot_general x69, matrix products, product_high(): jnp.dot(first, second, precision=highest, preferred_element_type=jnp.floa...  89.9 us
    unnamed x1, blocking collectives  51.4 us
    ppermute x8, starting transfers between devices, shifted(): return lax.ppermute(block, axis, route)  29.6 us
    reduce_scatter x1, waiting for transfers between devices, on_device(): reduced = lax.psum_scatter(term, 'row', scatter_dimension=2, tiled=True)  10.9 us
  transfers between devices with their start and end apart: 9, of which 9 were waited for; matrix products, arithmetic and copies ran while one was open for 0% of the time, Pallas kernels for 0%

commit v1 on v0

v1 whole, which is shorter than its diff:
```python
import functools

import jax
import jax.numpy as jnp
from jax import lax
from jax.experimental import pallas as pl
from jax.experimental.pallas import tpu as pltpu
from jax.sharding import PartitionSpec as P

PATCH_DEV = 4
LANES = 128
CHUNKS = 2

highest = lax.Precision.HIGHEST


def dot32(first, second):
    return jnp.dot(first, second, precision=highest, preferred_element_type=jnp.float32)


def dot16(first, second):
    return jnp.dot(first, second, preferred_element_type=jnp.float32)


def split(x):
    high = x.astype(jnp.bfloat16)
    return high, (x - high.astype(jnp.float32)).astype(jnp.bfloat16)


def product(left, right):
    rows, depth = left.shape[1], left.shape[2]
    first = jnp.concatenate([left[0], left[1]], axis=0)
    second = jnp.concatenate([left[1], -left[0]], axis=0)
    if depth % LANES == 0:
        joined = jnp.concatenate([first, second], axis=1)
        return dot32(joined, right.reshape(2 * depth, right.shape[2]))
    return dot32(first, right[0]) + dot32(second, right[1])


def step_kernel(step, members, width, *refs):
    refs = list(refs)
    out = refs.pop()
    rhs = [refs.pop(0) for _ in range(members)]
    inverse = [refs.pop(0) for _ in range(members)]
    inside = [refs.pop(0) for _ in range(members - 1)]
    earlier = refs.pop(0) if step else None
    pieces = refs
    observers = rhs[0].shape[1]
    held = None
    for group in range(step):
        for t in range(members):
            x = earlier[2 * group : 2 * group + 2, :, t * width : (t + 1) * width]
            term = product(x, pieces[(step - group - 1) * members + t][...])
            held = term if held is None else held + term
    solved = []
    for b in range(members):
        residual = jnp.concatenate([rhs[b][0], rhs[b][1]], axis=0)
        if held is not None:
            residual = residual - held[:, b * width : (b + 1) * width]
        for a in range(b):
            residual = residual - product(solved[a], inside[a][:, :, b * width : (b + 1) * width])
        value = product(residual.reshape(2, observers, width), inverse[b][...])
        solved.append(value.reshape(2, observers, width))
    if step:
        out[0 : 2 * step] = earlier[...]
    for b in range(members):
        out[2 * step : 2 * step + 2, :, b * width : (b + 1) * width] = solved[b]


def whole(shape):
    return jax.ShapeDtypeStruct(shape, jnp.float32)


def halve(values, axis, bit, rows):
    low = lax.index_in_dim(values, 0, axis, keepdims=False)
    high = lax.index_in_dim(values, 1, axis, keepdims=False)
    arrived = lax.ppermute(high, "row", [(i, i ^ (1 << bit)) for i in range(rows)])
    return low + arrived


def trail_kernel(members, devices, cols, flags, x_in, x_own, currents, owner, trail, sent, kept):
    row, col, last = flags[0], flags[1], flags[2]
    index = pl.program_id(0)
    half = devices // 2
    x = jnp.where(last == 1, x_own[...], x_in[...])
    observers, depth = x.shape[1], x.shape[2]
    first = jnp.concatenate([x[0], x[1]], axis=0)
    second = jnp.concatenate([x[1], -x[0]], axis=0)
    n = trail.shape[2]
    if depth % LANES == 0:
        high, low = split(jnp.concatenate([first, second], axis=1))
        pairs = [(high, low, trail[...].reshape(2 * depth, n))]
    else:
        pairs = [(*split(first), trail[0]), (*split(second), trail[1])]
    total = None
    for high, low, right in pairs:
        right_high, right_low = split(right)
        both = dot16(jnp.concatenate([high, low], axis=0), right_high)
        term = both[: 2 * observers] + both[2 * observers :] + dot16(high, right_low)
        total = term if total is None else total + term
    extra = sent.shape[3] - n
    if extra:
        relative = jnp.where(index < half, 2 * index + 1, 2 * (index - half))
        target = row ^ relative
        sums = jnp.sum(x, axis=1, keepdims=True)
        partial = currents[0:1] * sums[0] - currents[1:2] * sums[1]
        ids = (target * cols + col) * PATCH_DEV + lax.broadcasted_iota(jnp.int32, (observers, depth), 0)
        found = jnp.where(owner[...] == ids, partial, 0.0)
        gradient = jnp.broadcast_to(jnp.sum(found, axis=1, keepdims=True), (observers, extra))

    def put(ref):
        ref[0, 0, :, 0:n] = total[:observers]
        ref[0, 1, :, 0:n] = total[observers:]
        if extra:
            ref[0, 0, :, n:] = gradient
            ref[0, 1, :, n:] = gradient

    @pl.when(index < half)
    def _():
        put(sent)

    @pl.when(index >= half)
    def _():
        put(kept)


def trail_product(flags, x_in, x_own, currents, owner, trail, chunk, chunks, devices, cols, members):
    depth = trail.shape[1]
    observers = x_own.shape[1]
    columns = trail.shape[2] // devices // chunks
    half = devices // 2
    extra = LANES if chunk == 0 else 0

    def place(i, flags):
        relative = jnp.where(i < half, 2 * i + 1, 2 * (i - half))
        return 0, 0, (flags[0] ^ relative) * chunks + chunk

    def full(a):
        return pl.BlockSpec(a.shape, lambda i, flags: (0,) * a.ndim)

    out = jax.ShapeDtypeStruct((half, 2, observers, columns + extra), jnp.float32)
    block = (1, 2, observers, columns + extra)
    return pl.pallas_call(
        functools.partial(trail_kernel, members, devices, cols),
        grid_spec=pltpu.PrefetchScalarGridSpec(
            num_scalar_prefetch=1,
            grid=(devices,),
            in_specs=[
                full(x_in),
                full(x_own),
                full(currents),
                full(owner),
                pl.BlockSpec((2, depth, columns), place),
            ],
            out_specs=[
                pl.BlockSpec(block, lambda i, flags: (jnp.minimum(i, half - 1), 0, 0, 0)),
                pl.BlockSpec(block, lambda i, flags: (jnp.maximum(i - half, 0), 0, 0, 0)),
            ],
        ),
        out_shape=[out, out],
        cost_estimate=pl.CostEstimate(
            flops=12 * observers * depth * columns * devices,
            bytes_accessed=4 * 2 * depth * columns * devices,
            transcendentals=0,
        ),
    )(flags, x_in, x_own, currents, owner, trail)


def on_device(upper_block, block_inverse, panel_rhs, upper_trail, trail_rhs, currents, owner):
    rows = lax.axis_size("row")
    cols = lax.axis_size("col")
    row = lax.axis_index("row")
    col = lax.axis_index("col")
    width = block_inverse.shape[1]
    quarter = upper_block.shape[2]
    observers = panel_rhs.shape[1]
    members = rows // cols
    bits = rows.bit_length() - 1

    def flat(r, c):
        return r * cols + c

    def leader(k):
        return flat(members * k + members - 1, k)

    def send(value, pairs):
        return lax.ppermute(value, ("row", "col"), pairs)

    rhs, inverse, inside = [], [], []
    for t in range(members - 1):
        pairs = [(flat(members * k + t, k), leader(k)) for k in range(cols)]
        inside.append(send(upper_block, pairs))
        inverse.append(send(block_inverse, pairs))
        rhs.append(send(panel_rhs, pairs))
    rhs.append(panel_rhs)
    inverse.append(block_inverse)
    pieces = []
    for d in range(1, cols):
        for t in range(members):
            pieces.append(send(upper_block, [(flat(members * (k - d) + t, k), leader(k)) for k in range(d, cols)]))

    earlier = []
    results = []
    for step in range(cols):
        used = pieces[: step * members]
        message = pl.pallas_call(
            functools.partial(step_kernel, step, members, width),
            out_shape=whole((2 * step + 2, observers, quarter)),
        )(*rhs, *inverse, *inside, *earlier, *used)
        results.append(message[2 * step : 2 * step + 2])
        if step + 1 < cols:
            earlier = [send(message, [(leader(step), leader(step + 1))])]

    mine = results[0]
    for k in range(1, cols):
        mine = jnp.where(col == k, results[k], mine)
    at_leader = mine
    for s in range(1, cols):
        pairs = [(leader(k), flat(members * k + members - 1, (k + s) % cols)) for k in range(cols)]
        arrived = send(at_leader, pairs)
        mine = jnp.where((row // members + s) % cols == col, arrived, mine)
    own = mine[:, :, (members - 1) * width :]
    passed = jnp.zeros_like(own)
    for t in range(members - 1):
        pairs = [(members * k + members - 1, members * k + t) for k in range(cols)]
        arrived = lax.ppermute(mine[:, :, t * width : (t + 1) * width], "row", pairs)
        passed = arrived if members == 2 else jnp.where(row % members == t, arrived, passed)
    last = (row % members == members - 1).astype(jnp.int32)
    solved = jnp.where(last == 1, own, passed)

    flags = jnp.stack([row.astype(jnp.int32), col.astype(jnp.int32), last])
    owner_row = owner.reshape(1, width)
    columns = upper_trail.shape[2] // rows // CHUNKS
    pieces_out, gradient = [], None
    for chunk in range(CHUNKS):
        sent, kept = trail_product(
            flags, passed, own, currents, owner_row, upper_trail, chunk, CHUNKS, rows, cols, members
        )
        arrived = lax.ppermute(sent, "row", [(i, i ^ 1) for i in range(rows)])
        summed = kept + arrived
        shape = (2,) * (bits - 1)
        parts = []
        for part in range(2):
            value = summed[:, part]
            if part == 1:
                value = value[:, :, :columns]
            value = value.reshape(shape + value.shape[1:])
            left = list(range(bits - 1, 0, -1))
            order = list(range(1, bits)) if part == 0 else list(range(bits - 1, 0, -1))
            for bit in order:
                value = halve(value, left.index(bit), bit, rows)
                left.remove(bit)
            parts.append(value)
        if chunk == 0:
            gradient = parts[0][:PATCH_DEV, columns]
        pieces_out.append(jnp.stack([parts[0][:, :columns], parts[1]]))
    updated = trail_rhs - jnp.concatenate(pieces_out, axis=2)
    return solved, updated, gradient


def solution(mesh):
    in_specs = (
        P(None, "row", "col"),
        P(None, "row", None),
        P(None, None, "row"),
        P(None, "row", "col"),
        P(None, None, ("col", "row")),
        P(None, "row"),
        P("row"),
    )
    out_specs = (P(None, None, "row"), P(None, None, ("col", "row")), P(("row", "col")))
    return jax.shard_map(
        on_device, mesh=mesh, in_specs=in_specs, out_specs=out_specs, check_vma=False
    )
```

time: 358 us -> 102 us (0.28)
  blocking collectives: 189 us -> 0 us
  matrix products: 89.9 us -> 0 us
  Pallas kernels: 0 us -> 30.9 us
  between operations: 14.2 us -> 1.28 us
  other arithmetic: 11.3 us -> 3.55 us
  waiting for transfers between devices: 17.8 us -> 24.4 us
  local copies, waits for them, and re-layouts: 1.38 us -> 7.31 us
  starting transfers between devices: 29.6 us -> 33.2 us
    psum x8 -> x0, blocking collectives: 138 us -> none  [from_root(): return lax.psum(kept, axis)]
    dot_general x69 -> x0, matrix products: 89.9 us -> none  [product_high(): jnp.dot(first, second, precision=highest, preferred_element_type=jnp.floa...]
    unnamed x1 -> x0, blocking collectives: 51.4 us -> none
    pallas_call x0 -> x6, Pallas kernels: none -> 30.9 us  [the longest x2 17.7 us: trail_product(): pl.pallas_call(functools.partial(trail_kernel, members, devices, cols), g...]
    ppermute x8 -> x26, waiting for transfers between devices: 6.93 us -> 24.4 us  [the longest x1 14.7 us: on_device(): arrived = lax.ppermute(mine[:, :, t * width:(t + 1) * width], 'row', pairs)]
    reduce_scatter x1 -> x0, waiting for transfers between devices: 10.9 us -> none  [on_device(): reduced = lax.psum_scatter(term, 'row', scatter_dimension=2, tiled=True)]
    sub x9 -> x1, other arithmetic: 8.6 us -> 0.85 us  [on_device(): updated = trail_rhs - jnp.concatenate(pieces_out, axis=2)]
    unnamed x11 -> x38, local copies, waits for them, and re-layouts: 1.23 us -> 5 us
  transfers between devices with their start and end apart: 9 -> 26, of which waited for: 9 -> 6; matrix products, arithmetic and copies ran while one was open for 0% -> 3% of each run, Pallas kernels for 0% -> 18%
where the time goes in v1:
time: 102 us; the launch traced here: 101 us
  starting transfers between devices  33.2 us (33%)
  Pallas kernels  30.9 us (30%)
  waiting for transfers between devices  24.4 us (24%)
  local copies, waits for them, and re-layouts  7.31 us (7%)
  other arithmetic  3.55 us (3%)
  between operations  1.28 us (1%)
    ppermute x8, starting transfers between devices, halve(): lax.ppermute(high, 'row', [(i, i ^ 1 << bit) for i in range(rows)])  18.2 us
    pallas_call x2, Pallas kernels, trail_product(): pl.pallas_call(functools.partial(trail_kernel, members, devices, cols), g...  17.7 us
    ppermute x1, waiting for transfers between devices, on_device(): arrived = lax.ppermute(mine[:, :, t * width:(t + 1) * width], 'row', pairs)  14.7 us
    pallas_call x4, Pallas kernels, on_device(): pl.pallas_call(functools.partial(step_kernel, step, members, width), out_...  13.2 us
    ppermute x15, starting transfers between devices, send(): return lax.ppermute(value, ('row', 'col'), pairs)  13.2 us
    ppermute x8, waiting for transfers between devices, halve(): lax.ppermute(high, 'row', [(i, i ^ 1 << bit) for i in range(rows)])  8.67 us
    unnamed x38, local copies, waits for them, and re-layouts  5 us
  transfers between devices with their start and end apart: 26, of which 6 were waited for; matrix products, arithmetic and copies ran while one was open for 3% of the time, Pallas kernels for 18%

profile of v1, /device:TPU:0, one launch (start us, length us, event | category | flops | bytes accessed | tf_op | source)
XLA Modules:
  0.0 100.7 jit_solution(1935231045478708366)
XLA Ops:
  0.6 2.5 %collective-permute-start.2 = (f32[2,128,256]{2,1,0:T(8,128)}, f32[2,128,256]{2,1,0:T(8,128)S(1)}, u32[]{:S(2)}, u32[]{:S(2)}) collective-permute-start(f32[2,128,256]{2,1,0:T(8,128)} %param.7), channel_id=1, source_target_pairs={{0,4},{9,13},{18,22},{27,31}} | collective-permute-start | bytes 786440 | tf_op jit(solution)/shard_map/ppermute | solution.py:187
  3.2 0.7 collective-permute-start.4
  3.9 0.7 collective-permute-start.5
  4.6 1.3 %collective-permute-start.1 = (f32[2,128,128]{2,1,0:T(8,128)}, f32[2,128,128]{2,1,0:T(8,128)S(1)}, u32[]{:S(2)}, u32[]{:S(2)}) collective-permute-start(f32[2,128,128]{2,1,0:T(8,128)} %refs_3_.7), channel_id=1, source_target_pairs={{0,4},{9,13},{18,22},{27,31}} | collective-permute-start | bytes 393224 | tf_op jit(solution)/shard_map/ppermute | solution.py:187
  5.9 1.3 %collective-permute-start = (f32[2,32,128]{2,1,0:T(8,128)}, f32[2,32,128]{2,1,0:T(8,128)S(1)}, u32[]{:S(2)}, u32[]{:S(2)}) collective-permute-start(f32[2,32,128]{2,1,0:T(8,128)} %refs_1_.7), channel_id=1, source_target_pairs={{0,4},{9,13},{18,22},{27,31}} | collective-permute-start | bytes 98312 | tf_op jit(solution)/shard_map/ppermute | solution.py:187
  7.2 1.1 %collective-permute-done.refs_0_ = f32[2,32,128]{2,1,0:T(8,128)S(1)} collective-permute-done((f32[2,32,128]{2,1,0:T(8,128)}, f32[2,32,128]{2,1,0:T(8,128)S(1)}, u32[]{:S(2)}, u32[]{:S(2)}) %collective-permute-start) | collective-permute-done | bytes 32800 | tf_op jit(solution)/shard_map/ppermute | solution.py:187
  8.2 0.7 collective-permute-start.7
  8.9 0.7 collective-permute-start.8
  9.6 0.7 copy-done
  10.3 2.3 %shard_map.94 = f32[2,32,256]{2,1,0:T(8,128)} custom-call(f32[2,32,128]{2,1,0:T(8,128)} %copy-done.8, f32[2,32,128]{2,1,0:T(8,128)} %refs_1_.7, f32[2,128,128]{2,1,0:T(8,128)} %copy-done.3, f32[2,128,128]{2,1,0:T(8,128)} %refs_3_.7, f32[2,128,256]{2,1,0:T(8,128)} %copy-done), custom_call_target="tpu_custom_call" | custom-call | tf_op jit(solution)/shard_map/pallas_call | solution.py:206
  12.7 0.7 collective-permute-start.3
  13.4 0.7 copy-done.1
  14.2 0.6 copy-done.17
  14.8 3.2 %shard_map.95 = f32[4,32,256]{2,1,0:T(8,128)} custom-call(f32[2,32,128]{2,1,0:T(8,128)} %copy-done.8, f32[2,32,128]{2,1,0:T(8,128)} %refs_1_.7, f32[2,128,128]{2,1,0:T(8,128)} %copy-done.3, f32[2,128,128]{2,1,0:T(8,128)} %refs_3_.7, f32[2,128,256]{2,1,0:T(8,128)} %copy-done, f32[2,32,256]{2,1,0:T(8,128)} %copy-done.17, f32[2,128,256]{2,1,0:T(8,128)} %copy-done.1, ...), custom_call_target="tpu_custom_call" | custom-call | tf_op jit(solution)/shard_map/pallas_call | solution.py:206
  17.9 0.7 collective-permute-start.6
  18.6 0.7 collective-permute-start.10
  19.3 0.7 collective-permute-start.11
  20.0 0.7 copy-done.6
  20.8 0.7 copy-done.16
  21.5 3.6 %shard_map.96 = f32[6,32,256]{2,1,0:T(8,128)} custom-call(f32[2,32,128]{2,1,0:T(8,128)} %copy-done.8, f32[2,32,128]{2,1,0:T(8,128)} %refs_1_.7, f32[2,128,128]{2,1,0:T(8,128)} %copy-done.3, f32[2,128,128]{2,1,0:T(8,128)} %refs_3_.7, f32[2,128,256]{2,1,0:T(8,128)} %copy-done, f32[4,32,256]{2,1,0:T(8,128)} %copy-done.16, f32[2,128,256]{2,1,0:T(8,128)} %copy-done.1, ...), custom_call_target="tpu_custom_call" | custom-call | tf_op jit(solution)/shard_map/pallas_call | solution.py:206
  25.1 0.7 collective-permute-start.9
  25.8 0.7 copy-done.12
  26.6 0.7 copy-done.15
  27.3 4.1 %shard_map.97 = f32[8,32,256]{2,1,0:T(8,128)} custom-call(f32[2,32,128]{2,1,0:T(8,128)} %copy-done.8, f32[2,32,128]{2,1,0:T(8,128)} %refs_1_.7, f32[2,128,128]{2,1,0:T(8,128)} %copy-done.3, f32[2,128,128]{2,1,0:T(8,128)} %refs_3_.7, f32[2,128,256]{2,1,0:T(8,128)} %copy-done, f32[6,32,256]{2,1,0:T(8,128)} %copy-done.15, f32[2,128,256]{2,1,0:T(8,128)} %copy-done.1, ...), custom_call_target="tpu_custom_call" | custom-call | tf_op jit(solution)/shard_map/pallas_call | solution.py:206
  31.4 0.9 fusion.11
  32.3 0.7 collective-permute-start.12
  32.9 0.7 collective-permute-start.13
  33.6 0.7 collective-permute-start.14
  34.4 1.3 %collective-permute-start.15 = (f32[2,32,128]{2,1,0:T(8,128)S(1)}, f32[2,32,128]{2,1,0:T(8,128)S(1)}, u32[]{:S(2)}, u32[]{:S(2)}) collective-permute-start(f32[2,32,128]{2,1,0:T(8,128)S(1)} %slice.118), channel_id=1, source_target_pairs={{4,0},{12,8},{20,16},{28,24},{5,1},{13,9},{21,17},{29,25},{6,2},{1... | collective-permute-start | bytes 98312 | tf_op jit(solution)/shard_map/ppermute | solution.py:226
  35.7 0.7 pad_add_fusion.flags
  36.4 14.7 %collective-permute-done.15.x_in = f32[2,32,128]{2,1,0:T(8,128)S(1)} collective-permute-done((f32[2,32,128]{2,1,0:T(8,128)S(1)}, f32[2,32,128]{2,1,0:T(8,128)S(1)}, u32[]{:S(2)}, u32[]{:S(2)}) %collective-permute-start.15) | collective-permute-done | bytes 32800 | tf_op jit(solution)/shard_map/ppermute | solution.py:226
  51.1 0.6 fusion.13
  51.7 8.8 %shard_map.99 = (f32[4,2,32,1024]{3,2,1,0:T(8,128)}, f32[4,2,32,1024]{3,2,1,0:T(8,128)}) custom-call(s32[3]{0:T(128)} %pad_add_fusion.flags, f32[2,32,128]{2,1,0:T(8,128)} %copy-done.10, f32[2,32,128]{2,1,0:T(8,128)} %get-tuple-element.13.x_own, f32[2,128]{1,0:T(2,128)} %currents.3, s32[1,128]{1,0:T(1,128)} %bitcast.78, f32[2,128,16384]{2,1,0:T(8,128)} %trail.3), custom_call_target="tpu_custom_call" | custom-call | flops 402653184 | bytes 8388608 | tf_op jit(solution)/shard_map/pallas_call | solution.py:143
  60.7 8.9 %shard_map.98 = (f32[4,2,32,1152]{3,2,1,0:T(8,128)}, f32[4,2,32,1152]{3,2,1,0:T(8,128)}) custom-call(s32[3]{0:T(128)} %pad_add_fusion.flags, f32[2,32,128]{2,1,0:T(8,128)} %copy-done.10, f32[2,32,128]{2,1,0:T(8,128)} %get-tuple-element.13.x_own, f32[2,128]{1,0:T(2,128)} %currents.3, s32[1,128]{1,0:T(1,128)} %bitcast.79, f32[2,128,16384]{2,1,0:T(8,128)} %trail.3), custom_call_target="tpu_custom_call" | custom-call | flops 402653184 | bytes 8388608 | tf_op jit(solution)/shard_map/pallas_call | solution.py:143
  69.6 1.4 %copy.15 = f32[4,2,32,1152]{3,2,0,1:T(8,128)S(1)} copy(f32[4,2,32,1152]{3,2,1,0:T(8,128)} %get-tuple-element.8) | data formatting | bytes 2359296 | tf_op jit(solution)/shard_map/pallas_call | solution.py:143
  71.0 0.4 collective-permute-start.16
  71.4 0.2 add.65
  71.8 7.3 %collective-permute-start.24 = (f32[2,32,1024]{2,1,0:T(8,128)S(1)}, f32[2,32,1024]{2,1,0:T(8,128)S(1)}, u32[]{:S(2)}, u32[]{:S(2)}) collective-permute-start(f32[2,32,1024]{2,1,0:T(8,128)S(1)} %slice_bitcast_fusion.3), channel_id=1, source_target_pairs={{0,16},{4,20},{8,24},{12,28},{16,0},{20,4},{24,8},{28,12},{1,17},{... | collective-permute-start | bytes 786440 | tf_op jit(solution)/shard_map/ppermute | solution.py:77
  79.5 2.1 %collective-permute-start.19 = (f32[2,32,1024]{2,1,0:T(8,128)S(1)}, f32[2,32,1024]{2,1,0:T(8,128)S(1)}, u32[]{:S(2)}, u32[]{:S(2)}) collective-permute-start(f32[2,32,1024]{2,1,0:T(8,128)S(1)} %slice.127), channel_id=1, source_target_pairs={{0,16},{4,20},{8,24},{12,28},{16,0},{20,4},{24,8},{28,12},{1,17},{... | collective-permute-start | bytes 786440 | tf_op jit(solution)/shard_map/ppermute | solution.py:77
  81.6 4.7 %collective-permute-start.23 = (f32[32,1024]{1,0:T(8,128)S(1)}, f32[32,1024]{1,0:T(8,128)S(1)}, u32[]{:S(2)}, u32[]{:S(2)}) collective-permute-start(f32[32,1024]{1,0:T(8,128)S(1)} %slice_bitcast_fusion.11), channel_id=1, source_target_pairs={{0,16},{4,20},{8,24},{12,28},{16,0},{20,4},{24,8},{28,12},{1,17},{... | collective-permute-start | bytes 393224 | tf_op jit(solution)/shard_map/ppermute | solution.py:77
  86.3 2.1 %collective-permute-start.25 = (f32[32,1024]{1,0:T(8,128)S(1)}, f32[32,1024]{1,0:T(8,128)S(1)}, u32[]{:S(2)}, u32[]{:S(2)}) collective-permute-start(f32[32,1024]{1,0:T(8,128)S(1)} %slice_bitcast_fusion.9), channel_id=1, source_target_pairs={{0,8},{4,12},{8,0},{12,4},{16,24},{20,28},{24,16},{28,20},{1,9},{5... | collective-permute-start | bytes 393224 | tf_op jit(solution)/shard_map/ppermute | solution.py:77
  88.4 3.4 %collective-permute-done.19 = f32[2,32,1024]{2,1,0:T(8,128)S(1)} collective-permute-done((f32[2,32,1024]{2,1,0:T(8,128)S(1)}, f32[2,32,1024]{2,1,0:T(8,128)S(1)}, u32[]{:S(2)}, u32[]{:S(2)}) %collective-permute-start.19) | collective-permute-done | bytes 262176 | tf_op jit(solution)/shard_map/ppermute | solution.py:77
  92.0 1.8 %collective-permute-done.23 = f32[32,1024]{1,0:T(8,128)S(1)} collective-permute-done((f32[32,1024]{1,0:T(8,128)S(1)}, f32[32,1024]{1,0:T(8,128)S(1)}, u32[]{:S(2)}, u32[]{:S(2)}) %collective-permute-start.23) | collective-permute-done | bytes 131104 | tf_op jit(solution)/shard_map/ppermute | solution.py:77
  94.0 1.8 %collective-permute-start.18 = (f32[32,1152]{1,0:T(8,128)S(1)}, f32[32,1152]{1,0:T(8,128)S(1)}, u32[]{:S(2)}, u32[]{:S(2)}) collective-permute-start(f32[32,1152]{1,0:T(8,128)S(1)} %slice_bitcast_fusion.7), channel_id=1, source_target_pairs={{0,16},{4,20},{8,24},{12,28},{16,0},{20,4},{24,8},{28,12},{1,17},{... | collective-permute-start | bytes 442376 | tf_op jit(solution)/shard_map/ppermute | solution.py:77
  95.8 1.2 %collective-permute-done.20 = f32[32,1024]{1,0:T(8,128)S(1)} collective-permute-done((f32[32,1024]{1,0:T(8,128)S(1)}, f32[32,1024]{1,0:T(8,128)S(1)}, u32[]{:S(2)}, u32[]{:S(2)}) %collective-permute-start.20) | collective-permute-done | bytes 131104 | tf_op jit(solution)/shard_map/ppermute | solution.py:77
  97.0 2.2 %collective-permute-done.18 = f32[32,1152]{1,0:T(8,128)S(1)} collective-permute-done((f32[32,1152]{1,0:T(8,128)S(1)}, f32[32,1152]{1,0:T(8,128)S(1)}, u32[]{:S(2)}, u32[]{:S(2)}) %collective-permute-start.18) | collective-permute-done | bytes 147488 | tf_op jit(solution)/shard_map/ppermute | solution.py:77
  99.2 0.6 slice_reduce_fusion
  99.9 0.8 maximum_subtract_fusion
  (77 shorter events, 1.4 us)
Async XLA Ops:
  0.6 18.0 %copy-start.18 = (f32[2,128,256]{2,1,0:T(8,128)S(1)}, f32[2,128,256]{2,1,0:T(8,128)}, u32[]{:S(2)}) copy-start(f32[2,128,256]{2,1,0:T(8,128)} %param.7) | copy-start | bytes 786436
  0.6 9.0 %collective-permute-start.2 = (f32[2,128,256]{2,1,0:T(8,128)}, f32[2,128,256]{2,1,0:T(8,128)S(1)}, u32[]{:S(2)}, u32[]{:S(2)}) collective-permute-start(f32[2,128,256]{2,1,0:T(8,128)} %param.7), channel_id=1, source_target_pairs={{0,4},{9,13},{18,22},{27,31}} | collective-permute-start | bytes 786440 | tf_op jit(solution)/shard_map/ppermute | solution.py:187
  3.2 10.1 %collective-permute-start.4 = (f32[2,128,256]{2,1,0:T(8,128)}, f32[2,128,256]{2,1,0:T(8,128)S(1)}, u32[]{:S(2)}, u32[]{:S(2)}) collective-permute-start(f32[2,128,256]{2,1,0:T(8,128)} %param.7), channel_id=1, source_target_pairs={{1,13},{10,22},{19,31}} | collective-permute-start | bytes 786440 | tf_op jit(solution)/shard_map/ppermute | solution.py:187
  3.9 9.5 %collective-permute-start.5 = (f32[2,128,256]{2,1,0:T(8,128)}, f32[2,128,256]{2,1,0:T(8,128)S(1)}, u32[]{:S(2)}, u32[]{:S(2)}) collective-permute-start(f32[2,128,256]{2,1,0:T(8,128)} %param.7), channel_id=1, source_target_pairs={{5,13},{14,22},{23,31}} | collective-permute-start | bytes 786440 | tf_op jit(solution)/shard_map/ppermute | solution.py:187
  4.6 4.3 %collective-permute-start.1 = (f32[2,128,128]{2,1,0:T(8,128)}, f32[2,128,128]{2,1,0:T(8,128)S(1)}, u32[]{:S(2)}, u32[]{:S(2)}) collective-permute-start(f32[2,128,128]{2,1,0:T(8,128)} %refs_3_.7), channel_id=1, source_target_pairs={{0,4},{9,13},{18,22},{27,31}} | collective-permute-start | bytes 393224 | tf_op jit(solution)/shard_map/ppermute | solution.py:187
  5.9 2.4 %collective-permute-start = (f32[2,32,128]{2,1,0:T(8,128)}, f32[2,32,128]{2,1,0:T(8,128)S(1)}, u32[]{:S(2)}, u32[]{:S(2)}) collective-permute-start(f32[2,32,128]{2,1,0:T(8,128)} %refs_1_.7), channel_id=1, source_target_pairs={{0,4},{9,13},{18,22},{27,31}} | collective-permute-start | bytes 98312 | tf_op jit(solution)/shard_map/ppermute | solution.py:187
  8.2 1.4 %copy-start.8 = (f32[2,32,128]{2,1,0:T(8,128)}, f32[2,32,128]{2,1,0:T(8,128)S(1)}, u32[]{:S(2)}) copy-start(f32[2,32,128]{2,1,0:T(8,128)S(1)} %collective-permute-done.refs_0_) | copy-start | bytes 98308
  8.2 11.7 %collective-permute-start.7 = (f32[2,128,256]{2,1,0:T(8,128)}, f32[2,128,256]{2,1,0:T(8,128)S(1)}, u32[]{:S(2)}, u32[]{:S(2)}) collective-permute-start(f32[2,128,256]{2,1,0:T(8,128)} %param.7), channel_id=1, source_target_pairs={{2,22},{11,31}} | collective-permute-start | bytes 786440 | tf_op jit(solution)/shard_map/ppermute | solution.py:187
  8.9 0.7 copy-start.3
  8.9 11.1 %collective-permute-start.8 = (f32[2,128,256]{2,1,0:T(8,128)}, f32[2,128,256]{2,1,0:T(8,128)S(1)}, u32[]{:S(2)}, u32[]{:S(2)}) collective-permute-start(f32[2,128,256]{2,1,0:T(8,128)} %param.7), channel_id=1, source_target_pairs={{6,22},{15,31}} | collective-permute-start | bytes 786440 | tf_op jit(solution)/shard_map/ppermute | solution.py:187
  9.6 0.7 copy-start
  12.7 0.7 collective-permute-start.3
  13.3 0.7 copy-start.1
  13.4 0.8 copy-start.2
  14.1 0.6 copy-start.17
  17.9 2.1 %collective-permute-start.6 = (f32[4,32,256]{2,1,0:T(8,128)}, f32[4,32,256]{2,1,0:T(8,128)S(1)}, u32[]{:S(2)}, u32[]{:S(2)}) collective-permute-start(f32[4,32,256]{2,1,0:T(8,128)} %shard_map.95), channel_id=1, source_target_pairs={{13,22}} | collective-permute-start | bytes 393224 | tf_op jit(solution)/shard_map/ppermute | solution.py:187
  18.6 7.2 %collective-permute-start.10 = (f32[2,128,256]{2,1,0:T(8,128)S(1)}, f32[2,128,256]{2,1,0:T(8,128)S(1)}, u32[]{:S(2)}, u32[]{:S(2)}) collective-permute-start(f32[2,128,256]{2,1,0:T(8,128)S(1)} %copy-done.18), channel_id=1, source_target_pairs={{3,31}} | collective-permute-start | bytes 786440 | tf_op jit(solution)/shard_map/ppermute | solution.py:187
  19.3 6.5 %collective-permute-start.11 = (f32[2,128,256]{2,1,0:T(8,128)S(1)}, f32[2,128,256]{2,1,0:T(8,128)S(1)}, u32[]{:S(2)}, u32[]{:S(2)}) collective-permute-start(f32[2,128,256]{2,1,0:T(8,128)S(1)} %copy-done.18), channel_id=1, source_target_pairs={{7,31}} | collective-permute-start | bytes 786440 | tf_op jit(solution)/shard_map/ppermute | solution.py:187
  20.0 0.7 copy-start.6
  20.0 0.8 copy-start.7
  20.8 0.7 copy-start.16
  25.1 0.7 collective-permute-start.9
  25.8 5.6 %copy-start.11 = (f32[4,32,256]{2,1,0:T(8,128)S(1)}, f32[4,32,256]{2,1,0:T(8,128)}, u32[]{:S(2)}) copy-start(f32[4,32,256]{2,1,0:T(8,128)} %shard_map.95) | copy-start | bytes 393220
  25.8 5.6 %copy-start.14 = (f32[2,32,256]{2,1,0:T(8,128)S(1)}, f32[2,32,256]{2,1,0:T(8,128)}, u32[]{:S(2)}) copy-start(f32[2,32,256]{2,1,0:T(8,128)} %shard_map.94) | copy-start | bytes 196612
  25.8 0.7 copy-start.12
  25.8 0.8 copy-start.13
  26.6 0.7 copy-start.15
  32.3 2.1 %collective-permute-start.12 = (f32[2,32,256]{2,1,0:T(8,128)S(1)}, f32[2,32,256]{2,1,0:T(8,128)S(1)}, u32[]{:S(2)}, u32[]{:S(2)}) collective-permute-start(f32[2,32,256]{2,1,0:T(8,128)S(1)} %fusion.11), channel_id=1, source_target_pairs={{4,7},{13,12},{22,21},{31,30}} | collective-permute-start | bytes 196616 | tf_op jit(solution)/shard_map/ppermute | solution.py:187
  32.9 1.4 %collective-permute-start.13 = (f32[2,32,256]{2,1,0:T(8,128)S(1)}, f32[2,32,256]{2,1,0:T(8,128)S(1)}, u32[]{:S(2)}, u32[]{:S(2)}) collective-permute-start(f32[2,32,256]{2,1,0:T(8,128)S(1)} %fusion.11), channel_id=1, source_target_pairs={{4,6},{13,15},{22,20},{31,29}} | collective-permute-start | bytes 196616 | tf_op jit(solution)/shard_map/ppermute | solution.py:187
  33.6 0.8 collective-permute-start.14
  34.4 16.6 %collective-permute-start.15 = (f32[2,32,128]{2,1,0:T(8,128)S(1)}, f32[2,32,128]{2,1,0:T(8,128)S(1)}, u32[]{:S(2)}, u32[]{:S(2)}) collective-permute-start(f32[2,32,128]{2,1,0:T(8,128)S(1)} %slice.118), channel_id=1, source_target_pairs={{4,0},{12,8},{20,16},{28,24},{5,1},{13,9},{21,17},{29,25},{6,2},{1... | collective-permute-start | bytes 98312 | tf_op jit(solution)/shard_map/ppermute | solution.py:226
  51.1 0.6 copy-start.10
  60.5 10.9 %collective-permute-start.21 = (f32[4,2,32,1024]{3,2,1,0:T(8,128)}, f32[4,2,32,1024]{3,2,1,0:T(8,128)S(1)}, u32[]{:S(2)}, u32[]{:S(2)}) collective-permute-start(f32[4,2,32,1024]{3,2,1,0:T(8,128)} %get-tuple-element.10), channel_id=1, source_target_pairs={{0,4},{4,0},{8,12},{12,8},{16,20},{20,16},{24,28},{28,24},{1,5},{5... | collective-permute-start | bytes 3145736 | tf_op jit(solution)/shard_map/ppermute | solution.py:239
  69.6 1.8 %copy-start.5 = (f32[4,2,32,1024]{3,2,1,0:T(8,128)S(1)}, f32[4,2,32,1024]{3,2,1,0:T(8,128)}, u32[]{:S(2)}) copy-start(f32[4,2,32,1024]{3,2,1,0:T(8,128)} %get-tuple-element.9) | copy-start | bytes 3145732
  71.0 8.1 %collective-permute-start.16 = (f32[4,2,32,1152]{3,2,0,1:T(8,128)S(1)}, f32[4,2,32,1152]{3,2,0,1:T(8,128)S(1)}, u32[]{:S(2)}, u32[]{:S(2)}) collective-permute-start(f32[4,2,32,1152]{3,2,0,1:T(8,128)S(1)} %copy.15), channel_id=1, source_target_pairs={{0,4},{4,0},{8,12},{12,8},{16,20},{20,16},{24,28},{28,24},{1,5},{5... | collective-permute-start | bytes 3538952 | tf_op jit(solution)/shard_map/ppermute | solution.py:239
  71.6 7.5 %copy-start.4 = (f32[4,2,32,1152]{3,2,1,0:T(8,128)S(1)}, f32[4,2,32,1152]{3,2,1,0:T(8,128)}, u32[]{:S(2)}) copy-start(f32[4,2,32,1152]{3,2,1,0:T(8,128)} %get-tuple-element.7) | copy-start | bytes 3538948
  71.7 9.9 %collective-permute-start.22 = (f32[2,32,1024]{2,1,0:T(8,128)S(1)}, f32[2,32,1024]{2,1,0:T(8,128)S(1)}, u32[]{:S(2)}, u32[]{:S(2)}) collective-permute-start(f32[2,32,1024]{2,1,0:T(8,128)S(1)} %slice_bitcast_fusion.5), channel_id=1, source_target_pairs={{0,8},{4,12},{8,0},{12,4},{16,24},{20,28},{24,16},{28,20},{1,9},{5... | collective-permute-start | bytes 786440 | tf_op jit(solution)/shard_map/ppermute | solution.py:77
  71.8 14.5 %collective-permute-start.24 = (f32[2,32,1024]{2,1,0:T(8,128)S(1)}, f32[2,32,1024]{2,1,0:T(8,128)S(1)}, u32[]{:S(2)}, u32[]{:S(2)}) collective-permute-start(f32[2,32,1024]{2,1,0:T(8,128)S(1)} %slice_bitcast_fusion.3), channel_id=1, source_target_pairs={{0,16},{4,20},{8,24},{12,28},{16,0},{20,4},{24,8},{28,12},{1,17},{... | collective-permute-start | bytes 786440 | tf_op jit(solution)/shard_map/ppermute | solution.py:77
  79.3 14.6 %collective-permute-start.17 = (f32[2,32,1152]{2,1,0:T(8,128)S(1)}, f32[2,32,1152]{2,1,0:T(8,128)S(1)}, u32[]{:S(2)}, u32[]{:S(2)}) collective-permute-start(f32[2,32,1152]{2,1,0:T(8,128)S(1)} %slice_bitcast_fusion.1), channel_id=1, source_target_pairs={{0,8},{4,12},{8,0},{12,4},{16,24},{20,28},{24,16},{28,20},{1,9},{5... | collective-permute-start | bytes 884744 | tf_op jit(solution)/shard_map/ppermute | solution.py:77
  79.5 12.4 %collective-permute-start.19 = (f32[2,32,1024]{2,1,0:T(8,128)S(1)}, f32[2,32,1024]{2,1,0:T(8,128)S(1)}, u32[]{:S(2)}, u32[]{:S(2)}) collective-permute-start(f32[2,32,1024]{2,1,0:T(8,128)S(1)} %slice.127), channel_id=1, source_target_pairs={{0,16},{4,20},{8,24},{12,28},{16,0},{20,4},{24,8},{28,12},{1,17},{... | collective-permute-start | bytes 786440 | tf_op jit(solution)/shard_map/ppermute | solution.py:77
  81.6 12.2 %collective-permute-start.23 = (f32[32,1024]{1,0:T(8,128)S(1)}, f32[32,1024]{1,0:T(8,128)S(1)}, u32[]{:S(2)}, u32[]{:S(2)}) collective-permute-start(f32[32,1024]{1,0:T(8,128)S(1)} %slice_bitcast_fusion.11), channel_id=1, source_target_pairs={{0,16},{4,20},{8,24},{12,28},{16,0},{20,4},{24,8},{28,12},{1,17},{... | collective-permute-start | bytes 393224 | tf_op jit(solution)/shard_map/ppermute | solution.py:77
  86.3 7.5 %collective-permute-start.25 = (f32[32,1024]{1,0:T(8,128)S(1)}, f32[32,1024]{1,0:T(8,128)S(1)}, u32[]{:S(2)}, u32[]{:S(2)}) collective-permute-start(f32[32,1024]{1,0:T(8,128)S(1)} %slice_bitcast_fusion.9), channel_id=1, source_target_pairs={{0,8},{4,12},{8,0},{12,4},{16,24},{20,28},{24,16},{28,20},{1,9},{5... | collective-permute-start | bytes 393224 | tf_op jit(solution)/shard_map/ppermute | solution.py:77
  91.9 5.0 %collective-permute-start.20 = (f32[32,1024]{1,0:T(8,128)S(1)}, f32[32,1024]{1,0:T(8,128)S(1)}, u32[]{:S(2)}, u32[]{:S(2)}) collective-permute-start(f32[32,1024]{1,0:T(8,128)S(1)} %slice_bitcast_fusion.13), channel_id=1, source_target_pairs={{0,8},{4,12},{8,0},{12,4},{16,24},{20,28},{24,16},{28,20},{1,9},{5... | collective-permute-start | bytes 393224 | tf_op jit(solution)/shard_map/ppermute | solution.py:77
  93.9 6.0 %copy-start.9 = (f32[2,32,2048]{2,1,0:T(8,128)S(1)}, f32[2,32,2048]{2,1,0:T(8,128)}, u32[]{:S(2)}) copy-start(f32[2,32,2048]{2,1,0:T(8,128)} %param.11) | copy-start | bytes 1572868
  94.0 5.2 %collective-permute-start.18 = (f32[32,1152]{1,0:T(8,128)S(1)}, f32[32,1152]{1,0:T(8,128)S(1)}, u32[]{:S(2)}, u32[]{:S(2)}) collective-permute-start(f32[32,1152]{1,0:T(8,128)S(1)} %slice_bitcast_fusion.7), channel_id=1, source_target_pairs={{0,16},{4,20},{8,24},{12,28},{16,0},{20,4},{24,8},{28,12},{1,17},{... | collective-permute-start | bytes 442376 | tf_op jit(solution)/shard_map/ppermute | solution.py:77

commit v2 on v0

v2 whole, which is shorter than its diff:
```python
import functools

import jax
import jax.numpy as jnp
from jax import lax
from jax.experimental import pallas as pl
from jax.experimental.pallas import tpu as pltpu
from jax.sharding import PartitionSpec as P


PATCH_DEV = 4
LANES = 128
CHUNKS = 2


def dot16(first, second):
    return jnp.dot(first, second, preferred_element_type=jnp.float32)


def split(x):
    high = x.astype(jnp.bfloat16)
    return high, (x - high.astype(jnp.float32)).astype(jnp.bfloat16)


def stacked(left):
    first = jnp.concatenate([left[0], left[1]], axis=0)
    second = jnp.concatenate([left[1], -left[0]], axis=0)
    return first, second


def product(left, right):
    depth, n = left.shape[2], right.shape[2]
    first, second = stacked(left)
    rows = first.shape[0]
    if depth % LANES == 0:
        pairs = [(jnp.concatenate([first, second], axis=1), right.reshape(2 * depth, n))]
    else:
        pairs = [(first, right[0]), (second, right[1])]
    total = None
    for x, y in pairs:
        x_high, x_low = split(x)
        y_high, y_low = split(y)
        both = dot16(jnp.concatenate([x_high, x_low], axis=0), y_high)
        term = both[:rows] + both[rows:] + dot16(x_high, y_low)
        total = term if total is None else total + term
    return total


VMEM = pl.BlockSpec(memory_space=pltpu.VMEM)
ANY = pl.BlockSpec(memory_space=pl.ANY)


def local_call(kernel, outs, near, far=(), scratch=(), limit=16 << 20, far_outs=()):
    near = [pltpu.with_memory_space_constraint(a, pltpu.VMEM) for a in near]
    far = [pltpu.with_memory_space_constraint(a, pltpu.HBM) for a in far]
    return pl.pallas_call(
        kernel,
        in_specs=[VMEM] * len(near) + [ANY] * len(far),
        out_specs=[VMEM] * len(outs) + [ANY] * len(far_outs),
        out_shape=[pltpu.VMEM(shape, dtype) for shape, dtype in outs]
        + [pltpu.HBM(shape, dtype) for shape, dtype in far_outs],
        scratch_shapes=scratch,
        compiler_params=pltpu.CompilerParams(vmem_limit_bytes=limit),
    )(*near, *far)


def load_kernel(count, *refs):
    sources, targets, sems = refs[:count], refs[count : 2 * count], refs[2 * count]
    copies = [pltpu.make_async_copy(a, b, sems.at[i]) for i, (a, b) in enumerate(zip(sources, targets))]
    for copy in copies:
        copy.start()
    for copy in copies:
        copy.wait()


def after(value, other):
    return lax.optimization_barrier((value, other))[0]


def step_kernel(step, groups, members, width, *refs):
    refs = list(refs)
    out = refs.pop()
    rhs = [refs.pop(0) for _ in range(members)]
    inverse = [refs.pop(0) for _ in range(members)]
    inside = [refs.pop(0) for _ in range(members - 1)]
    earlier = refs.pop(0) if step else None
    pieces = [refs.pop(0) for _ in range(step * members)]
    results = refs
    observers = rhs[0].shape[1]
    final = step + 1 == groups
    row, col = lax.axis_index("row"), lax.axis_index("col")

    @pl.when((col == step) & (row == members * step + members - 1))
    def _():
        held = None
        for group in range(step):
            for t in range(members):
                x = earlier[2 * group : 2 * group + 2, :, t * width : (t + 1) * width]
                term = product(x, pieces[(step - group - 1) * members + t][...])
                held = term if held is None else held + term
        solved = []
        for b in range(members):
            residual = jnp.concatenate([rhs[b][0], rhs[b][1]], axis=0)
            if held is not None:
                residual = residual - held[:, b * width : (b + 1) * width]
            for a in range(b):
                residual = residual - product(solved[a], inside[a][:, :, b * width : (b + 1) * width])
            value = product(residual.reshape(2, observers, width), inverse[b][...])
            solved.append(value.reshape(2, observers, width))
        base = 0
        if not final:
            if step:
                out[0 : 2 * step] = earlier[...]
            base = 2 * step
        for b in range(members):
            out[base : base + 2, :, b * width : (b + 1) * width] = solved[b]

    if final:
        for k in range(step):
            @pl.when(col == k)
            def _(k=k):
                out[...] = results[k][2 * k : 2 * k + 2]


def merge_kernel(members, *refs):
    outs = refs[-members:]
    sources = refs[:-members]
    cols = len(sources)
    width = outs[0].shape[2]
    group, col = lax.div(lax.axis_index("row"), members), lax.axis_index("col")
    for s, source in enumerate(sources):
        @pl.when(lax.rem(group + s, cols) == col)
        def _(source=source):
            for t in range(members):
                outs[t][...] = source[:, :, t * width : (t + 1) * width]


def prepare_kernel(chunk, chunks, trail, high, low, room, sems):
    devices, columns = room.shape[0], room.shape[3]
    copies = []
    for i in range(devices):
        start = (i * chunks + chunk) * columns
        copies.append(pltpu.make_async_copy(trail.at[:, :, start : start + columns], room.at[i], sems.at[i]))
        copies[-1].start()
    for i in range(devices):
        copies[i].wait()
        for part in range(2):
            depth = room.shape[2]
            a, b = split(room[i, part])
            high[i, part * depth : (part + 1) * depth] = a
            low[i, part * depth : (part + 1) * depth] = b


def trail_kernel(chunk, chunks, cols, ready, members, currents, owner, *refs):
    row = lax.axis_index("row")
    if ready:
        candidates, refs = refs[:members], refs[members:]
        high, low, x, sent_a, sent_b, kept_a, kept_b, solved, sem = refs
        for t in range(members):
            @pl.when(lax.rem(row, members) == t)
            def _(t=t):
                x[...] = candidates[t][...]
        out = pltpu.make_async_copy(x, solved, sem)
        out.start()
    else:
        x, refs = refs[0], refs[1:]
    observers, depth = x.shape[1], x.shape[2]
    if ready:
        devices, columns = high.shape[0], high.shape[2]
    else:
        trail, sent_a, sent_b, kept_a, kept_b, room, sems = refs
        devices, columns = room.shape[0], room.shape[3]
    half = devices // 2
    targets = [row ^ (2 * (i % half) + (1 if i < half else 0)) for i in range(devices)]
    copies = []
    if not ready:
        for i, target in enumerate(targets):
            start = pl.multiple_of((target * chunks + chunk) * columns, LANES)
            copies.append(pltpu.make_async_copy(trail.at[:, :, pl.ds(start, columns)], room.at[i], sems.at[i]))
            copies[-1].start()
    first, second = stacked(x[...])
    if depth % LANES == 0:
        lefts = [split(jnp.concatenate([first, second], axis=1))]
    else:
        lefts = [split(first), split(second)]
    lefts = [(a, jnp.concatenate([a, b], axis=0)) for a, b in lefts]
    share = 2 * depth // len(lefts)
    extra = kept_a.shape[2] - columns
    if extra:
        col = lax.axis_index("col")
        sums = jnp.sum(x[...], axis=1, keepdims=True)
        partial = currents[0:1] * sums[0] - currents[1:2] * sums[1]
        patch = lax.broadcasted_iota(jnp.int32, (observers, depth), 0)
    for i, target in enumerate(targets):
        e = i % half
        ref_a, ref_b = (sent_a, sent_b) if i < half else (kept_a, kept_b)
        total = None
        if not ready:
            copies[i].wait()
            whole = room[i].reshape(2 * depth, columns)
        for j, (left, pair) in enumerate(lefts):
            place = slice(j * share, (j + 1) * share)
            if ready:
                right_high, right_low = high[target, place], low[target, place]
            else:
                right_high, right_low = split(whole[place])
            both = dot16(pair, right_high)
            term = both[: 2 * observers] + both[2 * observers :] + dot16(left, right_low)
            total = term if total is None else total + term
        ref_a[e, :, 0:columns] = total[:observers]
        ref_b[e] = total[observers:]
        if extra:
            found = jnp.where(owner[...] == patch + (target * cols + col) * PATCH_DEV, partial, 0.0)
            gradient = jnp.sum(found, axis=1, keepdims=True)
            ref_a[e, :, columns:] = jnp.broadcast_to(gradient, (observers, extra))
    if ready:
        out.wait()


def halve(values, axis, bit, rows):
    low = lax.index_in_dim(values, 0, axis, keepdims=False)
    high = lax.index_in_dim(values, 1, axis, keepdims=False)
    arrived = lax.ppermute(high, "row", [(i, i ^ (1 << bit)) for i in range(rows)])
    return low + arrived


def on_device(upper_block, block_inverse, panel_rhs, upper_trail, trail_rhs, currents, owner):
    rows = lax.axis_size("row")
    cols = lax.axis_size("col")
    width = block_inverse.shape[1]
    quarter = upper_block.shape[2]
    observers = panel_rhs.shape[1]
    members = rows // cols
    bits = rows.bit_length() - 1

    def flat(r, c):
        return r * cols + c

    def leader(k):
        return flat(members * k + members - 1, k)

    def send(value, pairs):
        return lax.ppermute(value, ("row", "col"), pairs)

    pieces = []

    def above(d, source):
        for t in range(members):
            pairs = [(flat(members * (k - d) + t, k), leader(k)) for k in range(d, cols)]
            pieces.append(send(source, pairs))

    above(1, upper_block)
    rhs, inverse, inside = [], [], []
    for t in range(members - 1):
        turn = members - 1 - t
        pairs = [(i, i // members * members + (i + turn) % members) for i in range(rows)]
        rhs.append(lax.ppermute(panel_rhs, "row", pairs))
        inverse.append(lax.ppermute(block_inverse, "row", pairs))
        inside.append(lax.ppermute(upper_block, "row", pairs))
    owner_row = owner.reshape(1, width)
    loaded = [panel_rhs, block_inverse, currents, owner_row]
    panel_near, inverse_near, currents_near, owner_near = local_call(
        functools.partial(load_kernel, len(loaded)),
        [(a.shape, a.dtype) for a in loaded],
        [],
        loaded,
        [pltpu.SemaphoreType.DMA((len(loaded),))],
        limit=2 << 20,
    )
    rhs.append(panel_near)
    inverse.append(inverse_near)

    columns = upper_trail.shape[2] // rows // CHUNKS
    room = [pltpu.VMEM((rows, 2, width, columns), jnp.float32), pltpu.SemaphoreType.DMA((rows,))]
    earlier, messages = [], []
    for step in range(cols):
        final = step + 1 == cols
        shape = (2 if final else 2 * step + 2, observers, quarter)
        message = local_call(
            functools.partial(step_kernel, step, cols, members, width),
            [(shape, jnp.float32)],
            [*rhs, *inverse, *inside, *earlier, *pieces[: step * members], *(messages if final else [])],
        )[0]
        messages.append(message)
        if not final:
            earlier = [send(message, [(leader(step), leader(step + 1))])]
        if step + 2 < cols:
            above(step + 2, after(upper_block, message))
        if step == min(1, cols - 2):
            ready = local_call(
                functools.partial(prepare_kernel, 0, CHUNKS),
                [((rows, 2 * width, columns), jnp.bfloat16)] * 2,
                [],
                [after(upper_trail, message)],
                room,
            )

    arrived = [messages[-1]]
    for s in range(1, cols):
        pairs = [(leader(k), flat(members * k + members - 1, (k + s) % cols)) for k in range(cols)]
        arrived.append(send(messages[-1], pairs))
    parts = local_call(
        functools.partial(merge_kernel, members),
        [((2, observers, width), jnp.float32)] * members,
        arrived,
        limit=2 << 20,
    )
    candidates = []
    for t in range(members - 1):
        turn = t - (members - 1)
        pairs = [(i, i // members * members + (i + turn) % members) for i in range(rows)]
        candidates.append(lax.ppermute(parts[t], "row", pairs))
    candidates.append(parts[-1])

    half = rows // 2
    out_parts, gradient, factor, solved = [], None, None, None
    for chunk in range(CHUNKS):
        extra = LANES if chunk == 0 else 0
        real, imag = (half, observers, columns + extra), (half, observers, columns)
        results = local_call(
            functools.partial(trail_kernel, chunk, CHUNKS, cols, chunk == 0, members),
            [(a, jnp.float32) for a in ([candidates[0].shape] if chunk == 0 else []) + [real, imag, real, imag]],
            [currents_near, owner_near, *([*candidates, *ready] if chunk == 0 else [factor])],
            [] if chunk == 0 else [upper_trail],
            [pltpu.SemaphoreType.DMA] if chunk == 0 else room,
            far_outs=[(candidates[0].shape, jnp.float32)] if chunk == 0 else [],
        )
        if chunk == 0:
            factor, *results, solved = results
        parts = []
        for part in range(2):
            arrived = lax.ppermute(results[part], "row", [(i, i ^ 1) for i in range(rows)])
            value = results[2 + part] + arrived
            value = value.reshape((2,) * (bits - 1) + value.shape[1:])
            left = list(range(bits - 1, 0, -1))
            order = left[::-1] if part == 0 else left[:]
            for bit in order:
                value = halve(value, left.index(bit), bit, rows)
                left.remove(bit)
            parts.append(value)
        if extra:
            gradient = parts[0][:PATCH_DEV, columns]
        out_parts.append(jnp.stack([parts[0][:, :columns], parts[1]]))
    updated = trail_rhs - jnp.concatenate(out_parts, axis=2)
    return solved, updated, gradient


def solution(mesh):
    in_specs = (
        P(None, "row", "col"),
        P(None, "row", None),
        P(None, None, "row"),
        P(None, "row", "col"),
        P(None, None, ("col", "row")),
        P(None, "row"),
        P("row"),
    )
    out_specs = (P(None, None, "row"), P(None, None, ("col", "row")), P(("row", "col")))

    return jax.shard_map(on_device, mesh=mesh, in_specs=in_specs, out_specs=out_specs, check_vma=False)
```

time: 358 us -> 70.7 us (0.20)
  blocking collectives: 189 us -> 0 us
  matrix products: 89.9 us -> 0 us
  starting transfers between devices: 29.6 us -> 52.3 us
  between operations: 14.2 us -> 1.03 us
  waiting for transfers between devices: 17.8 us -> 4.76 us
  Pallas kernels: 0 us -> 10.2 us
  other arithmetic: 11.3 us -> 1.34 us
    psum x8 -> x0, blocking collectives: 138 us -> none  [from_root(): return lax.psum(kept, axis)]
    dot_general x69 -> x0, matrix products: 89.9 us -> none  [product_high(): jnp.dot(first, second, precision=highest, preferred_element_type=jnp.floa...]
    unnamed x1 -> x0, blocking collectives: 51.4 us -> none
    ppermute x8 -> x28, starting transfers between devices: 29.6 us -> 52.3 us  [the longest x8 21.9 us: halve(): lax.ppermute(high, 'row', [(i, i ^ 1 << bit) for i in range(rows)])]
    reduce_scatter x1 -> x0, waiting for transfers between devices: 10.9 us -> none  [on_device(): reduced = lax.psum_scatter(term, 'row', scatter_dimension=2, tiled=True)]
    pallas_call x0 -> x9, Pallas kernels: none -> 10.2 us  [local_call(): pl.pallas_call(kernel, in_specs=[VMEM] * len(near) + [ANY] * len(far), ou...]
    sub x9 -> x1, other arithmetic: 8.6 us -> 0.85 us  [on_device(): updated = trail_rhs - jnp.concatenate(out_parts, axis=2)]
  transfers between devices with their start and end apart: 9 -> 28, of which waited for: 9 -> 6; matrix products, arithmetic and copies ran while one was open for 0% -> 1% of each run, Pallas kernels for 0% -> 12%
where the time goes in v2:
time: 70.7 us; the launch traced here: 70.4 us
  starting transfers between devices  52.3 us (74%)
  Pallas kernels  10.2 us (14%)
  waiting for transfers between devices  4.76 us (7%)
  other arithmetic  1.34 us (2%)
  between operations  1.03 us (1%)
  local copies, waits for them, and re-layouts  0.76 us (1%)
    ppermute x8, starting transfers between devices, halve(): lax.ppermute(high, 'row', [(i, i ^ 1 << bit) for i in range(rows)])  21.9 us
    ppermute x1, starting transfers between devices, on_device(): candidates.append(lax.ppermute(parts[t], 'row', pairs))  20.1 us
    pallas_call x9, Pallas kernels, local_call(): pl.pallas_call(kernel, in_specs=[VMEM] * len(near) + [ANY] * len(far), ou...  10.2 us
    ppermute x12, starting transfers between devices, send(): return lax.ppermute(value, ('row', 'col'), pairs)  8.04 us
    ppermute x8, waiting for transfers between devices, halve(): lax.ppermute(high, 'row', [(i, i ^ 1 << bit) for i in range(rows)])  4.61 us
  transfers between devices with their start and end apart: 28, of which 6 were waited for; matrix products, arithmetic and copies ran while one was open for 1% of the time, Pallas kernels for 12%

profile of v2, /device:TPU:0, one launch (start us, length us, event | category | flops | bytes accessed | tf_op | source)
XLA Modules:
  0.0 70.4 jit_solution(10874329667924890645)
XLA Ops:
  0.6 0.6 collective-permute-start.2
  1.2 0.1 collective-permute-start.1
  1.3 0.7 collective-permute-start.5
  1.9 0.7 collective-permute-start.4
  2.6 0.5 collective-permute-start
  3.1 1.0 %shard_map.94 = (f32[2,32,128]{2,1,0:T(8,128)S(1)}, f32[2,128,128]{2,1,0:T(8,128)S(1)}, f32[2,128]{1,0:T(2,128)S(1)}, s32[1,128]{1,0:T(1,128)S(1)}) custom-call(f32[2,32,128]{2,1,0:T(8,128)} %refs_0_.1, f32[2,128,128]{2,1,0:T(8,128)} %refs_1_.2, f32[2,128]{1,0:T(2,128)} %refs_2_.1, s32[1,128]{1,0:T(1,128)} %bitcast.65), custom_call_target="tpu_custom_call" | custom-call | tf_op jit(solution)/shard_map/pallas_call | solution.py:56
  4.1 0.1 collective-permute-done.refs_0_
  4.2 0.0 collective-permute-done.1.refs_2_
  4.2 0.0 collective-permute-done.2.refs_4_
  4.2 0.7 collective-permute-start.8
  4.9 0.7 collective-permute-start.7
  5.6 0.7 collective-permute-start.3
  6.2 0.0 collective-permute-done.4.refs_6_
  6.3 0.0 collective-permute-done.3.refs_5_
  6.3 0.7 collective-permute-start.6
  7.0 0.7 collective-permute-start.11
  7.7 0.7 collective-permute-start.10
  8.4 0.7 collective-permute-start.9
  9.2 0.7 collective-permute-start.14
  9.8 0.7 collective-permute-start.13
  10.5 0.7 collective-permute-start.12
  11.3 20.1 %collective-permute-start.15 = (f32[2,32,128]{2,1,0:T(8,128)S(1)}, f32[2,32,128]{2,1,0:T(8,128)S(1)}, u32[]{:S(2)}, u32[]{:S(2)}) collective-permute-start(f32[2,32,128]{2,1,0:T(8,128)S(1)} %get-tuple-element.30), channel_id=1, source_target_pairs={{0,4},{4,0},{8,12},{12,8},{16,20},{20,16},{24,28},{28,24},{1,5},{5... | collective-permute-start | bytes 98312 | tf_op jit(solution)/shard_map/ppermute | solution.py:312
  31.3 3.7 %shard_map.100 = (bf16[8,256,1024]{2,1,0:T(8,128)(2,1)S(1)}, bf16[8,256,1024]{2,1,0:T(8,128)(2,1)S(1)}) custom-call(f32[2,128,16384]{2,1,0:T(8,128)} %refs_1_.3), custom_call_target="tpu_custom_call" | custom-call | tf_op jit(solution)/shard_map/pallas_call | solution.py:56
  35.0 1.6 %shard_map.101 = (f32[2,32,128]{2,1,0:T(8,128)S(1)}, f32[4,32,1152]{2,1,0:T(8,128)S(1)}, f32[4,32,1024]{2,1,0:T(8,128)S(1)}, f32[4,32,1152]{2,1,0:T(8,128)S(1)},...) custom-call(f32[2,128]{1,0:T(2,128)S(1)} %get-tuple-element.24.currents, s32[1,128]{1,0:T(1,128)S(1)} %get-tuple-element.25.owner, ...), custom_call_target="tpu_custom_call" | custom-call | tf_op jit(solution)/shard_map/pallas_call | solution.py:56
  36.6 0.1 collective-permute-start.19
  36.7 3.8 %shard_map.102 = (f32[4,32,1024]{2,1,0:T(8,128)S(1)}, f32[4,32,1024]{2,1,0:T(8,128)S(1)}, f32[4,32,1024]{2,1,0:T(8,128)S(1)}, f32[4,32,1024]{2,1,0:T(8,128)S(1)}) custom-call(f32[2,128]{1,0:T(2,128)S(1)} %get-tuple-element.24.currents, s32[1,128]{1,0:T(1,128)S(1)} %get-tuple-element.25.owner, f32[2,32,128]{2,1,0:T(8,128)S(1)} %get-tuple-element.40.refs_0_, ...), custom_call_target="tpu_custom_call" | custom-call | tf_op jit(solution)/shard_map/pallas_call | solution.py:56
  40.5 0.6 collective-permute-start.22
  41.1 0.1 collective-permute-start.16
  41.2 0.4 collective-permute-start.25
  41.6 0.1 add.39
  41.7 3.0 %collective-permute-start.20 = (f32[2,32,1024]{2,1,0:T(8,128)S(1)}, f32[2,32,1024]{2,1,0:T(8,128)S(1)}, u32[]{:S(2)}, u32[]{:S(2)}) collective-permute-start(f32[2,32,1024]{2,1,0:T(8,128)S(1)} %slice.82), channel_id=1, source_target_pairs={{0,16},{4,20},{8,24},{12,28},{16,0},{20,4},{24,8},{28,12},{1,17},{... | collective-permute-start | bytes 786440 | tf_op jit(solution)/shard_map/ppermute | solution.py:223
  44.7 0.1 add.42
  44.8 5.3 %collective-permute-start.23 = (f32[2,32,1024]{2,1,0:T(8,128)S(1)}, f32[2,32,1024]{2,1,0:T(8,128)S(1)}, u32[]{:S(2)}, u32[]{:S(2)}) collective-permute-start(f32[2,32,1024]{2,1,0:T(8,128)S(1)} %slice_bitcast_fusion.2), channel_id=1, source_target_pairs={{0,8},{4,12},{8,0},{12,4},{16,24},{20,28},{24,16},{28,20},{1,9},{5... | collective-permute-start | bytes 786440 | tf_op jit(solution)/shard_map/ppermute | solution.py:223
  50.1 0.1 add.45
  50.2 0.9 %collective-permute-start.26 = (f32[2,32,1024]{2,1,0:T(8,128)S(1)}, f32[2,32,1024]{2,1,0:T(8,128)S(1)}, u32[]{:S(2)}, u32[]{:S(2)}) collective-permute-start(f32[2,32,1024]{2,1,0:T(8,128)S(1)} %slice.90), channel_id=1, source_target_pairs={{0,16},{4,20},{8,24},{12,28},{16,0},{20,4},{24,8},{28,12},{1,17},{... | collective-permute-start | bytes 786440 | tf_op jit(solution)/shard_map/ppermute | solution.py:223
  51.1 0.1 add.36
  51.3 1.5 %collective-permute-start.17 = (f32[2,32,1152]{2,1,0:T(8,128)S(1)}, f32[2,32,1152]{2,1,0:T(8,128)S(1)}, u32[]{:S(2)}, u32[]{:S(2)}) collective-permute-start(f32[2,32,1152]{2,1,0:T(8,128)S(1)} %slice_bitcast_fusion), channel_id=1, source_target_pairs={{0,8},{4,12},{8,0},{12,4},{16,24},{20,28},{24,16},{28,20},{1,9},{5... | collective-permute-start | bytes 884744 | tf_op jit(solution)/shard_map/ppermute | solution.py:223
  52.8 4.4 %collective-permute-start.21 = (f32[32,1024]{1,0:T(8,128)S(1)}, f32[32,1024]{1,0:T(8,128)S(1)}, u32[]{:S(2)}, u32[]{:S(2)}) collective-permute-start(f32[32,1024]{1,0:T(8,128)S(1)} %slice_bitcast_fusion.10), channel_id=1, source_target_pairs={{0,8},{4,12},{8,0},{12,4},{16,24},{20,28},{24,16},{28,20},{1,9},{5... | collective-permute-start | bytes 393224 | tf_op jit(solution)/shard_map/ppermute | solution.py:223
  57.2 0.1 collective-permute-done.23
  57.3 2.0 %collective-permute-start.24 = (f32[32,1024]{1,0:T(8,128)S(1)}, f32[32,1024]{1,0:T(8,128)S(1)}, u32[]{:S(2)}, u32[]{:S(2)}) collective-permute-start(f32[32,1024]{1,0:T(8,128)S(1)} %slice_bitcast_fusion.8), channel_id=1, source_target_pairs={{0,16},{4,20},{8,24},{12,28},{16,0},{20,4},{24,8},{28,12},{1,17},{... | collective-permute-start | bytes 393224 | tf_op jit(solution)/shard_map/ppermute | solution.py:223
  59.4 3.4 %collective-permute-start.27 = (f32[32,1024]{1,0:T(8,128)S(1)}, f32[32,1024]{1,0:T(8,128)S(1)}, u32[]{:S(2)}, u32[]{:S(2)}) collective-permute-start(f32[32,1024]{1,0:T(8,128)S(1)} %slice_bitcast_fusion.6), channel_id=1, source_target_pairs={{0,8},{4,12},{8,0},{12,4},{16,24},{20,28},{24,16},{28,20},{1,9},{5... | collective-permute-start | bytes 393224 | tf_op jit(solution)/shard_map/ppermute | solution.py:223
  62.8 0.8 %collective-permute-done.17 = f32[2,32,1152]{2,1,0:T(8,128)S(1)} collective-permute-done((f32[2,32,1152]{2,1,0:T(8,128)S(1)}, f32[2,32,1152]{2,1,0:T(8,128)S(1)}, u32[]{:S(2)}, u32[]{:S(2)}) %collective-permute-start.17) | collective-permute-done | bytes 294944 | tf_op jit(solution)/shard_map/ppermute | solution.py:223
  63.6 1.3 %collective-permute-start.18 = (f32[32,1152]{1,0:T(8,128)S(1)}, f32[32,1152]{1,0:T(8,128)S(1)}, u32[]{:S(2)}, u32[]{:S(2)}) collective-permute-start(f32[32,1152]{1,0:T(8,128)S(1)} %slice_bitcast_fusion.4), channel_id=1, source_target_pairs={{0,16},{4,20},{8,24},{12,28},{16,0},{20,4},{24,8},{28,12},{1,17},{... | collective-permute-start | bytes 442376 | tf_op jit(solution)/shard_map/ppermute | solution.py:223
  65.0 1.4 %collective-permute-done.21 = f32[32,1024]{1,0:T(8,128)S(1)} collective-permute-done((f32[32,1024]{1,0:T(8,128)S(1)}, f32[32,1024]{1,0:T(8,128)S(1)}, u32[]{:S(2)}, u32[]{:S(2)}) %collective-permute-start.21) | collective-permute-done | bytes 131104 | tf_op jit(solution)/shard_map/ppermute | solution.py:223
  66.4 1.9 %collective-permute-done.27 = f32[32,1024]{1,0:T(8,128)S(1)} collective-permute-done((f32[32,1024]{1,0:T(8,128)S(1)}, f32[32,1024]{1,0:T(8,128)S(1)}, u32[]{:S(2)}, u32[]{:S(2)}) %collective-permute-start.27) | collective-permute-done | bytes 131104 | tf_op jit(solution)/shard_map/ppermute | solution.py:223
  68.3 0.5 collective-permute-done.18
  68.9 0.6 slice_reduce_fusion
  69.5 0.9 %maximum_subtract_fusion = f32[2,32,2048]{2,1,0:T(8,128)} fusion(f32[2,32,2048]{2,1,0:T(8,128)S(1)} %copy-done, f32[1,32,1024]{2,1,0:T(8,128)S(1)} %fusion.4, f32[1,32,1024]{2,1,0:T(8,128)S(1)} %fusion.6, f32[1,32,1024]{2,1,0:T(8,128)S(1)} %fusion.8, f32[1,32,1024]{2,1,0:T(8,128)S(1)} %slice_bitcast_fusion.12), kind=kLoop, calls=%fused_computation | loop fusion | flops 524288 | bytes 1572864 | tf_op jit(solution)/shard_map/sub | solution.py:344
  (42 shorter events, 0.5 us)
Async XLA Ops:
  0.6 3.6 %collective-permute-start.2 = (f32[2,128,256]{2,1,0:T(8,128)}, f32[2,128,256]{2,1,0:T(8,128)S(1)}, u32[]{:S(2)}, u32[]{:S(2)}) collective-permute-start(f32[2,128,256]{2,1,0:T(8,128)} %param.7), channel_id=1, source_target_pairs={{0,4},{4,0},{8,12},{12,8},{16,20},{20,16},{24,28},{28,24},{1,5},{5... | collective-permute-start | bytes 786440 | tf_op jit(solution)/shard_map/ppermute | solution.py:259
  1.2 3.0 %collective-permute-start.1 = (f32[2,128,128]{2,1,0:T(8,128)}, f32[2,128,128]{2,1,0:T(8,128)S(1)}, u32[]{:S(2)}, u32[]{:S(2)}) collective-permute-start(f32[2,128,128]{2,1,0:T(8,128)} %refs_1_.2), channel_id=1, source_target_pairs={{0,4},{4,0},{8,12},{12,8},{16,20},{20,16},{24,28},{28,24},{1,5},{5... | collective-permute-start | bytes 393224 | tf_op jit(solution)/shard_map/ppermute | solution.py:258
  1.3 5.0 %collective-permute-start.5 = (f32[2,128,256]{2,1,0:T(8,128)}, f32[2,128,256]{2,1,0:T(8,128)S(1)}, u32[]{:S(2)}, u32[]{:S(2)}) collective-permute-start(f32[2,128,256]{2,1,0:T(8,128)} %param.7), channel_id=1, source_target_pairs={{5,13},{14,22},{23,31}} | collective-permute-start | bytes 786440 | tf_op jit(solution)/shard_map/ppermute | solution.py:243
  1.9 4.3 %collective-permute-start.4 = (f32[2,128,256]{2,1,0:T(8,128)}, f32[2,128,256]{2,1,0:T(8,128)S(1)}, u32[]{:S(2)}, u32[]{:S(2)}) collective-permute-start(f32[2,128,256]{2,1,0:T(8,128)} %param.7), channel_id=1, source_target_pairs={{1,13},{10,22},{19,31}} | collective-permute-start | bytes 786440 | tf_op jit(solution)/shard_map/ppermute | solution.py:243
  2.6 1.6 %collective-permute-start = (f32[2,32,128]{2,1,0:T(8,128)}, f32[2,32,128]{2,1,0:T(8,128)S(1)}, u32[]{:S(2)}, u32[]{:S(2)}) collective-permute-start(f32[2,32,128]{2,1,0:T(8,128)} %refs_0_.1), channel_id=1, source_target_pairs={{0,4},{4,0},{8,12},{12,8},{16,20},{20,16},{24,28},{28,24},{1,5},{5... | collective-permute-start | bytes 98312 | tf_op jit(solution)/shard_map/ppermute | solution.py:257
  4.2 4.2 %collective-permute-start.8 = (f32[2,128,256]{2,1,0:T(8,128)}, f32[2,128,256]{2,1,0:T(8,128)S(1)}, u32[]{:S(2)}, u32[]{:S(2)}) collective-permute-start(f32[2,128,256]{2,1,0:T(8,128)} %param.7), channel_id=1, source_target_pairs={{6,22},{15,31}} | collective-permute-start | bytes 786440 | tf_op jit(solution)/shard_map/ppermute | solution.py:243
  4.9 3.5 %collective-permute-start.7 = (f32[2,128,256]{2,1,0:T(8,128)}, f32[2,128,256]{2,1,0:T(8,128)S(1)}, u32[]{:S(2)}, u32[]{:S(2)}) collective-permute-start(f32[2,128,256]{2,1,0:T(8,128)} %param.7), channel_id=1, source_target_pairs={{2,22},{11,31}} | collective-permute-start | bytes 786440 | tf_op jit(solution)/shard_map/ppermute | solution.py:243
  5.6 0.7 collective-permute-start.3
  6.3 2.0 %collective-permute-start.6 = (f32[4,32,256]{2,1,0:T(8,128)S(1)}, f32[4,32,256]{2,1,0:T(8,128)S(1)}, u32[]{:S(2)}, u32[]{:S(2)}) collective-permute-start(f32[4,32,256]{2,1,0:T(8,128)S(1)} %shard_map.96.refs_13_), channel_id=1, source_target_pairs={{13,22}} | collective-permute-start | bytes 393224 | tf_op jit(solution)/shard_map/ppermute | solution.py:243
  7.0 2.1 %collective-permute-start.11 = (f32[2,128,256]{2,1,0:T(8,128)}, f32[2,128,256]{2,1,0:T(8,128)S(1)}, u32[]{:S(2)}, u32[]{:S(2)}) collective-permute-start(f32[2,128,256]{2,1,0:T(8,128)} %param.7), channel_id=1, source_target_pairs={{7,31}} | collective-permute-start | bytes 786440 | tf_op jit(solution)/shard_map/ppermute | solution.py:243
  7.7 1.4 %collective-permute-start.10 = (f32[2,128,256]{2,1,0:T(8,128)}, f32[2,128,256]{2,1,0:T(8,128)S(1)}, u32[]{:S(2)}, u32[]{:S(2)}) collective-permute-start(f32[2,128,256]{2,1,0:T(8,128)} %param.7), channel_id=1, source_target_pairs={{3,31}} | collective-permute-start | bytes 786440 | tf_op jit(solution)/shard_map/ppermute | solution.py:243
  8.4 0.7 %collective-permute-start.9 = (f32[6,32,256]{2,1,0:T(8,128)S(1)}, f32[6,32,256]{2,1,0:T(8,128)S(1)}, u32[]{:S(2)}, u32[]{:S(2)}) collective-permute-start(f32[6,32,256]{2,1,0:T(8,128)S(1)} %shard_map.97.refs_14_), channel_id=1, source_target_pairs={{22,31}} | collective-permute-start | bytes 589832 | tf_op jit(solution)/shard_map/ppermute | solution.py:243
  9.2 2.0 %collective-permute-start.14 = (f32[2,32,256]{2,1,0:T(8,128)S(1)}, f32[2,32,256]{2,1,0:T(8,128)S(1)}, u32[]{:S(2)}, u32[]{:S(2)}) collective-permute-start(f32[2,32,256]{2,1,0:T(8,128)S(1)} %shard_map.98.refs_0_), channel_id=1, source_target_pairs={{4,7},{13,12},{22,21},{31,30}} | collective-permute-start | bytes 196616 | tf_op jit(solution)/shard_map/ppermute | solution.py:243
  9.8 1.4 %collective-permute-start.13 = (f32[2,32,256]{2,1,0:T(8,128)S(1)}, f32[2,32,256]{2,1,0:T(8,128)S(1)}, u32[]{:S(2)}, u32[]{:S(2)}) collective-permute-start(f32[2,32,256]{2,1,0:T(8,128)S(1)} %shard_map.98.refs_0_), channel_id=1, source_target_pairs={{4,6},{13,15},{22,20},{31,29}} | collective-permute-start | bytes 196616 | tf_op jit(solution)/shard_map/ppermute | solution.py:243
  10.5 0.7 collective-permute-start.12
  11.3 23.8 %collective-permute-start.15 = (f32[2,32,128]{2,1,0:T(8,128)S(1)}, f32[2,32,128]{2,1,0:T(8,128)S(1)}, u32[]{:S(2)}, u32[]{:S(2)}) collective-permute-start(f32[2,32,128]{2,1,0:T(8,128)S(1)} %get-tuple-element.30), channel_id=1, source_target_pairs={{0,4},{4,0},{8,12},{12,8},{16,20},{20,16},{24,28},{28,24},{1,5},{5... | collective-permute-start | bytes 98312 | tf_op jit(solution)/shard_map/ppermute | solution.py:312
  36.6 5.0 %collective-permute-start.19 = (f32[4,32,1024]{2,1,0:T(8,128)S(1)}, f32[4,32,1024]{2,1,0:T(8,128)S(1)}, u32[]{:S(2)}, u32[]{:S(2)}) collective-permute-start(f32[4,32,1024]{2,1,0:T(8,128)S(1)} %get-tuple-element.39), channel_id=1, source_target_pairs={{0,4},{4,0},{8,12},{12,8},{16,20},{20,16},{24,28},{28,24},{1,5},{5... | collective-permute-start | bytes 1572872 | tf_op jit(solution)/shard_map/ppermute | solution.py:332
  40.5 4.2 %collective-permute-start.22 = (f32[4,32,1024]{2,1,0:T(8,128)S(1)}, f32[4,32,1024]{2,1,0:T(8,128)S(1)}, u32[]{:S(2)}, u32[]{:S(2)}) collective-permute-start(f32[4,32,1024]{2,1,0:T(8,128)S(1)} %get-tuple-element.42), channel_id=1, source_target_pairs={{0,4},{4,0},{8,12},{12,8},{16,20},{20,16},{24,28},{28,24},{1,5},{5... | collective-permute-start | bytes 1572872 | tf_op jit(solution)/shard_map/ppermute | solution.py:332
  41.1 10.1 %collective-permute-start.16 = (f32[4,32,1152]{2,1,0:T(8,128)S(1)}, f32[4,32,1152]{2,1,0:T(8,128)S(1)}, u32[]{:S(2)}, u32[]{:S(2)}) collective-permute-start(f32[4,32,1152]{2,1,0:T(8,128)S(1)} %get-tuple-element.37), channel_id=1, source_target_pairs={{0,4},{4,0},{8,12},{12,8},{16,20},{20,16},{24,28},{28,24},{1,5},{5... | collective-permute-start | bytes 1769480 | tf_op jit(solution)/shard_map/ppermute | solution.py:332
  41.2 8.9 %collective-permute-start.25 = (f32[4,32,1024]{2,1,0:T(8,128)S(1)}, f32[4,32,1024]{2,1,0:T(8,128)S(1)}, u32[]{:S(2)}, u32[]{:S(2)}) collective-permute-start(f32[4,32,1024]{2,1,0:T(8,128)S(1)} %get-tuple-element.44), channel_id=1, source_target_pairs={{0,4},{4,0},{8,12},{12,8},{16,20},{20,16},{24,28},{28,24},{1,5},{5... | collective-permute-start | bytes 1572872 | tf_op jit(solution)/shard_map/ppermute | solution.py:332
  41.7 11.1 %collective-permute-start.20 = (f32[2,32,1024]{2,1,0:T(8,128)S(1)}, f32[2,32,1024]{2,1,0:T(8,128)S(1)}, u32[]{:S(2)}, u32[]{:S(2)}) collective-permute-start(f32[2,32,1024]{2,1,0:T(8,128)S(1)} %slice.82), channel_id=1, source_target_pairs={{0,16},{4,20},{8,24},{12,28},{16,0},{20,4},{24,8},{28,12},{1,17},{... | collective-permute-start | bytes 786440 | tf_op jit(solution)/shard_map/ppermute | solution.py:223
  44.8 12.5 %collective-permute-start.23 = (f32[2,32,1024]{2,1,0:T(8,128)S(1)}, f32[2,32,1024]{2,1,0:T(8,128)S(1)}, u32[]{:S(2)}, u32[]{:S(2)}) collective-permute-start(f32[2,32,1024]{2,1,0:T(8,128)S(1)} %slice_bitcast_fusion.2), channel_id=1, source_target_pairs={{0,8},{4,12},{8,0},{12,4},{16,24},{20,28},{24,16},{28,20},{1,9},{5... | collective-permute-start | bytes 786440 | tf_op jit(solution)/shard_map/ppermute | solution.py:223
  50.2 9.1 %collective-permute-start.26 = (f32[2,32,1024]{2,1,0:T(8,128)S(1)}, f32[2,32,1024]{2,1,0:T(8,128)S(1)}, u32[]{:S(2)}, u32[]{:S(2)}) collective-permute-start(f32[2,32,1024]{2,1,0:T(8,128)S(1)} %slice.90), channel_id=1, source_target_pairs={{0,16},{4,20},{8,24},{12,28},{16,0},{20,4},{24,8},{28,12},{1,17},{... | collective-permute-start | bytes 786440 | tf_op jit(solution)/shard_map/ppermute | solution.py:223
  51.1 18.4 %copy-start = (f32[2,32,2048]{2,1,0:T(8,128)S(1)}, f32[2,32,2048]{2,1,0:T(8,128)}, u32[]{:S(2)}) copy-start(f32[2,32,2048]{2,1,0:T(8,128)} %param.11) | copy-start | bytes 1572868
  51.3 12.3 %collective-permute-start.17 = (f32[2,32,1152]{2,1,0:T(8,128)S(1)}, f32[2,32,1152]{2,1,0:T(8,128)S(1)}, u32[]{:S(2)}, u32[]{:S(2)}) collective-permute-start(f32[2,32,1152]{2,1,0:T(8,128)S(1)} %slice_bitcast_fusion), channel_id=1, source_target_pairs={{0,8},{4,12},{8,0},{12,4},{16,24},{20,28},{24,16},{28,20},{1,9},{5... | collective-permute-start | bytes 884744 | tf_op jit(solution)/shard_map/ppermute | solution.py:223
  52.8 13.6 %collective-permute-start.21 = (f32[32,1024]{1,0:T(8,128)S(1)}, f32[32,1024]{1,0:T(8,128)S(1)}, u32[]{:S(2)}, u32[]{:S(2)}) collective-permute-start(f32[32,1024]{1,0:T(8,128)S(1)} %slice_bitcast_fusion.10), channel_id=1, source_target_pairs={{0,8},{4,12},{8,0},{12,4},{16,24},{20,28},{24,16},{28,20},{1,9},{5... | collective-permute-start | bytes 393224 | tf_op jit(solution)/shard_map/ppermute | solution.py:223
  57.3 9.1 %collective-permute-start.24 = (f32[32,1024]{1,0:T(8,128)S(1)}, f32[32,1024]{1,0:T(8,128)S(1)}, u32[]{:S(2)}, u32[]{:S(2)}) collective-permute-start(f32[32,1024]{1,0:T(8,128)S(1)} %slice_bitcast_fusion.8), channel_id=1, source_target_pairs={{0,16},{4,20},{8,24},{12,28},{16,0},{20,4},{24,8},{28,12},{1,17},{... | collective-permute-start | bytes 393224 | tf_op jit(solution)/shard_map/ppermute | solution.py:223
  59.4 8.9 %collective-permute-start.27 = (f32[32,1024]{1,0:T(8,128)S(1)}, f32[32,1024]{1,0:T(8,128)S(1)}, u32[]{:S(2)}, u32[]{:S(2)}) collective-permute-start(f32[32,1024]{1,0:T(8,128)S(1)} %slice_bitcast_fusion.6), channel_id=1, source_target_pairs={{0,8},{4,12},{8,0},{12,4},{16,24},{20,28},{24,16},{28,20},{1,9},{5... | collective-permute-start | bytes 393224 | tf_op jit(solution)/shard_map/ppermute | solution.py:223
  63.6 5.2 %collective-permute-start.18 = (f32[32,1152]{1,0:T(8,128)S(1)}, f32[32,1152]{1,0:T(8,128)S(1)}, u32[]{:S(2)}, u32[]{:S(2)}) collective-permute-start(f32[32,1152]{1,0:T(8,128)S(1)} %slice_bitcast_fusion.4), channel_id=1, source_target_pairs={{0,16},{4,20},{8,24},{12,28},{16,0},{20,4},{24,8},{28,12},{1,17},{... | collective-permute-start | bytes 442376 | tf_op jit(solution)/shard_map/ppermute | solution.py:223

commit v3 on v2

--- a/solution.py
+++ b/solution.py
@@ -50,7 +50,7 @@
 ANY = pl.BlockSpec(memory_space=pl.ANY)
 
 
-def local_call(kernel, outs, near, far=(), scratch=(), limit=16 << 20, far_outs=()):
+def local_call(kernel, outs, near, far=(), scratch=(), limit=16 << 20, far_outs=(), aliases=None):
     near = [pltpu.with_memory_space_constraint(a, pltpu.VMEM) for a in near]
     far = [pltpu.with_memory_space_constraint(a, pltpu.HBM) for a in far]
     return pl.pallas_call(
@@ -60,6 +60,7 @@
         out_shape=[pltpu.VMEM(shape, dtype) for shape, dtype in outs]
         + [pltpu.HBM(shape, dtype) for shape, dtype in far_outs],
         scratch_shapes=scratch,
+        input_output_aliases=aliases or {},
         compiler_params=pltpu.CompilerParams(vmem_limit_bytes=limit),
     )(*near, *far)
 
@@ -135,6 +136,14 @@
                 outs[t][...] = source[:, :, t * width : (t + 1) * width]
 
 
+def when_kernel(last, members, skip, kernel, *refs):
+    inside = lax.axis_index("row") >= lax.axis_size("row") - members
+
+    @pl.when(inside if last else jnp.logical_not(inside))
+    def _():
+        kernel(*refs[skip[0] : skip[1]], *refs[skip[2] :])
+
+
 def prepare_kernel(chunk, chunks, trail, high, low, room, sems):
     devices, columns = room.shape[0], room.shape[3]
     copies = []
@@ -151,30 +160,33 @@
             low[i, part * depth : (part + 1) * depth] = b
 
 
-def trail_kernel(chunk, chunks, cols, ready, members, currents, owner, *refs):
+def trail_kernel(chunk, chunks, cols, ready, select, odds, members, currents, owner, *refs):
     row = lax.axis_index("row")
-    if ready:
-        candidates, refs = refs[:members], refs[members:]
-        high, low, x, sent_a, sent_b, kept_a, kept_b, solved, sem = refs
+    refs = list(refs)
+    candidates = [refs.pop(0) for _ in range(members if select else 1)]
+    factors = [refs.pop(0) for _ in range(2 if ready else 1)]
+    x = refs.pop(0) if select else candidates[0]
+    outs = {odd: (refs.pop(0), refs.pop(0)) for odd in odds}
+    if select:
+        solved, sem = refs
         for t in range(members):
             @pl.when(lax.rem(row, members) == t)
             def _(t=t):
                 x[...] = candidates[t][...]
         out = pltpu.make_async_copy(x, solved, sem)
         out.start()
-    else:
-        x, refs = refs[0], refs[1:]
     observers, depth = x.shape[1], x.shape[2]
     if ready:
+        high, low = factors
         devices, columns = high.shape[0], high.shape[2]
     else:
-        trail, sent_a, sent_b, kept_a, kept_b, room, sems = refs
+        trail, (room, sems) = factors[0], refs
         devices, columns = room.shape[0], room.shape[3]
     half = devices // 2
-    targets = [row ^ (2 * (i % half) + (1 if i < half else 0)) for i in range(devices)]
+    work = [(row ^ (2 * e + odd), e, odd) for odd in odds for e in range(half)]
     copies = []
     if not ready:
-        for i, target in enumerate(targets):
+        for i, (target, _, _) in enumerate(work):
             start = pl.multiple_of((target * chunks + chunk) * columns, LANES)
             copies.append(pltpu.make_async_copy(trail.at[:, :, pl.ds(start, columns)], room.at[i], sems.at[i]))
             copies[-1].start()
@@ -185,15 +197,14 @@
         lefts = [split(first), split(second)]
     lefts = [(a, jnp.concatenate([a, b], axis=0)) for a, b in lefts]
     share = 2 * depth // len(lefts)
-    extra = kept_a.shape[2] - columns
+    extra = outs[odds[0]][0].shape[2] - columns
     if extra:
         col = lax.axis_index("col")
         sums = jnp.sum(x[...], axis=1, keepdims=True)
         partial = currents[0:1] * sums[0] - currents[1:2] * sums[1]
         patch = lax.broadcasted_iota(jnp.int32, (observers, depth), 0)
-    for i, target in enumerate(targets):
-        e = i % half
-        ref_a, ref_b = (sent_a, sent_b) if i < half else (kept_a, kept_b)
+    for i, (target, e, odd) in enumerate(work):
+        ref_a, ref_b = outs[odd]
         total = None
         if not ready:
             copies[i].wait()
@@ -213,7 +224,7 @@
             found = jnp.where(owner[...] == patch + (target * cols + col) * PATCH_DEV, partial, 0.0)
             gradient = jnp.sum(found, axis=1, keepdims=True)
             ref_a[e, :, columns:] = jnp.broadcast_to(gradient, (observers, extra))
-    if ready:
+    if select:
         out.wait()
 
 
@@ -314,23 +325,50 @@
 
     half = rows // 2
     out_parts, gradient, factor, solved = [], None, None, None
+    small = [currents_near, owner_near]
     for chunk in range(CHUNKS):
         extra = LANES if chunk == 0 else 0
-        real, imag = (half, observers, columns + extra), (half, observers, columns)
-        results = local_call(
-            functools.partial(trail_kernel, chunk, CHUNKS, cols, chunk == 0, members),
-            [(a, jnp.float32) for a in ([candidates[0].shape] if chunk == 0 else []) + [real, imag, real, imag]],
-            [currents_near, owner_near, *([*candidates, *ready] if chunk == 0 else [factor])],
-            [] if chunk == 0 else [upper_trail],
-            [pltpu.SemaphoreType.DMA] if chunk == 0 else room,
-            far_outs=[(candidates[0].shape, jnp.float32)] if chunk == 0 else [],
-        )
+        shapes = [((half, observers, columns + extra), jnp.float32), ((half, observers, columns), jnp.float32)]
+
+        def trail(select, odds, operands, far, scratch):
+            return local_call(
+                functools.partial(trail_kernel, chunk, CHUNKS, cols, chunk == 0, select, odds, members),
+                ([(candidates[0].shape, jnp.float32)] if select else []) + shapes * len(odds),
+                [*small, *operands],
+                far,
+                scratch,
+                far_outs=[(candidates[0].shape, jnp.float32)] if select else [],
+            )
+
         if chunk == 0:
-            factor, *results, solved = results
+            factor, *sent, solved = trail(True, (1,), [*candidates, *ready], [], [pltpu.SemaphoreType.DMA])
+            kept = trail(False, (0,), [after(factor, sent[0]), *ready], [], [])
+        else:
+            kernel = functools.partial(trail_kernel, chunk, CHUNKS, cols, False, False, (1, 0), members)
+            outs = shapes * 2
+            operands = [*small, factor]
+            count = len(operands)
+            results = local_call(
+                functools.partial(when_kernel, False, members, (0, count, count), kernel),
+                outs,
+                [*small, after(factor, kept[0])],
+                [upper_trail],
+                room,
+            )
+            total = count + len(outs)
+            results = local_call(
+                functools.partial(when_kernel, True, members, (0, count, total), kernel),
+                outs,
+                [*operands, *results],
+                [upper_trail],
+                room,
+                aliases={count + i: i for i in range(len(outs))},
+            )
+            sent, kept = results[:2], results[2:]
         parts = []
         for part in range(2):
-            arrived = lax.ppermute(results[part], "row", [(i, i ^ 1) for i in range(rows)])
-            value = results[2 + part] + arrived
+            arrived = lax.ppermute(sent[part], "row", [(i, i ^ 1) for i in range(rows)])
+            value = kept[part] + arrived
             value = value.reshape((2,) * (bits - 1) + value.shape[1:])
             left = list(range(bits - 1, 0, -1))
             order = left[::-1] if part == 0 else left[:]

time: 70.7 us -> 70.9 us (level)
    pallas_call x9 -> x11, Pallas kernels: 10.2 us -> 10.4 us  [local_call(): pl.pallas_call(kernel, in_specs=[VMEM] * len(near) + [ANY] * len(far), ou...]
where the time goes in v3:
time: 70.9 us; the launch traced here: 70.6 us
  starting transfers between devices  52.3 us (74%)
  Pallas kernels  10.4 us (15%)
  waiting for transfers between devices  4.75 us (7%)
  other arithmetic  1.37 us (2%)
  between operations  1.04 us (1%)
  local copies, waits for them, and re-layouts  0.76 us (1%)
    ppermute x8, starting transfers between devices, halve(): lax.ppermute(high, 'row', [(i, i ^ 1 << bit) for i in range(rows)])  21.9 us
    ppermute x1, starting transfers between devices, on_device(): candidates.append(lax.ppermute(parts[t], 'row', pairs))  20.1 us
    pallas_call x11, Pallas kernels, local_call(): pl.pallas_call(kernel, in_specs=[VMEM] * len(near) + [ANY] * len(far), ou...  10.4 us
    ppermute x12, starting transfers between devices, send(): return lax.ppermute(value, ('row', 'col'), pairs)  8.04 us
    ppermute x8, waiting for transfers between devices, halve(): lax.ppermute(high, 'row', [(i, i ^ 1 << bit) for i in range(rows)])  4.6 us
  transfers between devices with their start and end apart: 28, of which 6 were waited for; matrix products, arithmetic and copies ran while one was open for 1% of the time, Pallas kernels for 12%

profile of v3, /device:TPU:0, one launch (start us, length us, event | category | flops | bytes accessed | tf_op | source)
XLA Modules:
  0.0 70.6 jit_solution(12846797968090060002)
XLA Ops:
  0.6 0.6 collective-permute-start.2
  1.2 0.1 collective-permute-start.1
  1.3 0.7 collective-permute-start.5
  1.9 0.7 collective-permute-start.4
  2.6 0.5 collective-permute-start
  3.1 1.0 %shard_map.94 = (f32[2,32,128]{2,1,0:T(8,128)S(1)}, f32[2,128,128]{2,1,0:T(8,128)S(1)}, f32[2,128]{1,0:T(2,128)S(1)}, s32[1,128]{1,0:T(1,128)S(1)}) custom-call(f32[2,32,128]{2,1,0:T(8,128)} %refs_0_.1, f32[2,128,128]{2,1,0:T(8,128)} %refs_1_.1, f32[2,128]{1,0:T(2,128)} %refs_2_.1, s32[1,128]{1,0:T(1,128)} %bitcast.65), custom_call_target="tpu_custom_call" | custom-call | tf_op jit(solution)/shard_map/pallas_call | solution.py:56
  4.1 0.1 collective-permute-done.refs_0_
  4.2 0.0 collective-permute-done.1.refs_2_
  4.2 0.7 collective-permute-start.8
  4.9 0.7 collective-permute-start.7
  5.6 0.7 collective-permute-start.3
  6.3 0.7 collective-permute-start.6
  7.0 0.7 collective-permute-start.11
  7.7 0.7 collective-permute-start.10
  8.4 0.7 collective-permute-start.9
  9.2 0.7 collective-permute-start.14
  9.8 0.7 collective-permute-start.13
  10.5 0.7 collective-permute-start.12
  11.3 20.1 %collective-permute-start.15 = (f32[2,32,128]{2,1,0:T(8,128)S(1)}, f32[2,32,128]{2,1,0:T(8,128)S(1)}, u32[]{:S(2)}, u32[]{:S(2)}) collective-permute-start(f32[2,32,128]{2,1,0:T(8,128)S(1)} %get-tuple-element.36), channel_id=1, source_target_pairs={{0,4},{4,0},{8,12},{12,8},{16,20},{20,16},{24,28},{28,24},{1,5},{5... | collective-permute-start | bytes 98312 | tf_op jit(solution)/shard_map/ppermute | solution.py:323
  31.3 3.7 %shard_map.100 = (bf16[8,256,1024]{2,1,0:T(8,128)(2,1)S(1)}, bf16[8,256,1024]{2,1,0:T(8,128)(2,1)S(1)}) custom-call(f32[2,128,16384]{2,1,0:T(8,128)} %refs_7_.1), custom_call_target="tpu_custom_call" | custom-call | tf_op jit(solution)/shard_map/pallas_call | solution.py:56
  35.0 0.9 %shard_map.101 = (f32[2,32,128]{2,1,0:T(8,128)S(1)}, f32[4,32,1152]{2,1,0:T(8,128)S(1)}, f32[4,32,1024]{2,1,0:T(8,128)S(1)}, f32[2,32,128]{2,1,0:T(8,128)}) custom-call(f32[2,128]{1,0:T(2,128)S(1)} %get-tuple-element.30.currents.refs_0_, s32[1,128]{1,0:T(1,128)S(1)} %get-tuple-element.31.owner.refs_1_, f32[2,32,128]{2,1,0:T(8,128)S(1)} %collective-permute-done.15.refs_0_, ...), custom_call_target="tpu_custom_call" | custom-call | tf_op jit(solution)/shard_map/pallas_call | solution.py:56
  35.9 0.8 %shard_map.102 = (f32[4,32,1152]{2,1,0:T(8,128)S(1)}, f32[4,32,1024]{2,1,0:T(8,128)S(1)}) custom-call(f32[2,128]{1,0:T(2,128)S(1)} %get-tuple-element.30.currents.refs_0_, s32[1,128]{1,0:T(1,128)S(1)} %get-tuple-element.31.owner.refs_1_, f32[2,32,128]{2,1,0:T(8,128)S(1)} %get-tuple-element.48.refs_0_.refs_2_, ...), custom_call_target="tpu_custom_call" | custom-call | tf_op jit(solution)/shard_map/pallas_call | solution.py:56
  36.8 0.1 collective-permute-start.19
  36.8 3.8 %shard_map.103 = (f32[4,32,1024]{2,1,0:T(8,128)S(1)}, f32[4,32,1024]{2,1,0:T(8,128)S(1)}, f32[4,32,1024]{2,1,0:T(8,128)S(1)}, f32[4,32,1024]{2,1,0:T(8,128)S(1)}) custom-call(f32[2,128]{1,0:T(2,128)S(1)} %get-tuple-element.30.currents.refs_0_, s32[1,128]{1,0:T(1,128)S(1)} %get-tuple-element.31.owner.refs_1_, ...), custom_call_target="tpu_custom_call" | custom-call | tf_op jit(solution)/shard_map/pallas_call | solution.py:56
  40.7 0.1 shard_map.104
  40.8 0.5 collective-permute-start.22
  41.3 0.1 collective-permute-start.16
  41.4 0.4 collective-permute-start.25
  41.8 0.1 add.39
  41.9 3.0 %collective-permute-start.20 = (f32[2,32,1024]{2,1,0:T(8,128)S(1)}, f32[2,32,1024]{2,1,0:T(8,128)S(1)}, u32[]{:S(2)}, u32[]{:S(2)}) collective-permute-start(f32[2,32,1024]{2,1,0:T(8,128)S(1)} %slice.82), channel_id=1, source_target_pairs={{0,16},{4,20},{8,24},{12,28},{16,0},{20,4},{24,8},{28,12},{1,17},{... | collective-permute-start | bytes 786440 | tf_op jit(solution)/shard_map/ppermute | solution.py:234
  44.9 0.1 add.42
  45.0 5.3 %collective-permute-start.23 = (f32[2,32,1024]{2,1,0:T(8,128)S(1)}, f32[2,32,1024]{2,1,0:T(8,128)S(1)}, u32[]{:S(2)}, u32[]{:S(2)}) collective-permute-start(f32[2,32,1024]{2,1,0:T(8,128)S(1)} %slice_bitcast_fusion.2), channel_id=1, source_target_pairs={{0,8},{4,12},{8,0},{12,4},{16,24},{20,28},{24,16},{28,20},{1,9},{5... | collective-permute-start | bytes 786440 | tf_op jit(solution)/shard_map/ppermute | solution.py:234
  50.3 0.1 add.45
  50.4 0.0 copy-start
  50.5 0.9 %collective-permute-start.26 = (f32[2,32,1024]{2,1,0:T(8,128)S(1)}, f32[2,32,1024]{2,1,0:T(8,128)S(1)}, u32[]{:S(2)}, u32[]{:S(2)}) collective-permute-start(f32[2,32,1024]{2,1,0:T(8,128)S(1)} %slice.90), channel_id=1, source_target_pairs={{0,16},{4,20},{8,24},{12,28},{16,0},{20,4},{24,8},{28,12},{1,17},{... | collective-permute-start | bytes 786440 | tf_op jit(solution)/shard_map/ppermute | solution.py:234
  51.4 0.1 add.36
  51.5 1.5 %collective-permute-start.17 = (f32[2,32,1152]{2,1,0:T(8,128)S(1)}, f32[2,32,1152]{2,1,0:T(8,128)S(1)}, u32[]{:S(2)}, u32[]{:S(2)}) collective-permute-start(f32[2,32,1152]{2,1,0:T(8,128)S(1)} %slice_bitcast_fusion), channel_id=1, source_target_pairs={{0,8},{4,12},{8,0},{12,4},{16,24},{20,28},{24,16},{28,20},{1,9},{5... | collective-permute-start | bytes 884744 | tf_op jit(solution)/shard_map/ppermute | solution.py:234
  53.0 4.4 %collective-permute-start.21 = (f32[32,1024]{1,0:T(8,128)S(1)}, f32[32,1024]{1,0:T(8,128)S(1)}, u32[]{:S(2)}, u32[]{:S(2)}) collective-permute-start(f32[32,1024]{1,0:T(8,128)S(1)} %slice_bitcast_fusion.10), channel_id=1, source_target_pairs={{0,8},{4,12},{8,0},{12,4},{16,24},{20,28},{24,16},{28,20},{1,9},{5... | collective-permute-start | bytes 393224 | tf_op jit(solution)/shard_map/ppermute | solution.py:234
  57.4 0.1 collective-permute-done.23
  57.5 2.0 %collective-permute-start.24 = (f32[32,1024]{1,0:T(8,128)S(1)}, f32[32,1024]{1,0:T(8,128)S(1)}, u32[]{:S(2)}, u32[]{:S(2)}) collective-permute-start(f32[32,1024]{1,0:T(8,128)S(1)} %slice_bitcast_fusion.8), channel_id=1, source_target_pairs={{0,16},{4,20},{8,24},{12,28},{16,0},{20,4},{24,8},{28,12},{1,17},{... | collective-permute-start | bytes 393224 | tf_op jit(solution)/shard_map/ppermute | solution.py:234
  59.6 3.4 %collective-permute-start.27 = (f32[32,1024]{1,0:T(8,128)S(1)}, f32[32,1024]{1,0:T(8,128)S(1)}, u32[]{:S(2)}, u32[]{:S(2)}) collective-permute-start(f32[32,1024]{1,0:T(8,128)S(1)} %slice_bitcast_fusion.6), channel_id=1, source_target_pairs={{0,8},{4,12},{8,0},{12,4},{16,24},{20,28},{24,16},{28,20},{1,9},{5... | collective-permute-start | bytes 393224 | tf_op jit(solution)/shard_map/ppermute | solution.py:234
  63.1 0.8 %collective-permute-done.17 = f32[2,32,1152]{2,1,0:T(8,128)S(1)} collective-permute-done((f32[2,32,1152]{2,1,0:T(8,128)S(1)}, f32[2,32,1152]{2,1,0:T(8,128)S(1)}, u32[]{:S(2)}, u32[]{:S(2)}) %collective-permute-start.17) | collective-permute-done | bytes 294944 | tf_op jit(solution)/shard_map/ppermute | solution.py:234
  63.9 1.3 %collective-permute-start.18 = (f32[32,1152]{1,0:T(8,128)S(1)}, f32[32,1152]{1,0:T(8,128)S(1)}, u32[]{:S(2)}, u32[]{:S(2)}) collective-permute-start(f32[32,1152]{1,0:T(8,128)S(1)} %slice_bitcast_fusion.4), channel_id=1, source_target_pairs={{0,16},{4,20},{8,24},{12,28},{16,0},{20,4},{24,8},{28,12},{1,17},{... | collective-permute-start | bytes 442376 | tf_op jit(solution)/shard_map/ppermute | solution.py:234
  65.2 1.4 %collective-permute-done.21 = f32[32,1024]{1,0:T(8,128)S(1)} collective-permute-done((f32[32,1024]{1,0:T(8,128)S(1)}, f32[32,1024]{1,0:T(8,128)S(1)}, u32[]{:S(2)}, u32[]{:S(2)}) %collective-permute-start.21) | collective-permute-done | bytes 131104 | tf_op jit(solution)/shard_map/ppermute | solution.py:234
  66.7 1.9 %collective-permute-done.27 = f32[32,1024]{1,0:T(8,128)S(1)} collective-permute-done((f32[32,1024]{1,0:T(8,128)S(1)}, f32[32,1024]{1,0:T(8,128)S(1)}, u32[]{:S(2)}, u32[]{:S(2)}) %collective-permute-start.27) | collective-permute-done | bytes 131104 | tf_op jit(solution)/shard_map/ppermute | solution.py:234
  68.6 0.5 collective-permute-done.18
  69.1 0.6 slice_reduce_fusion
  69.8 0.9 %maximum_subtract_fusion = f32[2,32,2048]{2,1,0:T(8,128)} fusion(f32[2,32,2048]{2,1,0:T(8,128)S(1)} %copy-done, f32[1,32,1024]{2,1,0:T(8,128)S(1)} %fusion.4, f32[1,32,1024]{2,1,0:T(8,128)S(1)} %fusion.6, f32[1,32,1024]{2,1,0:T(8,128)S(1)} %fusion.8, f32[1,32,1024]{2,1,0:T(8,128)S(1)} %slice_bitcast_fusion.12), kind=kLoop, calls=%fused_computation | loop fusion | flops 524288 | bytes 1572864 | tf_op jit(solution)/shard_map/sub | solution.py:382
  (44 shorter events, 0.5 us)
Async XLA Ops:
  0.6 3.6 %collective-permute-start.2 = (f32[2,128,256]{2,1,0:T(8,128)}, f32[2,128,256]{2,1,0:T(8,128)S(1)}, u32[]{:S(2)}, u32[]{:S(2)}) collective-permute-start(f32[2,128,256]{2,1,0:T(8,128)} %param.7), channel_id=1, source_target_pairs={{0,4},{4,0},{8,12},{12,8},{16,20},{20,16},{24,28},{28,24},{1,5},{5... | collective-permute-start | bytes 786440 | tf_op jit(solution)/shard_map/ppermute | solution.py:270
  1.2 3.0 %collective-permute-start.1 = (f32[2,128,128]{2,1,0:T(8,128)}, f32[2,128,128]{2,1,0:T(8,128)S(1)}, u32[]{:S(2)}, u32[]{:S(2)}) collective-permute-start(f32[2,128,128]{2,1,0:T(8,128)} %refs_1_.1), channel_id=1, source_target_pairs={{0,4},{4,0},{8,12},{12,8},{16,20},{20,16},{24,28},{28,24},{1,5},{5... | collective-permute-start | bytes 393224 | tf_op jit(solution)/shard_map/ppermute | solution.py:269
  1.3 5.0 %collective-permute-start.5 = (f32[2,128,256]{2,1,0:T(8,128)}, f32[2,128,256]{2,1,0:T(8,128)S(1)}, u32[]{:S(2)}, u32[]{:S(2)}) collective-permute-start(f32[2,128,256]{2,1,0:T(8,128)} %param.7), channel_id=1, source_target_pairs={{5,13},{14,22},{23,31}} | collective-permute-start | bytes 786440 | tf_op jit(solution)/shard_map/ppermute | solution.py:254
  1.9 4.3 %collective-permute-start.4 = (f32[2,128,256]{2,1,0:T(8,128)}, f32[2,128,256]{2,1,0:T(8,128)S(1)}, u32[]{:S(2)}, u32[]{:S(2)}) collective-permute-start(f32[2,128,256]{2,1,0:T(8,128)} %param.7), channel_id=1, source_target_pairs={{1,13},{10,22},{19,31}} | collective-permute-start | bytes 786440 | tf_op jit(solution)/shard_map/ppermute | solution.py:254
  2.6 1.6 %collective-permute-start = (f32[2,32,128]{2,1,0:T(8,128)}, f32[2,32,128]{2,1,0:T(8,128)S(1)}, u32[]{:S(2)}, u32[]{:S(2)}) collective-permute-start(f32[2,32,128]{2,1,0:T(8,128)} %refs_0_.1), channel_id=1, source_target_pairs={{0,4},{4,0},{8,12},{12,8},{16,20},{20,16},{24,28},{28,24},{1,5},{5... | collective-permute-start | bytes 98312 | tf_op jit(solution)/shard_map/ppermute | solution.py:268
  4.2 4.2 %collective-permute-start.8 = (f32[2,128,256]{2,1,0:T(8,128)}, f32[2,128,256]{2,1,0:T(8,128)S(1)}, u32[]{:S(2)}, u32[]{:S(2)}) collective-permute-start(f32[2,128,256]{2,1,0:T(8,128)} %param.7), channel_id=1, source_target_pairs={{6,22},{15,31}} | collective-permute-start | bytes 786440 | tf_op jit(solution)/shard_map/ppermute | solution.py:254
  4.9 3.5 %collective-permute-start.7 = (f32[2,128,256]{2,1,0:T(8,128)}, f32[2,128,256]{2,1,0:T(8,128)S(1)}, u32[]{:S(2)}, u32[]{:S(2)}) collective-permute-start(f32[2,128,256]{2,1,0:T(8,128)} %param.7), channel_id=1, source_target_pairs={{2,22},{11,31}} | collective-permute-start | bytes 786440 | tf_op jit(solution)/shard_map/ppermute | solution.py:254
  5.6 0.7 collective-permute-start.3
  6.3 2.0 %collective-permute-start.6 = (f32[4,32,256]{2,1,0:T(8,128)S(1)}, f32[4,32,256]{2,1,0:T(8,128)S(1)}, u32[]{:S(2)}, u32[]{:S(2)}) collective-permute-start(f32[4,32,256]{2,1,0:T(8,128)S(1)} %shard_map.96.refs_13_), channel_id=1, source_target_pairs={{13,22}} | collective-permute-start | bytes 393224 | tf_op jit(solution)/shard_map/ppermute | solution.py:254
  7.0 2.1 %collective-permute-start.11 = (f32[2,128,256]{2,1,0:T(8,128)}, f32[2,128,256]{2,1,0:T(8,128)S(1)}, u32[]{:S(2)}, u32[]{:S(2)}) collective-permute-start(f32[2,128,256]{2,1,0:T(8,128)} %param.7), channel_id=1, source_target_pairs={{7,31}} | collective-permute-start | bytes 786440 | tf_op jit(solution)/shard_map/ppermute | solution.py:254
  7.7 1.4 %collective-permute-start.10 = (f32[2,128,256]{2,1,0:T(8,128)}, f32[2,128,256]{2,1,0:T(8,128)S(1)}, u32[]{:S(2)}, u32[]{:S(2)}) collective-permute-start(f32[2,128,256]{2,1,0:T(8,128)} %param.7), channel_id=1, source_target_pairs={{3,31}} | collective-permute-start | bytes 786440 | tf_op jit(solution)/shard_map/ppermute | solution.py:254
  8.4 0.7 collective-permute-start.9
  9.2 2.0 %collective-permute-start.14 = (f32[2,32,256]{2,1,0:T(8,128)S(1)}, f32[2,32,256]{2,1,0:T(8,128)S(1)}, u32[]{:S(2)}, u32[]{:S(2)}) collective-permute-start(f32[2,32,256]{2,1,0:T(8,128)S(1)} %shard_map.98.refs_0_), channel_id=1, source_target_pairs={{4,7},{13,12},{22,21},{31,30}} | collective-permute-start | bytes 196616 | tf_op jit(solution)/shard_map/ppermute | solution.py:254
  9.8 1.4 %collective-permute-start.13 = (f32[2,32,256]{2,1,0:T(8,128)S(1)}, f32[2,32,256]{2,1,0:T(8,128)S(1)}, u32[]{:S(2)}, u32[]{:S(2)}) collective-permute-start(f32[2,32,256]{2,1,0:T(8,128)S(1)} %shard_map.98.refs_0_), channel_id=1, source_target_pairs={{4,6},{13,15},{22,20},{31,29}} | collective-permute-start | bytes 196616 | tf_op jit(solution)/shard_map/ppermute | solution.py:254
  10.5 0.7 collective-permute-start.12
  11.3 23.8 %collective-permute-start.15 = (f32[2,32,128]{2,1,0:T(8,128)S(1)}, f32[2,32,128]{2,1,0:T(8,128)S(1)}, u32[]{:S(2)}, u32[]{:S(2)}) collective-permute-start(f32[2,32,128]{2,1,0:T(8,128)S(1)} %get-tuple-element.36), channel_id=1, source_target_pairs={{0,4},{4,0},{8,12},{12,8},{16,20},{20,16},{24,28},{28,24},{1,5},{5... | collective-permute-start | bytes 98312 | tf_op jit(solution)/shard_map/ppermute | solution.py:323
  36.8 5.1 %collective-permute-start.19 = (f32[4,32,1024]{2,1,0:T(8,128)S(1)}, f32[4,32,1024]{2,1,0:T(8,128)S(1)}, u32[]{:S(2)}, u32[]{:S(2)}) collective-permute-start(f32[4,32,1024]{2,1,0:T(8,128)S(1)} %get-tuple-element.47), channel_id=1, source_target_pairs={{0,4},{4,0},{8,12},{12,8},{16,20},{20,16},{24,28},{28,24},{1,5},{5... | collective-permute-start | bytes 1572872 | tf_op jit(solution)/shard_map/ppermute | solution.py:370
  40.8 4.2 %collective-permute-start.22 = (f32[4,32,1024]{2,1,0:T(8,128)S(1)}, f32[4,32,1024]{2,1,0:T(8,128)S(1)}, u32[]{:S(2)}, u32[]{:S(2)}) collective-permute-start(f32[4,32,1024]{2,1,0:T(8,128)S(1)} %get-tuple-element.54), channel_id=1, source_target_pairs={{0,4},{4,0},{8,12},{12,8},{16,20},{20,16},{24,28},{28,24},{1,5},{5... | collective-permute-start | bytes 1572872 | tf_op jit(solution)/shard_map/ppermute | solution.py:370
  41.3 10.1 %collective-permute-start.16 = (f32[4,32,1152]{2,1,0:T(8,128)S(1)}, f32[4,32,1152]{2,1,0:T(8,128)S(1)}, u32[]{:S(2)}, u32[]{:S(2)}) collective-permute-start(f32[4,32,1152]{2,1,0:T(8,128)S(1)} %get-tuple-element.43), channel_id=1, source_target_pairs={{0,4},{4,0},{8,12},{12,8},{16,20},{20,16},{24,28},{28,24},{1,5},{5... | collective-permute-start | bytes 1769480 | tf_op jit(solution)/shard_map/ppermute | solution.py:370
  41.4 9.0 %collective-permute-start.25 = (f32[4,32,1024]{2,1,0:T(8,128)S(1)}, f32[4,32,1024]{2,1,0:T(8,128)S(1)}, u32[]{:S(2)}, u32[]{:S(2)}) collective-permute-start(f32[4,32,1024]{2,1,0:T(8,128)S(1)} %get-tuple-element.56), channel_id=1, source_target_pairs={{0,4},{4,0},{8,12},{12,8},{16,20},{20,16},{24,28},{28,24},{1,5},{5... | collective-permute-start | bytes 1572872 | tf_op jit(solution)/shard_map/ppermute | solution.py:370
  41.9 11.1 %collective-permute-start.20 = (f32[2,32,1024]{2,1,0:T(8,128)S(1)}, f32[2,32,1024]{2,1,0:T(8,128)S(1)}, u32[]{:S(2)}, u32[]{:S(2)}) collective-permute-start(f32[2,32,1024]{2,1,0:T(8,128)S(1)} %slice.82), channel_id=1, source_target_pairs={{0,16},{4,20},{8,24},{12,28},{16,0},{20,4},{24,8},{28,12},{1,17},{... | collective-permute-start | bytes 786440 | tf_op jit(solution)/shard_map/ppermute | solution.py:234
  45.0 12.5 %collective-permute-start.23 = (f32[2,32,1024]{2,1,0:T(8,128)S(1)}, f32[2,32,1024]{2,1,0:T(8,128)S(1)}, u32[]{:S(2)}, u32[]{:S(2)}) collective-permute-start(f32[2,32,1024]{2,1,0:T(8,128)S(1)} %slice_bitcast_fusion.2), channel_id=1, source_target_pairs={{0,8},{4,12},{8,0},{12,4},{16,24},{20,28},{24,16},{28,20},{1,9},{5... | collective-permute-start | bytes 786440 | tf_op jit(solution)/shard_map/ppermute | solution.py:234
  50.4 19.3 %copy-start = (f32[2,32,2048]{2,1,0:T(8,128)S(1)}, f32[2,32,2048]{2,1,0:T(8,128)}, u32[]{:S(2)}) copy-start(f32[2,32,2048]{2,1,0:T(8,128)} %param.11) | copy-start | bytes 1572868
  50.5 9.1 %collective-permute-start.26 = (f32[2,32,1024]{2,1,0:T(8,128)S(1)}, f32[2,32,1024]{2,1,0:T(8,128)S(1)}, u32[]{:S(2)}, u32[]{:S(2)}) collective-permute-start(f32[2,32,1024]{2,1,0:T(8,128)S(1)} %slice.90), channel_id=1, source_target_pairs={{0,16},{4,20},{8,24},{12,28},{16,0},{20,4},{24,8},{28,12},{1,17},{... | collective-permute-start | bytes 786440 | tf_op jit(solution)/shard_map/ppermute | solution.py:234
  51.5 12.3 %collective-permute-start.17 = (f32[2,32,1152]{2,1,0:T(8,128)S(1)}, f32[2,32,1152]{2,1,0:T(8,128)S(1)}, u32[]{:S(2)}, u32[]{:S(2)}) collective-permute-start(f32[2,32,1152]{2,1,0:T(8,128)S(1)} %slice_bitcast_fusion), channel_id=1, source_target_pairs={{0,8},{4,12},{8,0},{12,4},{16,24},{20,28},{24,16},{28,20},{1,9},{5... | collective-permute-start | bytes 884744 | tf_op jit(solution)/shard_map/ppermute | solution.py:234
  53.0 13.6 %collective-permute-start.21 = (f32[32,1024]{1,0:T(8,128)S(1)}, f32[32,1024]{1,0:T(8,128)S(1)}, u32[]{:S(2)}, u32[]{:S(2)}) collective-permute-start(f32[32,1024]{1,0:T(8,128)S(1)} %slice_bitcast_fusion.10), channel_id=1, source_target_pairs={{0,8},{4,12},{8,0},{12,4},{16,24},{20,28},{24,16},{28,20},{1,9},{5... | collective-permute-start | bytes 393224 | tf_op jit(solution)/shard_map/ppermute | solution.py:234
  57.5 9.1 %collective-permute-start.24 = (f32[32,1024]{1,0:T(8,128)S(1)}, f32[32,1024]{1,0:T(8,128)S(1)}, u32[]{:S(2)}, u32[]{:S(2)}) collective-permute-start(f32[32,1024]{1,0:T(8,128)S(1)} %slice_bitcast_fusion.8), channel_id=1, source_target_pairs={{0,16},{4,20},{8,24},{12,28},{16,0},{20,4},{24,8},{28,12},{1,17},{... | collective-permute-start | bytes 393224 | tf_op jit(solution)/shard_map/ppermute | solution.py:234
  59.6 8.9 %collective-permute-start.27 = (f32[32,1024]{1,0:T(8,128)S(1)}, f32[32,1024]{1,0:T(8,128)S(1)}, u32[]{:S(2)}, u32[]{:S(2)}) collective-permute-start(f32[32,1024]{1,0:T(8,128)S(1)} %slice_bitcast_fusion.6), channel_id=1, source_target_pairs={{0,8},{4,12},{8,0},{12,4},{16,24},{20,28},{24,16},{28,20},{1,9},{5... | collective-permute-start | bytes 393224 | tf_op jit(solution)/shard_map/ppermute | solution.py:234
  63.9 5.2 %collective-permute-start.18 = (f32[32,1152]{1,0:T(8,128)S(1)}, f32[32,1152]{1,0:T(8,128)S(1)}, u32[]{:S(2)}, u32[]{:S(2)}) collective-permute-start(f32[32,1152]{1,0:T(8,128)S(1)} %slice_bitcast_fusion.4), channel_id=1, source_target_pairs={{0,16},{4,20},{8,24},{12,28},{16,0},{20,4},{24,8},{28,12},{1,17},{... | collective-permute-start | bytes 442376 | tf_op jit(solution)/shard_map/ppermute | solution.py:234

commit v4 on v3

--- a/solution.py
+++ b/solution.py
@@ -78,62 +78,72 @@
     return lax.optimization_barrier((value, other))[0]
 
 
-def step_kernel(step, groups, members, width, *refs):
+def leads(group, members):
+    return (lax.axis_index("col") == group) & (lax.axis_index("row") == members * group + members - 1)
+
+
+def step_kernel(step, members, width, near, held, *refs):
     refs = list(refs)
     out = refs.pop()
     rhs = [refs.pop(0) for _ in range(members)]
     inverse = [refs.pop(0) for _ in range(members)]
     inside = [refs.pop(0) for _ in range(members - 1)]
-    earlier = refs.pop(0) if step else None
-    pieces = [refs.pop(0) for _ in range(step * members)]
+    terms = [refs.pop(0) for _ in range(held)]
+    earlier = [(refs.pop(0), [refs.pop(0) for _ in range(members)]) for _ in range(near)]
     results = refs
     observers = rhs[0].shape[1]
-    final = step + 1 == groups
-    row, col = lax.axis_index("row"), lax.axis_index("col")
-
-    @pl.when((col == step) & (row == members * step + members - 1))
+
+    @pl.when(leads(step, members))
     def _():
-        held = None
-        for group in range(step):
+        total = None
+        for x, pieces in earlier:
             for t in range(members):
-                x = earlier[2 * group : 2 * group + 2, :, t * width : (t + 1) * width]
-                term = product(x, pieces[(step - group - 1) * members + t][...])
-                held = term if held is None else held + term
+                term = product(x[:, :, t * width : (t + 1) * width], pieces[t][...])
+                total = term if total is None else total + term
+        for ref in terms:
+            term = ref[...].reshape(2 * observers, members * width)
+            total = term if total is None else total + term
         solved = []
         for b in range(members):
             residual = jnp.concatenate([rhs[b][0], rhs[b][1]], axis=0)
-            if held is not None:
-                residual = residual - held[:, b * width : (b + 1) * width]
+            if total is not None:
+                residual = residual - total[:, b * width : (b + 1) * width]
             for a in range(b):
                 residual = residual - product(solved[a], inside[a][:, :, b * width : (b + 1) * width])
             value = product(residual.reshape(2, observers, width), inverse[b][...])
             solved.append(value.reshape(2, observers, width))
-        base = 0
-        if not final:
-            if step:
-                out[0 : 2 * step] = earlier[...]
-            base = 2 * step
-        for b in range(members):
-            out[base : base + 2, :, b * width : (b + 1) * width] = solved[b]
-
-    if final:
-        for k in range(step):
-            @pl.when(col == k)
-            def _(k=k):
-                out[...] = results[k][2 * k : 2 * k + 2]
-
-
-def merge_kernel(members, *refs):
+            out[:, :, b * width : (b + 1) * width] = solved[b]
+
+    for k, result in enumerate(results):
+        @pl.when(leads(k, members))
+        def _(result=result):
+            out[...] = result[...]
+
+
+def held_kernel(group, targets, members, width, *refs):
+    out = refs[-1]
+    pieces = refs[-1 - members : -1]
+    row, col = lax.axis_index("row"), lax.axis_index("col")
+    for k, x in zip(targets, refs):
+        @pl.when((row == members * group + members - 1) & (col == k))
+        def _(x=x):
+            total = None
+            for t in range(members):
+                term = product(x[:, :, t * width : (t + 1) * width], pieces[t][...])
+                total = term if total is None else total + term
+            out[...] = total.reshape(out.shape)
+
+
+def merge_kernel(members, sources, *refs):
     outs = refs[-members:]
-    sources = refs[:-members]
-    cols = len(sources)
     width = outs[0].shape[2]
     group, col = lax.div(lax.axis_index("row"), members), lax.axis_index("col")
-    for s, source in enumerate(sources):
-        @pl.when(lax.rem(group + s, cols) == col)
-        def _(source=source):
-            for t in range(members):
-                outs[t][...] = source[:, :, t * width : (t + 1) * width]
+    for source, places in zip(refs, sources):
+        for i, k in places:
+            @pl.when((group == i) & (col == k))
+            def _(source=source):
+                for t in range(members):
+                    outs[t][...] = source[:, :, t * width : (t + 1) * width]
 
 
 def when_kernel(last, members, skip, kernel, *refs):
@@ -144,20 +154,27 @@
         kernel(*refs[skip[0] : skip[1]], *refs[skip[2] :])
 
 
-def prepare_kernel(chunk, chunks, trail, high, low, room, sems):
+def prepare_kernel(chunk, chunks, members, busy, late, skip, *refs):
+    trail, high, low, room, sems = refs[skip:]
     devices, columns = room.shape[0], room.shape[3]
-    copies = []
-    for i in range(devices):
-        start = (i * chunks + chunk) * columns
-        copies.append(pltpu.make_async_copy(trail.at[:, :, start : start + columns], room.at[i], sems.at[i]))
-        copies[-1].start()
-    for i in range(devices):
-        copies[i].wait()
-        for part in range(2):
-            depth = room.shape[2]
-            a, b = split(room[i, part])
-            high[i, part * depth : (part + 1) * depth] = a
-            low[i, part * depth : (part + 1) * depth] = b
+    waits = jnp.bool_(False)
+    for k in busy:
+        waits = waits | leads(k, members)
+
+    @pl.when(waits if late else jnp.logical_not(waits))
+    def _():
+        copies = []
+        for i in range(devices):
+            start = (i * chunks + chunk) * columns
+            copies.append(pltpu.make_async_copy(trail.at[:, :, start : start + columns], room.at[i], sems.at[i]))
+            copies[-1].start()
+        for i in range(devices):
+            copies[i].wait()
+            for part in range(2):
+                depth = room.shape[2]
+                a, b = split(room[i, part])
+                high[i, part * depth : (part + 1) * depth] = a
+                low[i, part * depth : (part + 1) * depth] = b
 
 
 def trail_kernel(chunk, chunks, cols, ready, select, odds, members, currents, owner, *refs):
@@ -253,14 +270,23 @@
     def send(value, pairs):
         return lax.ppermute(value, ("row", "col"), pairs)
 
-    pieces = []
-
-    def above(d, source):
+    def near(k):
+        return [g for g in ([k - 1, k - 2] if k % 2 and k > 1 else [k - 1]) if g >= 0]
+
+    def far(g):
+        return [k for k in range(g + 2, cols) if g not in near(k)]
+
+    pieces = {}
+
+    def bring(number):
         for t in range(members):
-            pairs = [(flat(members * (k - d) + t, k), leader(k)) for k in range(d, cols)]
-            pieces.append(send(source, pairs))
-
-    above(1, upper_block)
+            moves = [(k, near(k)[number - 1]) for k in range(1, cols) if len(near(k)) >= number]
+            if moves:
+                arrived = send(upper_block, [(flat(members * g + t, k), leader(k)) for k, g in moves])
+                for k, g in moves:
+                    pieces[k, g, t] = arrived
+
+    bring(1)
     rhs, inverse, inside = [], [], []
     for t in range(members - 1):
         turn = members - 1 - t
@@ -268,9 +294,10 @@
         rhs.append(lax.ppermute(panel_rhs, "row", pairs))
         inverse.append(lax.ppermute(block_inverse, "row", pairs))
         inside.append(lax.ppermute(upper_block, "row", pairs))
+    bring(2)
     owner_row = owner.reshape(1, width)
-    loaded = [panel_rhs, block_inverse, currents, owner_row]
-    panel_near, inverse_near, currents_near, owner_near = local_call(
+    loaded = [panel_rhs, block_inverse, currents, owner_row, upper_block]
+    panel_near, inverse_near, currents_near, owner_near, upper_near = local_call(
         functools.partial(load_kernel, len(loaded)),
         [(a.shape, a.dtype) for a in loaded],
         [],
@@ -280,38 +307,72 @@
     )
     rhs.append(panel_near)
     inverse.append(inverse_near)
+    upper_rows = [*inside, upper_near]
 
     columns = upper_trail.shape[2] // rows // CHUNKS
     room = [pltpu.VMEM((rows, 2, width, columns), jnp.float32), pltpu.SemaphoreType.DMA((rows,))]
-    earlier, messages = [], []
+    part = (2, observers, quarter)
+    results, passed, held, early = [], {}, {}, {}
+    arrived, sources = [], []
+
+    def spread(value, places):
+        arrived.append(send(value, [(leader(g), flat(members * g + members - 1, k)) for g, k in places]))
+        sources.append(places)
+
+    busy = []
+    ready = []
+
+    def prepare(place, source):
+        nonlocal ready
+        ready = local_call(
+            functools.partial(prepare_kernel, 0, CHUNKS, members, busy, place == 1, len(ready)),
+            [((rows, 2 * width, columns), jnp.bfloat16)] * 2,
+            ready,
+            [source],
+            room,
+            aliases={i: i for i in range(len(ready))},
+        )
+
     for step in range(cols):
         final = step + 1 == cols
-        shape = (2 if final else 2 * step + 2, observers, quarter)
-        message = local_call(
-            functools.partial(step_kernel, step, cols, members, width),
-            [(shape, jnp.float32)],
-            [*rhs, *inverse, *inside, *earlier, *pieces[: step * members], *(messages if final else [])],
+        terms = [held[g] for g in range(step) if step in far(g)]
+        factors = []
+        for g in near(step):
+            factors += [passed[g, step], *(pieces[step, g, t] for t in range(members))]
+        result = local_call(
+            functools.partial(step_kernel, step, members, width, len(near(step)), len(terms)),
+            [(part, jnp.float32)],
+            [*rhs, *inverse, *inside, *terms, *factors, *(results if step == cols - 2 else [])],
         )[0]
-        messages.append(message)
+        results.append(result)
         if not final:
-            earlier = [send(message, [(leader(step), leader(step + 1))])]
-        if step + 2 < cols:
-            above(step + 2, after(upper_block, message))
+            passed[step, step + 1] = send(result, [(leader(step), leader(step + 1))])
+        if step + 2 < cols and step in near(step + 2):
+            passed[step, step + 2] = send(result, [(leader(step), leader(step + 2))])
+        for k in far(step):
+            early[step, k] = send(result, [(leader(step), flat(members * step + members - 1, k))])
+        if far(step):
+            term = local_call(
+                functools.partial(held_kernel, step, far(step), members, width),
+                [(part, jnp.float32)],
+                [*(early[step, k] for k in far(step)), *upper_rows],
+            )[0]
+            held[step] = send(term, [(flat(members * step + members - 1, k), leader(k)) for k in far(step)])
         if step == min(1, cols - 2):
-            ready = local_call(
-                functools.partial(prepare_kernel, 0, CHUNKS),
-                [((rows, 2 * width, columns), jnp.bfloat16)] * 2,
-                [],
-                [after(upper_trail, message)],
-                room,
-            )
-
-    arrived = [messages[-1]]
+            prepare(0, after(upper_trail, result))
+        if step == cols - 2:
+            arrived += [result, *early.values()]
+            sources += [[(k, k) for k in range(cols - 1)], *([place] for place in early)]
+            for s in range(1, cols):
+                places = [(k, (k + s) % cols) for k in range(cols - 1)]
+                spread(result, [place for place in places if place not in early])
+
+    arrived += [results[-1]]
+    sources += [[(cols - 1, cols - 1)]]
     for s in range(1, cols):
-        pairs = [(leader(k), flat(members * k + members - 1, (k + s) % cols)) for k in range(cols)]
-        arrived.append(send(messages[-1], pairs))
+        spread(results[-1], [(cols - 1, (cols - 1 + s) % cols)])
     parts = local_call(
-        functools.partial(merge_kernel, members),
+        functools.partial(merge_kernel, members, sources),
         [((2, observers, width), jnp.float32)] * members,
         arrived,
         limit=2 << 20,

time: 70.9 us -> 70.2 us (level)
  starting transfers between devices: 52.3 us -> 50.2 us
  waiting for transfers between devices: 4.75 us -> 5.76 us
    ppermute x1, starting transfers between devices: 20.1 us -> 8.68 us  [on_device(): candidates.append(lax.ppermute(parts[t], 'row', pairs))]
    ppermute x8, starting transfers between devices: 21.9 us -> 27.9 us  [halve(): lax.ppermute(high, 'row', [(i, i ^ 1 << bit) for i in range(rows)])]
    ppermute x12 -> x17, starting transfers between devices: 8.04 us -> 11.3 us  [send(): return lax.ppermute(value, ('row', 'col'), pairs)]
    ppermute x1, waiting for transfers between devices: 0.1 us -> 1.09 us  [on_device(): rhs.append(lax.ppermute(panel_rhs, 'row', pairs))]
    pallas_call x11 -> x12, Pallas kernels: 10.4 us -> 10.6 us  [local_call(): pl.pallas_call(kernel, in_specs=[VMEM] * len(near) + [ANY] * len(far), ou...]
  transfers between devices with their start and end apart: 28 -> 33, of which waited for: 6 -> 6; matrix products, arithmetic and copies ran while one was open for 1% -> 1% of each run, Pallas kernels for 12% -> 13%
where the time goes in v4:
time: 70.2 us; the launch traced here: 69.8 us
  starting transfers between devices  50.2 us (72%)
  Pallas kernels  10.6 us (15%)
  waiting for transfers between devices  5.76 us (8%)
  other arithmetic  1.34 us (2%)
  between operations  1.15 us (2%)
  local copies, waits for them, and re-layouts  0.76 us (1%)
    ppermute x8, starting transfers between devices, halve(): lax.ppermute(high, 'row', [(i, i ^ 1 << bit) for i in range(rows)])  27.9 us
    ppermute x17, starting transfers between devices, send(): return lax.ppermute(value, ('row', 'col'), pairs)  11.3 us
    pallas_call x12, Pallas kernels, local_call(): pl.pallas_call(kernel, in_specs=[VMEM] * len(near) + [ANY] * len(far), ou...  10.6 us
    ppermute x1, starting transfers between devices, on_device(): candidates.append(lax.ppermute(parts[t], 'row', pairs))  8.68 us
    ppermute x8, waiting for transfers between devices, halve(): lax.ppermute(high, 'row', [(i, i ^ 1 << bit) for i in range(rows)])  4.6 us
  transfers between devices with their start and end apart: 33, of which 6 were waited for; matrix products, arithmetic and copies ran while one was open for 1% of the time, Pallas kernels for 13%

profile of v4, /device:TPU:0, one launch (start us, length us, event | category | flops | bytes accessed | tf_op | source)
XLA Modules:
  0.0 69.8 jit_solution(18255514978376360846)
XLA Ops:
  0.6 0.6 collective-permute-start.2
  1.2 0.7 collective-permute-start.8
  1.9 0.7 collective-permute-start.7
  2.5 0.1 collective-permute-start.1
  2.6 0.5 collective-permute-start
  3.1 1.1 %collective-permute-done.refs_0_ = f32[2,32,128]{2,1,0:T(8,128)S(1)} collective-permute-done((f32[2,32,128]{2,1,0:T(8,128)}, f32[2,32,128]{2,1,0:T(8,128)S(1)}, u32[]{:S(2)}, u32[]{:S(2)}) %collective-permute-start) | collective-permute-done | bytes 32800 | tf_op jit(solution)/shard_map/ppermute | solution.py:294
  4.2 0.7 collective-permute-start.16
  4.9 0.7 collective-permute-start.15
  5.6 1.1 %shard_map.94 = (f32[2,32,128]{2,1,0:T(8,128)S(1)}, f32[2,128,128]{2,1,0:T(8,128)S(1)}, f32[2,128]{1,0:T(2,128)S(1)}, s32[1,128]{1,0:T(1,128)S(1)}, f32[2,128,256]{2,1,0:T(8,128)S(1)}) custom-call(f32[2,32,128]{2,1,0:T(8,128)} %refs_0_.1, f32[2,128,128]{2,1,0:T(8,128)} %refs_1_.1, f32[2,128]{1,0:T(2,128)} %refs_2_.1, s32[1,128]{1,0:T(1,128)} %bitcast.65, ...), custom_call_target="tpu_custom_call" | custom-call | tf_op jit(solution)/shard_map/pallas_call | solution.py:56
  6.7 0.7 collective-permute-start.6
  7.4 0.7 collective-permute-start.4
  8.1 0.7 collective-permute-start.3
  8.8 0.7 collective-permute-start.9
  9.5 0.7 collective-permute-start.5
  10.2 0.7 collective-permute-start.14
  10.9 0.7 collective-permute-start.13
  11.6 0.7 collective-permute-start.12
  12.3 0.7 collective-permute-start.11
  13.0 0.7 collective-permute-start.10
  13.7 0.7 collective-permute-start.19
  14.4 0.7 collective-permute-start.18
  15.1 0.7 collective-permute-start.17
  15.8 0.1 shard_map.100
  15.9 8.7 %collective-permute-start.20 = (f32[2,32,128]{2,1,0:T(8,128)S(1)}, f32[2,32,128]{2,1,0:T(8,128)S(1)}, u32[]{:S(2)}, u32[]{:S(2)}) collective-permute-start(f32[2,32,128]{2,1,0:T(8,128)S(1)} %get-tuple-element.34), channel_id=1, source_target_pairs={{0,4},{4,0},{8,12},{12,8},{16,20},{20,16},{24,28},{28,24},{1,5},{5... | collective-permute-start | bytes 98312 | tf_op jit(solution)/shard_map/ppermute | solution.py:384
  24.6 3.7 %shard_map.101 = (bf16[8,256,1024]{2,1,0:T(8,128)(2,1)S(1)}, bf16[8,256,1024]{2,1,0:T(8,128)(2,1)S(1)}) custom-call(f32[2,128,16384]{2,1,0:T(8,128)} %refs_7_.1), custom_call_target="tpu_custom_call" | custom-call | tf_op jit(solution)/shard_map/pallas_call | solution.py:56
  28.3 0.9 %shard_map.102 = (f32[2,32,128]{2,1,0:T(8,128)S(1)}, f32[4,32,1152]{2,1,0:T(8,128)S(1)}, f32[4,32,1024]{2,1,0:T(8,128)S(1)}, f32[2,32,128]{2,1,0:T(8,128)}) custom-call(f32[2,128]{1,0:T(2,128)S(1)} %get-tuple-element.29.currents.refs_0_, s32[1,128]{1,0:T(1,128)S(1)} %get-tuple-element.30.owner.refs_1_, f32[2,32,128]{2,1,0:T(8,128)S(1)} %collective-permute-done.20.refs_0_, ...), custom_call_target="tpu_custom_call" | custom-call | tf_op jit(solution)/shard_map/pallas_call | solution.py:56
  29.1 0.8 %shard_map.103 = (f32[4,32,1152]{2,1,0:T(8,128)S(1)}, f32[4,32,1024]{2,1,0:T(8,128)S(1)}) custom-call(f32[2,128]{1,0:T(2,128)S(1)} %get-tuple-element.29.currents.refs_0_, s32[1,128]{1,0:T(1,128)S(1)} %get-tuple-element.30.owner.refs_1_, f32[2,32,128]{2,1,0:T(8,128)S(1)} %get-tuple-element.46.refs_0_.refs_2_, ...), custom_call_target="tpu_custom_call" | custom-call | tf_op jit(solution)/shard_map/pallas_call | solution.py:56
  30.0 0.1 collective-permute-start.24
  30.1 3.8 %shard_map.104 = (f32[4,32,1024]{2,1,0:T(8,128)S(1)}, f32[4,32,1024]{2,1,0:T(8,128)S(1)}, f32[4,32,1024]{2,1,0:T(8,128)S(1)}, f32[4,32,1024]{2,1,0:T(8,128)S(1)}) custom-call(f32[2,128]{1,0:T(2,128)S(1)} %get-tuple-element.29.currents.refs_0_, s32[1,128]{1,0:T(1,128)S(1)} %get-tuple-element.30.owner.refs_1_, ...), custom_call_target="tpu_custom_call" | custom-call | tf_op jit(solution)/shard_map/pallas_call | solution.py:56
  33.9 0.1 shard_map.105
  34.0 0.5 collective-permute-start.27
  34.5 0.1 collective-permute-start.21
  34.6 0.4 collective-permute-start.30
  35.1 8.0 %collective-permute-start.25 = (f32[2,32,1024]{2,1,0:T(8,128)S(1)}, f32[2,32,1024]{2,1,0:T(8,128)S(1)}, u32[]{:S(2)}, u32[]{:S(2)}) collective-permute-start(f32[2,32,1024]{2,1,0:T(8,128)S(1)} %slice.82), channel_id=1, source_target_pairs={{0,16},{4,20},{8,24},{12,28},{16,0},{20,4},{24,8},{28,12},{1,17},{... | collective-permute-start | bytes 786440 | tf_op jit(solution)/shard_map/ppermute | solution.py:251
  43.3 6.3 %collective-permute-start.28 = (f32[2,32,1024]{2,1,0:T(8,128)S(1)}, f32[2,32,1024]{2,1,0:T(8,128)S(1)}, u32[]{:S(2)}, u32[]{:S(2)}) collective-permute-start(f32[2,32,1024]{2,1,0:T(8,128)S(1)} %slice_bitcast_fusion.2), channel_id=1, source_target_pairs={{0,8},{4,12},{8,0},{12,4},{16,24},{20,28},{24,16},{28,20},{1,9},{5... | collective-permute-start | bytes 786440 | tf_op jit(solution)/shard_map/ppermute | solution.py:251
  49.6 0.1 add.45
  49.7 0.9 %collective-permute-start.31 = (f32[2,32,1024]{2,1,0:T(8,128)S(1)}, f32[2,32,1024]{2,1,0:T(8,128)S(1)}, u32[]{:S(2)}, u32[]{:S(2)}) collective-permute-start(f32[2,32,1024]{2,1,0:T(8,128)S(1)} %slice.90), channel_id=1, source_target_pairs={{0,16},{4,20},{8,24},{12,28},{16,0},{20,4},{24,8},{28,12},{1,17},{... | collective-permute-start | bytes 786440 | tf_op jit(solution)/shard_map/ppermute | solution.py:251
  50.7 1.5 %collective-permute-start.22 = (f32[2,32,1152]{2,1,0:T(8,128)S(1)}, f32[2,32,1152]{2,1,0:T(8,128)S(1)}, u32[]{:S(2)}, u32[]{:S(2)}) collective-permute-start(f32[2,32,1152]{2,1,0:T(8,128)S(1)} %slice_bitcast_fusion), channel_id=1, source_target_pairs={{0,8},{4,12},{8,0},{12,4},{16,24},{20,28},{24,16},{28,20},{1,9},{5... | collective-permute-start | bytes 884744 | tf_op jit(solution)/shard_map/ppermute | solution.py:251
  52.2 4.4 %collective-permute-start.26 = (f32[32,1024]{1,0:T(8,128)S(1)}, f32[32,1024]{1,0:T(8,128)S(1)}, u32[]{:S(2)}, u32[]{:S(2)}) collective-permute-start(f32[32,1024]{1,0:T(8,128)S(1)} %slice_bitcast_fusion.10), channel_id=1, source_target_pairs={{0,8},{4,12},{8,0},{12,4},{16,24},{20,28},{24,16},{28,20},{1,9},{5... | collective-permute-start | bytes 393224 | tf_op jit(solution)/shard_map/ppermute | solution.py:251
  56.8 2.0 %collective-permute-start.29 = (f32[32,1024]{1,0:T(8,128)S(1)}, f32[32,1024]{1,0:T(8,128)S(1)}, u32[]{:S(2)}, u32[]{:S(2)}) collective-permute-start(f32[32,1024]{1,0:T(8,128)S(1)} %slice_bitcast_fusion.8), channel_id=1, source_target_pairs={{0,16},{4,20},{8,24},{12,28},{16,0},{20,4},{24,8},{28,12},{1,17},{... | collective-permute-start | bytes 393224 | tf_op jit(solution)/shard_map/ppermute | solution.py:251
  58.9 3.4 %collective-permute-start.32 = (f32[32,1024]{1,0:T(8,128)S(1)}, f32[32,1024]{1,0:T(8,128)S(1)}, u32[]{:S(2)}, u32[]{:S(2)}) collective-permute-start(f32[32,1024]{1,0:T(8,128)S(1)} %slice_bitcast_fusion.6), channel_id=1, source_target_pairs={{0,8},{4,12},{8,0},{12,4},{16,24},{20,28},{24,16},{28,20},{1,9},{5... | collective-permute-start | bytes 393224 | tf_op jit(solution)/shard_map/ppermute | solution.py:251
  62.3 0.8 %collective-permute-done.22 = f32[2,32,1152]{2,1,0:T(8,128)S(1)} collective-permute-done((f32[2,32,1152]{2,1,0:T(8,128)S(1)}, f32[2,32,1152]{2,1,0:T(8,128)S(1)}, u32[]{:S(2)}, u32[]{:S(2)}) %collective-permute-start.22) | collective-permute-done | bytes 294944 | tf_op jit(solution)/shard_map/ppermute | solution.py:251
  63.1 1.3 %collective-permute-start.23 = (f32[32,1152]{1,0:T(8,128)S(1)}, f32[32,1152]{1,0:T(8,128)S(1)}, u32[]{:S(2)}, u32[]{:S(2)}) collective-permute-start(f32[32,1152]{1,0:T(8,128)S(1)} %slice_bitcast_fusion.4), channel_id=1, source_target_pairs={{0,16},{4,20},{8,24},{12,28},{16,0},{20,4},{24,8},{28,12},{1,17},{... | collective-permute-start | bytes 442376 | tf_op jit(solution)/shard_map/ppermute | solution.py:251
  64.4 1.4 %collective-permute-done.26 = f32[32,1024]{1,0:T(8,128)S(1)} collective-permute-done((f32[32,1024]{1,0:T(8,128)S(1)}, f32[32,1024]{1,0:T(8,128)S(1)}, u32[]{:S(2)}, u32[]{:S(2)}) %collective-permute-start.26) | collective-permute-done | bytes 131104 | tf_op jit(solution)/shard_map/ppermute | solution.py:251
  65.9 1.9 %collective-permute-done.32 = f32[32,1024]{1,0:T(8,128)S(1)} collective-permute-done((f32[32,1024]{1,0:T(8,128)S(1)}, f32[32,1024]{1,0:T(8,128)S(1)}, u32[]{:S(2)}, u32[]{:S(2)}) %collective-permute-start.32) | collective-permute-done | bytes 131104 | tf_op jit(solution)/shard_map/ppermute | solution.py:251
  67.8 0.5 collective-permute-done.23
  68.3 0.6 slice_reduce_fusion
  69.0 0.9 %maximum_subtract_fusion = f32[2,32,2048]{2,1,0:T(8,128)} fusion(f32[2,32,2048]{2,1,0:T(8,128)S(1)} %copy-done, f32[1,32,1024]{2,1,0:T(8,128)S(1)} %fusion.4, f32[1,32,1024]{2,1,0:T(8,128)S(1)} %fusion.6, f32[1,32,1024]{2,1,0:T(8,128)S(1)} %fusion.8, f32[1,32,1024]{2,1,0:T(8,128)S(1)} %slice_bitcast_fusion.12), kind=kLoop, calls=%fused_computation | loop fusion | flops 524288 | bytes 1572864 | tf_op jit(solution)/shard_map/sub | solution.py:443
  (55 shorter events, 0.8 us)
Async XLA Ops:
  0.6 6.1 %collective-permute-start.2 = (f32[2,128,256]{2,1,0:T(8,128)}, f32[2,128,256]{2,1,0:T(8,128)S(1)}, u32[]{:S(2)}, u32[]{:S(2)}) collective-permute-start(f32[2,128,256]{2,1,0:T(8,128)} %refs_4_.1), channel_id=1, source_target_pairs={{0,4},{4,0},{8,12},{12,8},{16,20},{20,16},{24,28},{28,24},{1,5},{5... | collective-permute-start | bytes 786440 | tf_op jit(solution)/shard_map/ppermute | solution.py:296
  1.2 6.2 %collective-permute-start.8 = (f32[2,128,256]{2,1,0:T(8,128)}, f32[2,128,256]{2,1,0:T(8,128)S(1)}, u32[]{:S(2)}, u32[]{:S(2)}) collective-permute-start(f32[2,128,256]{2,1,0:T(8,128)} %refs_4_.1), channel_id=1, source_target_pairs={{5,13},{14,22},{23,31}} | collective-permute-start | bytes 786440 | tf_op jit(solution)/shard_map/ppermute | solution.py:271
  1.9 6.2 %collective-permute-start.7 = (f32[2,128,256]{2,1,0:T(8,128)}, f32[2,128,256]{2,1,0:T(8,128)S(1)}, u32[]{:S(2)}, u32[]{:S(2)}) collective-permute-start(f32[2,128,256]{2,1,0:T(8,128)} %refs_4_.1), channel_id=1, source_target_pairs={{1,13},{10,22},{19,31}} | collective-permute-start | bytes 786440 | tf_op jit(solution)/shard_map/ppermute | solution.py:271
  2.5 2.3 %collective-permute-start.1 = (f32[2,128,128]{2,1,0:T(8,128)}, f32[2,128,128]{2,1,0:T(8,128)S(1)}, u32[]{:S(2)}, u32[]{:S(2)}) collective-permute-start(f32[2,128,128]{2,1,0:T(8,128)} %refs_1_.1), channel_id=1, source_target_pairs={{0,4},{4,0},{8,12},{12,8},{16,20},{20,16},{24,28},{28,24},{1,5},{5... | collective-permute-start | bytes 393224 | tf_op jit(solution)/shard_map/ppermute | solution.py:295
  2.6 1.6 %collective-permute-start = (f32[2,32,128]{2,1,0:T(8,128)}, f32[2,32,128]{2,1,0:T(8,128)S(1)}, u32[]{:S(2)}, u32[]{:S(2)}) collective-permute-start(f32[2,32,128]{2,1,0:T(8,128)} %refs_0_.1), channel_id=1, source_target_pairs={{0,4},{4,0},{8,12},{12,8},{16,20},{20,16},{24,28},{28,24},{1,5},{5... | collective-permute-start | bytes 98312 | tf_op jit(solution)/shard_map/ppermute | solution.py:294
  4.2 8.1 %collective-permute-start.16 = (f32[2,128,256]{2,1,0:T(8,128)}, f32[2,128,256]{2,1,0:T(8,128)S(1)}, u32[]{:S(2)}, u32[]{:S(2)}) collective-permute-start(f32[2,128,256]{2,1,0:T(8,128)} %refs_4_.1), channel_id=1, source_target_pairs={{15,31}} | collective-permute-start | bytes 786440 | tf_op jit(solution)/shard_map/ppermute | solution.py:271
  4.9 8.1 %collective-permute-start.15 = (f32[2,128,256]{2,1,0:T(8,128)}, f32[2,128,256]{2,1,0:T(8,128)S(1)}, u32[]{:S(2)}, u32[]{:S(2)}) collective-permute-start(f32[2,128,256]{2,1,0:T(8,128)} %refs_4_.1), channel_id=1, source_target_pairs={{11,31}} | collective-permute-start | bytes 786440 | tf_op jit(solution)/shard_map/ppermute | solution.py:271
  6.7 2.0 %collective-permute-start.6 = (f32[2,32,256]{2,1,0:T(8,128)S(1)}, f32[2,32,256]{2,1,0:T(8,128)S(1)}, u32[]{:S(2)}, u32[]{:S(2)}) collective-permute-start(f32[2,32,256]{2,1,0:T(8,128)S(1)} %shard_map.95.refs_9_), channel_id=1, source_target_pairs={{4,13}} | collective-permute-start | bytes 196616 | tf_op jit(solution)/shard_map/ppermute | solution.py:271
  7.4 2.1 %collective-permute-start.4 = (f32[2,32,256]{2,1,0:T(8,128)S(1)}, f32[2,32,256]{2,1,0:T(8,128)S(1)}, u32[]{:S(2)}, u32[]{:S(2)}) collective-permute-start(f32[2,32,256]{2,1,0:T(8,128)S(1)} %shard_map.95.refs_9_), channel_id=1, source_target_pairs={{4,7}} | collective-permute-start | bytes 196616 | tf_op jit(solution)/shard_map/ppermute | solution.py:271
  8.1 1.4 %collective-permute-start.3 = (f32[2,32,256]{2,1,0:T(8,128)S(1)}, f32[2,32,256]{2,1,0:T(8,128)S(1)}, u32[]{:S(2)}, u32[]{:S(2)}) collective-permute-start(f32[2,32,256]{2,1,0:T(8,128)S(1)} %shard_map.95.refs_9_), channel_id=1, source_target_pairs={{4,6}} | collective-permute-start | bytes 196616 | tf_op jit(solution)/shard_map/ppermute | solution.py:271
  8.8 2.1 %collective-permute-start.9 = (f32[2,32,256]{2,1,0:T(8,128)S(1)}, f32[2,32,256]{2,1,0:T(8,128)S(1)}, u32[]{:S(2)}, u32[]{:S(2)}) collective-permute-start(f32[2,32,256]{2,1,0:T(8,128)S(1)} %shard_map.97.refs_10_), channel_id=1, source_target_pairs={{13,22}} | collective-permute-start | bytes 196616 | tf_op jit(solution)/shard_map/ppermute | solution.py:271
  9.5 1.4 %collective-permute-start.5 = (f32[2,32,256]{2,1,0:T(8,128)S(1)}, f32[2,32,256]{2,1,0:T(8,128)S(1)}, u32[]{:S(2)}, u32[]{:S(2)}) collective-permute-start(f32[2,32,256]{2,1,0:T(8,128)S(1)} %shard_map.96), channel_id=1, source_target_pairs={{6,22},{7,31}} | collective-permute-start | bytes 196616 | tf_op jit(solution)/shard_map/ppermute | solution.py:271
  10.2 3.4 %collective-permute-start.14 = (f32[2,32,256]{2,1,0:T(8,128)S(1)}, f32[2,32,256]{2,1,0:T(8,128)S(1)}, u32[]{:S(2)}, u32[]{:S(2)}) collective-permute-start(f32[2,32,256]{2,1,0:T(8,128)S(1)} %shard_map.97.refs_10_), channel_id=1, source_target_pairs={{13,31}} | collective-permute-start | bytes 196616 | tf_op jit(solution)/shard_map/ppermute | solution.py:271
  10.9 2.7 %collective-permute-start.13 = (f32[2,32,256]{2,1,0:T(8,128)S(1)}, f32[2,32,256]{2,1,0:T(8,128)S(1)}, u32[]{:S(2)}, u32[]{:S(2)}) collective-permute-start(f32[2,32,256]{2,1,0:T(8,128)S(1)} %shard_map.98.refs_0_), channel_id=1, source_target_pairs={{22,31}} | collective-permute-start | bytes 196616 | tf_op jit(solution)/shard_map/ppermute | solution.py:271
  11.6 3.4 %collective-permute-start.12 = (f32[2,32,256]{2,1,0:T(8,128)S(1)}, f32[2,32,256]{2,1,0:T(8,128)S(1)}, u32[]{:S(2)}, u32[]{:S(2)}) collective-permute-start(f32[2,32,256]{2,1,0:T(8,128)S(1)} %shard_map.98.refs_0_), channel_id=1, source_target_pairs={{13,12},{22,21}} | collective-permute-start | bytes 196616 | tf_op jit(solution)/shard_map/ppermute | solution.py:271
  12.3 3.4 %collective-permute-start.11 = (f32[2,32,256]{2,1,0:T(8,128)S(1)}, f32[2,32,256]{2,1,0:T(8,128)S(1)}, u32[]{:S(2)}, u32[]{:S(2)}) collective-permute-start(f32[2,32,256]{2,1,0:T(8,128)S(1)} %shard_map.98.refs_0_), channel_id=1, source_target_pairs={{13,15},{22,20}} | collective-permute-start | bytes 196616 | tf_op jit(solution)/shard_map/ppermute | solution.py:271
  13.0 2.8 %collective-permute-start.10 = (f32[2,32,256]{2,1,0:T(8,128)S(1)}, f32[2,32,256]{2,1,0:T(8,128)S(1)}, u32[]{:S(2)}, u32[]{:S(2)}) collective-permute-start(f32[2,32,256]{2,1,0:T(8,128)S(1)} %shard_map.98.refs_0_), channel_id=1, source_target_pairs={{4,5},{13,14},{22,23}} | collective-permute-start | bytes 196616 | tf_op jit(solution)/shard_map/ppermute | solution.py:271
  13.7 2.1 %collective-permute-start.19 = (f32[2,32,256]{2,1,0:T(8,128)S(1)}, f32[2,32,256]{2,1,0:T(8,128)S(1)}, u32[]{:S(2)}, u32[]{:S(2)}) collective-permute-start(f32[2,32,256]{2,1,0:T(8,128)S(1)} %shard_map.99.refs_6_), channel_id=1, source_target_pairs={{31,30}} | collective-permute-start | bytes 196616 | tf_op jit(solution)/shard_map/ppermute | solution.py:271
  14.4 1.4 %collective-permute-start.18 = (f32[2,32,256]{2,1,0:T(8,128)S(1)}, f32[2,32,256]{2,1,0:T(8,128)S(1)}, u32[]{:S(2)}, u32[]{:S(2)}) collective-permute-start(f32[2,32,256]{2,1,0:T(8,128)S(1)} %shard_map.99.refs_6_), channel_id=1, source_target_pairs={{31,29}} | collective-permute-start | bytes 196616 | tf_op jit(solution)/shard_map/ppermute | solution.py:271
  15.1 0.7 %collective-permute-start.17 = (f32[2,32,256]{2,1,0:T(8,128)S(1)}, f32[2,32,256]{2,1,0:T(8,128)S(1)}, u32[]{:S(2)}, u32[]{:S(2)}) collective-permute-start(f32[2,32,256]{2,1,0:T(8,128)S(1)} %shard_map.99.refs_6_), channel_id=1, source_target_pairs={{31,28}} | collective-permute-start | bytes 196616 | tf_op jit(solution)/shard_map/ppermute | solution.py:271
  15.9 12.4 %collective-permute-start.20 = (f32[2,32,128]{2,1,0:T(8,128)S(1)}, f32[2,32,128]{2,1,0:T(8,128)S(1)}, u32[]{:S(2)}, u32[]{:S(2)}) collective-permute-start(f32[2,32,128]{2,1,0:T(8,128)S(1)} %get-tuple-element.34), channel_id=1, source_target_pairs={{0,4},{4,0},{8,12},{12,8},{16,20},{20,16},{24,28},{28,24},{1,5},{5... | collective-permute-start | bytes 98312 | tf_op jit(solution)/shard_map/ppermute | solution.py:384
  30.0 5.1 %collective-permute-start.24 = (f32[4,32,1024]{2,1,0:T(8,128)S(1)}, f32[4,32,1024]{2,1,0:T(8,128)S(1)}, u32[]{:S(2)}, u32[]{:S(2)}) collective-permute-start(f32[4,32,1024]{2,1,0:T(8,128)S(1)} %get-tuple-element.45), channel_id=1, source_target_pairs={{0,4},{4,0},{8,12},{12,8},{16,20},{20,16},{24,28},{28,24},{1,5},{5... | collective-permute-start | bytes 1572872 | tf_op jit(solution)/shard_map/ppermute | solution.py:431
  34.0 9.2 %collective-permute-start.27 = (f32[4,32,1024]{2,1,0:T(8,128)S(1)}, f32[4,32,1024]{2,1,0:T(8,128)S(1)}, u32[]{:S(2)}, u32[]{:S(2)}) collective-permute-start(f32[4,32,1024]{2,1,0:T(8,128)S(1)} %get-tuple-element.52), channel_id=1, source_target_pairs={{0,4},{4,0},{8,12},{12,8},{16,20},{20,16},{24,28},{28,24},{1,5},{5... | collective-permute-start | bytes 1572872 | tf_op jit(solution)/shard_map/ppermute | solution.py:431
  34.5 16.1 %collective-permute-start.21 = (f32[4,32,1152]{2,1,0:T(8,128)S(1)}, f32[4,32,1152]{2,1,0:T(8,128)S(1)}, u32[]{:S(2)}, u32[]{:S(2)}) collective-permute-start(f32[4,32,1152]{2,1,0:T(8,128)S(1)} %get-tuple-element.41), channel_id=1, source_target_pairs={{0,4},{4,0},{8,12},{12,8},{16,20},{20,16},{24,28},{28,24},{1,5},{5... | collective-permute-start | bytes 1769480 | tf_op jit(solution)/shard_map/ppermute | solution.py:431
  34.6 14.9 %collective-permute-start.30 = (f32[4,32,1024]{2,1,0:T(8,128)S(1)}, f32[4,32,1024]{2,1,0:T(8,128)S(1)}, u32[]{:S(2)}, u32[]{:S(2)}) collective-permute-start(f32[4,32,1024]{2,1,0:T(8,128)S(1)} %get-tuple-element.54), channel_id=1, source_target_pairs={{0,4},{4,0},{8,12},{12,8},{16,20},{20,16},{24,28},{28,24},{1,5},{5... | collective-permute-start | bytes 1572872 | tf_op jit(solution)/shard_map/ppermute | solution.py:431
  35.1 17.1 %collective-permute-start.25 = (f32[2,32,1024]{2,1,0:T(8,128)S(1)}, f32[2,32,1024]{2,1,0:T(8,128)S(1)}, u32[]{:S(2)}, u32[]{:S(2)}) collective-permute-start(f32[2,32,1024]{2,1,0:T(8,128)S(1)} %slice.82), channel_id=1, source_target_pairs={{0,16},{4,20},{8,24},{12,28},{16,0},{20,4},{24,8},{28,12},{1,17},{... | collective-permute-start | bytes 786440 | tf_op jit(solution)/shard_map/ppermute | solution.py:251
  43.3 13.4 %collective-permute-start.28 = (f32[2,32,1024]{2,1,0:T(8,128)S(1)}, f32[2,32,1024]{2,1,0:T(8,128)S(1)}, u32[]{:S(2)}, u32[]{:S(2)}) collective-permute-start(f32[2,32,1024]{2,1,0:T(8,128)S(1)} %slice_bitcast_fusion.2), channel_id=1, source_target_pairs={{0,8},{4,12},{8,0},{12,4},{16,24},{20,28},{24,16},{28,20},{1,9},{5... | collective-permute-start | bytes 786440 | tf_op jit(solution)/shard_map/ppermute | solution.py:251
  49.7 19.3 %copy-start = (f32[2,32,2048]{2,1,0:T(8,128)S(1)}, f32[2,32,2048]{2,1,0:T(8,128)}, u32[]{:S(2)}) copy-start(f32[2,32,2048]{2,1,0:T(8,128)} %param.11) | copy-start | bytes 1572868
  49.7 9.1 %collective-permute-start.31 = (f32[2,32,1024]{2,1,0:T(8,128)S(1)}, f32[2,32,1024]{2,1,0:T(8,128)S(1)}, u32[]{:S(2)}, u32[]{:S(2)}) collective-permute-start(f32[2,32,1024]{2,1,0:T(8,128)S(1)} %slice.90), channel_id=1, source_target_pairs={{0,16},{4,20},{8,24},{12,28},{16,0},{20,4},{24,8},{28,12},{1,17},{... | collective-permute-start | bytes 786440 | tf_op jit(solution)/shard_map/ppermute | solution.py:251
  50.7 12.3 %collective-permute-start.22 = (f32[2,32,1152]{2,1,0:T(8,128)S(1)}, f32[2,32,1152]{2,1,0:T(8,128)S(1)}, u32[]{:S(2)}, u32[]{:S(2)}) collective-permute-start(f32[2,32,1152]{2,1,0:T(8,128)S(1)} %slice_bitcast_fusion), channel_id=1, source_target_pairs={{0,8},{4,12},{8,0},{12,4},{16,24},{20,28},{24,16},{28,20},{1,9},{5... | collective-permute-start | bytes 884744 | tf_op jit(solution)/shard_map/ppermute | solution.py:251
  52.2 13.6 %collective-permute-start.26 = (f32[32,1024]{1,0:T(8,128)S(1)}, f32[32,1024]{1,0:T(8,128)S(1)}, u32[]{:S(2)}, u32[]{:S(2)}) collective-permute-start(f32[32,1024]{1,0:T(8,128)S(1)} %slice_bitcast_fusion.10), channel_id=1, source_target_pairs={{0,8},{4,12},{8,0},{12,4},{16,24},{20,28},{24,16},{28,20},{1,9},{5... | collective-permute-start | bytes 393224 | tf_op jit(solution)/shard_map/ppermute | solution.py:251
  56.8 9.1 %collective-permute-start.29 = (f32[32,1024]{1,0:T(8,128)S(1)}, f32[32,1024]{1,0:T(8,128)S(1)}, u32[]{:S(2)}, u32[]{:S(2)}) collective-permute-start(f32[32,1024]{1,0:T(8,128)S(1)} %slice_bitcast_fusion.8), channel_id=1, source_target_pairs={{0,16},{4,20},{8,24},{12,28},{16,0},{20,4},{24,8},{28,12},{1,17},{... | collective-permute-start | bytes 393224 | tf_op jit(solution)/shard_map/ppermute | solution.py:251
  58.9 8.9 %collective-permute-start.32 = (f32[32,1024]{1,0:T(8,128)S(1)}, f32[32,1024]{1,0:T(8,128)S(1)}, u32[]{:S(2)}, u32[]{:S(2)}) collective-permute-start(f32[32,1024]{1,0:T(8,128)S(1)} %slice_bitcast_fusion.6), channel_id=1, source_target_pairs={{0,8},{4,12},{8,0},{12,4},{16,24},{20,28},{24,16},{28,20},{1,9},{5... | collective-permute-start | bytes 393224 | tf_op jit(solution)/shard_map/ppermute | solution.py:251
  63.1 5.2 %collective-permute-start.23 = (f32[32,1152]{1,0:T(8,128)S(1)}, f32[32,1152]{1,0:T(8,128)S(1)}, u32[]{:S(2)}, u32[]{:S(2)}) collective-permute-start(f32[32,1152]{1,0:T(8,128)S(1)} %slice_bitcast_fusion.4), channel_id=1, source_target_pairs={{0,16},{4,20},{8,24},{12,28},{16,0},{20,4},{24,8},{28,12},{1,17},{... | collective-permute-start | bytes 442376 | tf_op jit(solution)/shard_map/ppermute | solution.py:251

commit v5 on v4

--- a/solution.py
+++ b/solution.py
@@ -146,22 +146,22 @@
                     outs[t][...] = source[:, :, t * width : (t + 1) * width]
 
 
-def when_kernel(last, members, skip, kernel, *refs):
-    inside = lax.axis_index("row") >= lax.axis_size("row") - members
-
-    @pl.when(inside if last else jnp.logical_not(inside))
+def when_kernel(late, members, skip, kernel, *refs):
+    inside = lax.axis_index("row") >= members
+
+    @pl.when(inside if late else jnp.logical_not(inside))
     def _():
         kernel(*refs[skip[0] : skip[1]], *refs[skip[2] :])
 
 
-def prepare_kernel(chunk, chunks, members, busy, late, skip, *refs):
+def prepare_kernel(chunk, chunks, members, who, invert, skip, *refs):
     trail, high, low, room, sems = refs[skip:]
     devices, columns = room.shape[0], room.shape[3]
-    waits = jnp.bool_(False)
-    for k in busy:
-        waits = waits | leads(k, members)
-
-    @pl.when(waits if late else jnp.logical_not(waits))
+    wanted = jnp.bool_(False)
+    for k in who:
+        wanted = wanted | leads(k, members)
+
+    @pl.when(jnp.logical_not(wanted) if invert else wanted)
     def _():
         copies = []
         for i in range(devices):
@@ -278,9 +278,12 @@
 
     pieces = {}
 
+    rounds = {1: [(k, k - 1) for k in range(1, cols, 2)]}
+    rounds[2] = [(k, g) for k in range(1, cols) for g in near(k) if (k, g) not in rounds[1]]
+
     def bring(number):
         for t in range(members):
-            moves = [(k, near(k)[number - 1]) for k in range(1, cols) if len(near(k)) >= number]
+            moves = rounds[number]
             if moves:
                 arrived = send(upper_block, [(flat(members * g + t, k), leader(k)) for k, g in moves])
                 for k, g in moves:
@@ -319,13 +322,12 @@
         arrived.append(send(value, [(leader(g), flat(members * g + members - 1, k)) for g, k in places]))
         sources.append(places)
 
-    busy = []
     ready = []
 
-    def prepare(place, source):
+    def prepare(source, who, invert=False):
         nonlocal ready
         ready = local_call(
-            functools.partial(prepare_kernel, 0, CHUNKS, members, busy, place == 1, len(ready)),
+            functools.partial(prepare_kernel, 0, CHUNKS, members, who, invert, len(ready)),
             [((rows, 2 * width, columns), jnp.bfloat16)] * 2,
             ready,
             [source],
@@ -335,7 +337,7 @@
 
     for step in range(cols):
         final = step + 1 == cols
-        terms = [held[g] for g in range(step) if step in far(g)]
+        terms = [held[g, step] for g in range(step) if step in far(g)]
         factors = []
         for g in near(step):
             factors += [passed[g, step], *(pieces[step, g, t] for t in range(members))]
@@ -357,20 +359,23 @@
                 [(part, jnp.float32)],
                 [*(early[step, k] for k in far(step)), *upper_rows],
             )[0]
-            held[step] = send(term, [(flat(members * step + members - 1, k), leader(k)) for k in far(step)])
+            for k in far(step):
+                held[step, k] = send(term, [(flat(members * step + members - 1, k), leader(k))])
         if step == min(1, cols - 2):
-            prepare(0, after(upper_trail, result))
+            prepare(after(upper_trail, result), list(range(2, cols)), True)
         if step == cols - 2:
             arrived += [result, *early.values()]
             sources += [[(k, k) for k in range(cols - 1)], *([place] for place in early)]
-            for s in range(1, cols):
+            for s in range(cols - 1, 0, -1):
                 places = [(k, (k + s) % cols) for k in range(cols - 1)]
                 spread(result, [place for place in places if place not in early])
+            prepare(after(upper_trail, result), list(range(2, cols - 1)))
 
     arrived += [results[-1]]
     sources += [[(cols - 1, cols - 1)]]
     for s in range(1, cols):
         spread(results[-1], [(cols - 1, (cols - 1 + s) % cols)])
+    prepare(after(upper_trail, results[-1]), [k for k in [cols - 1] if k > 1])
     parts = local_call(
         functools.partial(merge_kernel, members, sources),
         [((2, observers, width), jnp.float32)] * members,

time: 70.2 us -> 69.7 us (level)
  starting transfers between devices: 50.2 us -> 49.3 us
    ppermute x8, starting transfers between devices: 27.9 us -> 26.4 us  [halve(): lax.ppermute(high, 'row', [(i, i ^ 1 << bit) for i in range(rows)])]
    ppermute x17 -> x18, starting transfers between devices: 11.3 us -> 12 us  [send(): return lax.ppermute(value, ('row', 'col'), pairs)]
    pallas_call x12 -> x14, Pallas kernels: 10.6 us -> 10.9 us  [local_call(): pl.pallas_call(kernel, in_specs=[VMEM] * len(near) + [ANY] * len(far), ou...]
  transfers between devices with their start and end apart: 33 -> 34, of which waited for: 6 -> 6; matrix products, arithmetic and copies ran while one was open for 1% -> 1% of each run, Pallas kernels for 13% -> 13%
where the time goes in v5:
time: 69.7 us; the launch traced here: 69.3 us
  starting transfers between devices  49.3 us (71%)
  Pallas kernels  10.9 us (16%)
  waiting for transfers between devices  5.76 us (8%)
  other arithmetic  1.34 us (2%)
  between operations  1.19 us (2%)
  local copies, waits for them, and re-layouts  0.76 us (1%)
    ppermute x8, starting transfers between devices, halve(): lax.ppermute(high, 'row', [(i, i ^ 1 << bit) for i in range(rows)])  26.4 us
    ppermute x18, starting transfers between devices, send(): return lax.ppermute(value, ('row', 'col'), pairs)  12 us
    pallas_call x14, Pallas kernels, local_call(): pl.pallas_call(kernel, in_specs=[VMEM] * len(near) + [ANY] * len(far), ou...  10.9 us
    ppermute x1, starting transfers between devices, on_device(): candidates.append(lax.ppermute(parts[t], 'row', pairs))  8.68 us
    ppermute x8, waiting for transfers between devices, halve(): lax.ppermute(high, 'row', [(i, i ^ 1 << bit) for i in range(rows)])  4.6 us
  transfers between devices with their start and end apart: 34, of which 6 were waited for; matrix products, arithmetic and copies ran while one was open for 1% of the time, Pallas kernels for 13%

profile of v5, /device:TPU:0, one launch (start us, length us, event | category | flops | bytes accessed | tf_op | source)
XLA Modules:
  0.0 69.3 jit_solution(4666334204351010379)
XLA Ops:
  0.6 0.6 collective-permute-start.2
  1.2 0.7 collective-permute-start.8
  1.9 0.7 collective-permute-start.7
  2.5 0.1 collective-permute-start.1
  2.6 0.5 collective-permute-start
  3.1 1.1 %collective-permute-done.refs_0_ = f32[2,32,128]{2,1,0:T(8,128)S(1)} collective-permute-done((f32[2,32,128]{2,1,0:T(8,128)}, f32[2,32,128]{2,1,0:T(8,128)S(1)}, u32[]{:S(2)}, u32[]{:S(2)}) %collective-permute-start) | collective-permute-done | bytes 32800 | tf_op jit(solution)/shard_map/ppermute | solution.py:297
  4.2 0.7 collective-permute-start.11
  4.9 0.7 collective-permute-start.10
  5.6 1.1 %shard_map.94 = (f32[2,32,128]{2,1,0:T(8,128)S(1)}, f32[2,128,128]{2,1,0:T(8,128)S(1)}, f32[2,128]{1,0:T(2,128)S(1)}, s32[1,128]{1,0:T(1,128)S(1)}, f32[2,128,256]{2,1,0:T(8,128)S(1)}) custom-call(f32[2,32,128]{2,1,0:T(8,128)} %refs_0_.1, f32[2,128,128]{2,1,0:T(8,128)} %refs_1_.1, f32[2,128]{1,0:T(2,128)} %refs_2_.1, s32[1,128]{1,0:T(1,128)} %bitcast.65, ...), custom_call_target="tpu_custom_call" | custom-call | tf_op jit(solution)/shard_map/pallas_call | solution.py:56
  6.7 0.7 collective-permute-start.6
  7.4 0.7 collective-permute-start.4
  8.1 0.7 collective-permute-start.3
  8.8 0.7 collective-permute-start.9
  9.5 0.7 collective-permute-start.5
  10.2 0.7 collective-permute-start.17
  10.9 0.7 collective-permute-start.15
  11.6 0.7 collective-permute-start.16
  12.3 0.7 collective-permute-start.14
  13.0 0.7 collective-permute-start.13
  13.7 0.7 collective-permute-start.12
  14.4 0.7 collective-permute-start.20
  15.1 0.7 collective-permute-start.19
  15.7 0.7 collective-permute-start.18
  16.5 0.1 shard_map.100
  16.6 8.7 %collective-permute-start.21 = (f32[2,32,128]{2,1,0:T(8,128)S(1)}, f32[2,32,128]{2,1,0:T(8,128)S(1)}, u32[]{:S(2)}, u32[]{:S(2)}) collective-permute-start(f32[2,32,128]{2,1,0:T(8,128)S(1)} %get-tuple-element.40), channel_id=1, source_target_pairs={{0,4},{4,0},{8,12},{12,8},{16,20},{20,16},{24,28},{28,24},{1,5},{5... | collective-permute-start | bytes 98312 | tf_op jit(solution)/shard_map/ppermute | solution.py:389
  25.3 3.7 %shard_map.101 = (bf16[8,256,1024]{2,1,0:T(8,128)(2,1)S(1)}, bf16[8,256,1024]{2,1,0:T(8,128)(2,1)S(1)}) custom-call(f32[2,128,16384]{2,1,0:T(8,128)} %refs_7_.1), custom_call_target="tpu_custom_call" | custom-call | tf_op jit(solution)/shard_map/pallas_call | solution.py:56
  28.9 0.1 shard_map.102
  29.1 0.9 %shard_map.104 = (f32[2,32,128]{2,1,0:T(8,128)S(1)}, f32[4,32,1152]{2,1,0:T(8,128)S(1)}, f32[4,32,1024]{2,1,0:T(8,128)S(1)}, f32[2,32,128]{2,1,0:T(8,128)}) custom-call(f32[2,128]{1,0:T(2,128)S(1)} %get-tuple-element.35.currents.refs_0_, s32[1,128]{1,0:T(1,128)S(1)} %get-tuple-element.36.owner.refs_1_, f32[2,32,128]{2,1,0:T(8,128)S(1)} %collective-permute-done.21.refs_0_, ...), custom_call_target="tpu_custom_call" | custom-call | tf_op jit(solution)/shard_map/pallas_call | solution.py:56
  30.0 0.8 %shard_map.105 = (f32[4,32,1152]{2,1,0:T(8,128)S(1)}, f32[4,32,1024]{2,1,0:T(8,128)S(1)}) custom-call(f32[2,128]{1,0:T(2,128)S(1)} %get-tuple-element.35.currents.refs_0_, s32[1,128]{1,0:T(1,128)S(1)} %get-tuple-element.36.owner.refs_1_, f32[2,32,128]{2,1,0:T(8,128)S(1)} %get-tuple-element.58.refs_0_.refs_2_, ...), custom_call_target="tpu_custom_call" | custom-call | tf_op jit(solution)/shard_map/pallas_call | solution.py:56
  30.9 0.1 collective-permute-start.25
  31.0 3.8 %shard_map.106 = (f32[4,32,1024]{2,1,0:T(8,128)S(1)}, f32[4,32,1024]{2,1,0:T(8,128)S(1)}, f32[4,32,1024]{2,1,0:T(8,128)S(1)}, f32[4,32,1024]{2,1,0:T(8,128)S(1)}) custom-call(f32[2,128]{1,0:T(2,128)S(1)} %get-tuple-element.35.currents.refs_0_, s32[1,128]{1,0:T(1,128)S(1)} %get-tuple-element.36.owner.refs_1_, ...), custom_call_target="tpu_custom_call" | custom-call | tf_op jit(solution)/shard_map/pallas_call | solution.py:56
  34.8 0.3 shard_map.107
  35.1 0.5 collective-permute-start.28
  35.7 0.4 collective-permute-start.31
  36.2 6.4 %collective-permute-start.26 = (f32[2,32,1024]{2,1,0:T(8,128)S(1)}, f32[2,32,1024]{2,1,0:T(8,128)S(1)}, u32[]{:S(2)}, u32[]{:S(2)}) collective-permute-start(f32[2,32,1024]{2,1,0:T(8,128)S(1)} %slice.82), channel_id=1, source_target_pairs={{0,16},{4,20},{8,24},{12,28},{16,0},{20,4},{24,8},{28,12},{1,17},{... | collective-permute-start | bytes 786440 | tf_op jit(solution)/shard_map/ppermute | solution.py:251
  42.7 6.3 %collective-permute-start.29 = (f32[2,32,1024]{2,1,0:T(8,128)S(1)}, f32[2,32,1024]{2,1,0:T(8,128)S(1)}, u32[]{:S(2)}, u32[]{:S(2)}) collective-permute-start(f32[2,32,1024]{2,1,0:T(8,128)S(1)} %slice_bitcast_fusion.2), channel_id=1, source_target_pairs={{0,8},{4,12},{8,0},{12,4},{16,24},{20,28},{24,16},{28,20},{1,9},{5... | collective-permute-start | bytes 786440 | tf_op jit(solution)/shard_map/ppermute | solution.py:251
  49.2 0.9 %collective-permute-start.32 = (f32[2,32,1024]{2,1,0:T(8,128)S(1)}, f32[2,32,1024]{2,1,0:T(8,128)S(1)}, u32[]{:S(2)}, u32[]{:S(2)}) collective-permute-start(f32[2,32,1024]{2,1,0:T(8,128)S(1)} %slice.90), channel_id=1, source_target_pairs={{0,16},{4,20},{8,24},{12,28},{16,0},{20,4},{24,8},{28,12},{1,17},{... | collective-permute-start | bytes 786440 | tf_op jit(solution)/shard_map/ppermute | solution.py:251
  50.2 1.5 %collective-permute-start.23 = (f32[2,32,1152]{2,1,0:T(8,128)S(1)}, f32[2,32,1152]{2,1,0:T(8,128)S(1)}, u32[]{:S(2)}, u32[]{:S(2)}) collective-permute-start(f32[2,32,1152]{2,1,0:T(8,128)S(1)} %slice_bitcast_fusion), channel_id=1, source_target_pairs={{0,8},{4,12},{8,0},{12,4},{16,24},{20,28},{24,16},{28,20},{1,9},{5... | collective-permute-start | bytes 884744 | tf_op jit(solution)/shard_map/ppermute | solution.py:251
  51.7 4.4 %collective-permute-start.27 = (f32[32,1024]{1,0:T(8,128)S(1)}, f32[32,1024]{1,0:T(8,128)S(1)}, u32[]{:S(2)}, u32[]{:S(2)}) collective-permute-start(f32[32,1024]{1,0:T(8,128)S(1)} %slice_bitcast_fusion.10), channel_id=1, source_target_pairs={{0,8},{4,12},{8,0},{12,4},{16,24},{20,28},{24,16},{28,20},{1,9},{5... | collective-permute-start | bytes 393224 | tf_op jit(solution)/shard_map/ppermute | solution.py:251
  56.3 2.0 %collective-permute-start.30 = (f32[32,1024]{1,0:T(8,128)S(1)}, f32[32,1024]{1,0:T(8,128)S(1)}, u32[]{:S(2)}, u32[]{:S(2)}) collective-permute-start(f32[32,1024]{1,0:T(8,128)S(1)} %slice_bitcast_fusion.8), channel_id=1, source_target_pairs={{0,16},{4,20},{8,24},{12,28},{16,0},{20,4},{24,8},{28,12},{1,17},{... | collective-permute-start | bytes 393224 | tf_op jit(solution)/shard_map/ppermute | solution.py:251
  58.4 3.4 %collective-permute-start.33 = (f32[32,1024]{1,0:T(8,128)S(1)}, f32[32,1024]{1,0:T(8,128)S(1)}, u32[]{:S(2)}, u32[]{:S(2)}) collective-permute-start(f32[32,1024]{1,0:T(8,128)S(1)} %slice_bitcast_fusion.6), channel_id=1, source_target_pairs={{0,8},{4,12},{8,0},{12,4},{16,24},{20,28},{24,16},{28,20},{1,9},{5... | collective-permute-start | bytes 393224 | tf_op jit(solution)/shard_map/ppermute | solution.py:251
  61.8 0.8 %collective-permute-done.23 = f32[2,32,1152]{2,1,0:T(8,128)S(1)} collective-permute-done((f32[2,32,1152]{2,1,0:T(8,128)S(1)}, f32[2,32,1152]{2,1,0:T(8,128)S(1)}, u32[]{:S(2)}, u32[]{:S(2)}) %collective-permute-start.23) | collective-permute-done | bytes 294944 | tf_op jit(solution)/shard_map/ppermute | solution.py:251
  62.6 1.3 %collective-permute-start.24 = (f32[32,1152]{1,0:T(8,128)S(1)}, f32[32,1152]{1,0:T(8,128)S(1)}, u32[]{:S(2)}, u32[]{:S(2)}) collective-permute-start(f32[32,1152]{1,0:T(8,128)S(1)} %slice_bitcast_fusion.4), channel_id=1, source_target_pairs={{0,16},{4,20},{8,24},{12,28},{16,0},{20,4},{24,8},{28,12},{1,17},{... | collective-permute-start | bytes 442376 | tf_op jit(solution)/shard_map/ppermute | solution.py:251
  63.9 1.4 %collective-permute-done.27 = f32[32,1024]{1,0:T(8,128)S(1)} collective-permute-done((f32[32,1024]{1,0:T(8,128)S(1)}, f32[32,1024]{1,0:T(8,128)S(1)}, u32[]{:S(2)}, u32[]{:S(2)}) %collective-permute-start.27) | collective-permute-done | bytes 131104 | tf_op jit(solution)/shard_map/ppermute | solution.py:251
  65.4 1.9 %collective-permute-done.33 = f32[32,1024]{1,0:T(8,128)S(1)} collective-permute-done((f32[32,1024]{1,0:T(8,128)S(1)}, f32[32,1024]{1,0:T(8,128)S(1)}, u32[]{:S(2)}, u32[]{:S(2)}) %collective-permute-start.33) | collective-permute-done | bytes 131104 | tf_op jit(solution)/shard_map/ppermute | solution.py:251
  67.3 0.5 collective-permute-done.24
  67.8 0.6 slice_reduce_fusion
  68.5 0.9 %maximum_subtract_fusion = f32[2,32,2048]{2,1,0:T(8,128)} fusion(f32[2,32,2048]{2,1,0:T(8,128)S(1)} %copy-done, f32[1,32,1024]{2,1,0:T(8,128)S(1)} %fusion.4, f32[1,32,1024]{2,1,0:T(8,128)S(1)} %fusion.6, f32[1,32,1024]{2,1,0:T(8,128)S(1)} %fusion.8, f32[1,32,1024]{2,1,0:T(8,128)S(1)} %slice_bitcast_fusion.12), kind=kLoop, calls=%fused_computation | loop fusion | flops 524288 | bytes 1572864 | tf_op jit(solution)/shard_map/sub | solution.py:448
  (59 shorter events, 1.0 us)
Async XLA Ops:
  0.6 6.1 %collective-permute-start.2 = (f32[2,128,256]{2,1,0:T(8,128)}, f32[2,128,256]{2,1,0:T(8,128)S(1)}, u32[]{:S(2)}, u32[]{:S(2)}) collective-permute-start(f32[2,128,256]{2,1,0:T(8,128)} %refs_4_.1), channel_id=1, source_target_pairs={{0,4},{4,0},{8,12},{12,8},{16,20},{20,16},{24,28},{28,24},{1,5},{5... | collective-permute-start | bytes 786440 | tf_op jit(solution)/shard_map/ppermute | solution.py:299
  1.2 6.2 %collective-permute-start.8 = (f32[2,128,256]{2,1,0:T(8,128)}, f32[2,128,256]{2,1,0:T(8,128)S(1)}, u32[]{:S(2)}, u32[]{:S(2)}) collective-permute-start(f32[2,128,256]{2,1,0:T(8,128)} %refs_4_.1), channel_id=1, source_target_pairs={{5,13},{23,31}} | collective-permute-start | bytes 786440 | tf_op jit(solution)/shard_map/ppermute | solution.py:271
  1.9 6.2 %collective-permute-start.7 = (f32[2,128,256]{2,1,0:T(8,128)}, f32[2,128,256]{2,1,0:T(8,128)S(1)}, u32[]{:S(2)}, u32[]{:S(2)}) collective-permute-start(f32[2,128,256]{2,1,0:T(8,128)} %refs_4_.1), channel_id=1, source_target_pairs={{1,13},{19,31}} | collective-permute-start | bytes 786440 | tf_op jit(solution)/shard_map/ppermute | solution.py:271
  2.5 2.3 %collective-permute-start.1 = (f32[2,128,128]{2,1,0:T(8,128)}, f32[2,128,128]{2,1,0:T(8,128)S(1)}, u32[]{:S(2)}, u32[]{:S(2)}) collective-permute-start(f32[2,128,128]{2,1,0:T(8,128)} %refs_1_.1), channel_id=1, source_target_pairs={{0,4},{4,0},{8,12},{12,8},{16,20},{20,16},{24,28},{28,24},{1,5},{5... | collective-permute-start | bytes 393224 | tf_op jit(solution)/shard_map/ppermute | solution.py:298
  2.6 1.6 %collective-permute-start = (f32[2,32,128]{2,1,0:T(8,128)}, f32[2,32,128]{2,1,0:T(8,128)S(1)}, u32[]{:S(2)}, u32[]{:S(2)}) collective-permute-start(f32[2,32,128]{2,1,0:T(8,128)} %refs_0_.1), channel_id=1, source_target_pairs={{0,4},{4,0},{8,12},{12,8},{16,20},{20,16},{24,28},{28,24},{1,5},{5... | collective-permute-start | bytes 98312 | tf_op jit(solution)/shard_map/ppermute | solution.py:297
  4.2 6.7 %collective-permute-start.11 = (f32[2,128,256]{2,1,0:T(8,128)}, f32[2,128,256]{2,1,0:T(8,128)S(1)}, u32[]{:S(2)}, u32[]{:S(2)}) collective-permute-start(f32[2,128,256]{2,1,0:T(8,128)} %refs_4_.1), channel_id=1, source_target_pairs={{14,22},{15,31}} | collective-permute-start | bytes 786440 | tf_op jit(solution)/shard_map/ppermute | solution.py:271
  4.9 6.7 %collective-permute-start.10 = (f32[2,128,256]{2,1,0:T(8,128)}, f32[2,128,256]{2,1,0:T(8,128)S(1)}, u32[]{:S(2)}, u32[]{:S(2)}) collective-permute-start(f32[2,128,256]{2,1,0:T(8,128)} %refs_4_.1), channel_id=1, source_target_pairs={{10,22},{11,31}} | collective-permute-start | bytes 786440 | tf_op jit(solution)/shard_map/ppermute | solution.py:271
  6.7 2.0 %collective-permute-start.6 = (f32[2,32,256]{2,1,0:T(8,128)S(1)}, f32[2,32,256]{2,1,0:T(8,128)S(1)}, u32[]{:S(2)}, u32[]{:S(2)}) collective-permute-start(f32[2,32,256]{2,1,0:T(8,128)S(1)} %shard_map.95.refs_9_), channel_id=1, source_target_pairs={{4,13}} | collective-permute-start | bytes 196616 | tf_op jit(solution)/shard_map/ppermute | solution.py:271
  7.4 2.1 %collective-permute-start.4 = (f32[2,32,256]{2,1,0:T(8,128)S(1)}, f32[2,32,256]{2,1,0:T(8,128)S(1)}, u32[]{:S(2)}, u32[]{:S(2)}) collective-permute-start(f32[2,32,256]{2,1,0:T(8,128)S(1)} %shard_map.95.refs_9_), channel_id=1, source_target_pairs={{4,7}} | collective-permute-start | bytes 196616 | tf_op jit(solution)/shard_map/ppermute | solution.py:271
  8.1 1.4 %collective-permute-start.3 = (f32[2,32,256]{2,1,0:T(8,128)S(1)}, f32[2,32,256]{2,1,0:T(8,128)S(1)}, u32[]{:S(2)}, u32[]{:S(2)}) collective-permute-start(f32[2,32,256]{2,1,0:T(8,128)S(1)} %shard_map.95.refs_9_), channel_id=1, source_target_pairs={{4,6}} | collective-permute-start | bytes 196616 | tf_op jit(solution)/shard_map/ppermute | solution.py:271
  8.8 2.8 %collective-permute-start.9 = (f32[2,32,256]{2,1,0:T(8,128)S(1)}, f32[2,32,256]{2,1,0:T(8,128)S(1)}, u32[]{:S(2)}, u32[]{:S(2)}) collective-permute-start(f32[2,32,256]{2,1,0:T(8,128)S(1)} %shard_map.97.refs_10_), channel_id=1, source_target_pairs={{13,22}} | collective-permute-start | bytes 196616 | tf_op jit(solution)/shard_map/ppermute | solution.py:271
  9.5 2.1 %collective-permute-start.5 = (f32[2,32,256]{2,1,0:T(8,128)S(1)}, f32[2,32,256]{2,1,0:T(8,128)S(1)}, u32[]{:S(2)}, u32[]{:S(2)}) collective-permute-start(f32[2,32,256]{2,1,0:T(8,128)S(1)} %shard_map.96), channel_id=1, source_target_pairs={{6,22}} | collective-permute-start | bytes 196616 | tf_op jit(solution)/shard_map/ppermute | solution.py:271
  10.2 3.4 %collective-permute-start.17 = (f32[2,32,256]{2,1,0:T(8,128)S(1)}, f32[2,32,256]{2,1,0:T(8,128)S(1)}, u32[]{:S(2)}, u32[]{:S(2)}) collective-permute-start(f32[2,32,256]{2,1,0:T(8,128)S(1)} %shard_map.97.refs_10_), channel_id=1, source_target_pairs={{13,31}} | collective-permute-start | bytes 196616 | tf_op jit(solution)/shard_map/ppermute | solution.py:271
  10.9 3.4 %collective-permute-start.15 = (f32[2,32,256]{2,1,0:T(8,128)S(1)}, f32[2,32,256]{2,1,0:T(8,128)S(1)}, u32[]{:S(2)}, u32[]{:S(2)}) collective-permute-start(f32[2,32,256]{2,1,0:T(8,128)S(1)} %shard_map.96), channel_id=1, source_target_pairs={{7,31}} | collective-permute-start | bytes 196616 | tf_op jit(solution)/shard_map/ppermute | solution.py:271
  11.6 2.7 %collective-permute-start.16 = (f32[2,32,256]{2,1,0:T(8,128)S(1)}, f32[2,32,256]{2,1,0:T(8,128)S(1)}, u32[]{:S(2)}, u32[]{:S(2)}) collective-permute-start(f32[2,32,256]{2,1,0:T(8,128)S(1)} %shard_map.98.refs_0_), channel_id=1, source_target_pairs={{22,31}} | collective-permute-start | bytes 196616 | tf_op jit(solution)/shard_map/ppermute | solution.py:271
  12.3 3.4 %collective-permute-start.14 = (f32[2,32,256]{2,1,0:T(8,128)S(1)}, f32[2,32,256]{2,1,0:T(8,128)S(1)}, u32[]{:S(2)}, u32[]{:S(2)}) collective-permute-start(f32[2,32,256]{2,1,0:T(8,128)S(1)} %shard_map.98.refs_0_), channel_id=1, source_target_pairs={{4,5},{13,14},{22,23}} | collective-permute-start | bytes 196616 | tf_op jit(solution)/shard_map/ppermute | solution.py:271
  13.0 3.4 %collective-permute-start.13 = (f32[2,32,256]{2,1,0:T(8,128)S(1)}, f32[2,32,256]{2,1,0:T(8,128)S(1)}, u32[]{:S(2)}, u32[]{:S(2)}) collective-permute-start(f32[2,32,256]{2,1,0:T(8,128)S(1)} %shard_map.98.refs_0_), channel_id=1, source_target_pairs={{13,15},{22,20}} | collective-permute-start | bytes 196616 | tf_op jit(solution)/shard_map/ppermute | solution.py:271
  13.7 2.8 %collective-permute-start.12 = (f32[2,32,256]{2,1,0:T(8,128)S(1)}, f32[2,32,256]{2,1,0:T(8,128)S(1)}, u32[]{:S(2)}, u32[]{:S(2)}) collective-permute-start(f32[2,32,256]{2,1,0:T(8,128)S(1)} %shard_map.98.refs_0_), channel_id=1, source_target_pairs={{13,12},{22,21}} | collective-permute-start | bytes 196616 | tf_op jit(solution)/shard_map/ppermute | solution.py:271
  14.4 2.1 %collective-permute-start.20 = (f32[2,32,256]{2,1,0:T(8,128)S(1)}, f32[2,32,256]{2,1,0:T(8,128)S(1)}, u32[]{:S(2)}, u32[]{:S(2)}) collective-permute-start(f32[2,32,256]{2,1,0:T(8,128)S(1)} %shard_map.99.refs_6_), channel_id=1, source_target_pairs={{31,30}} | collective-permute-start | bytes 196616 | tf_op jit(solution)/shard_map/ppermute | solution.py:271
  15.1 1.4 %collective-permute-start.19 = (f32[2,32,256]{2,1,0:T(8,128)S(1)}, f32[2,32,256]{2,1,0:T(8,128)S(1)}, u32[]{:S(2)}, u32[]{:S(2)}) collective-permute-start(f32[2,32,256]{2,1,0:T(8,128)S(1)} %shard_map.99.refs_6_), channel_id=1, source_target_pairs={{31,29}} | collective-permute-start | bytes 196616 | tf_op jit(solution)/shard_map/ppermute | solution.py:271
  15.7 0.7 %collective-permute-start.18 = (f32[2,32,256]{2,1,0:T(8,128)S(1)}, f32[2,32,256]{2,1,0:T(8,128)S(1)}, u32[]{:S(2)}, u32[]{:S(2)}) collective-permute-start(f32[2,32,256]{2,1,0:T(8,128)S(1)} %shard_map.99.refs_6_), channel_id=1, source_target_pairs={{31,28}} | collective-permute-start | bytes 196616 | tf_op jit(solution)/shard_map/ppermute | solution.py:271
  16.6 12.6 %collective-permute-start.21 = (f32[2,32,128]{2,1,0:T(8,128)S(1)}, f32[2,32,128]{2,1,0:T(8,128)S(1)}, u32[]{:S(2)}, u32[]{:S(2)}) collective-permute-start(f32[2,32,128]{2,1,0:T(8,128)S(1)} %get-tuple-element.40), channel_id=1, source_target_pairs={{0,4},{4,0},{8,12},{12,8},{16,20},{20,16},{24,28},{28,24},{1,5},{5... | collective-permute-start | bytes 98312 | tf_op jit(solution)/shard_map/ppermute | solution.py:389
  30.9 5.2 %collective-permute-start.25 = (f32[4,32,1024]{2,1,0:T(8,128)S(1)}, f32[4,32,1024]{2,1,0:T(8,128)S(1)}, u32[]{:S(2)}, u32[]{:S(2)}) collective-permute-start(f32[4,32,1024]{2,1,0:T(8,128)S(1)} %get-tuple-element.57), channel_id=1, source_target_pairs={{0,4},{4,0},{8,12},{12,8},{16,20},{20,16},{24,28},{28,24},{1,5},{5... | collective-permute-start | bytes 1572872 | tf_op jit(solution)/shard_map/ppermute | solution.py:436
  35.1 7.6 %collective-permute-start.28 = (f32[4,32,1024]{2,1,0:T(8,128)S(1)}, f32[4,32,1024]{2,1,0:T(8,128)S(1)}, u32[]{:S(2)}, u32[]{:S(2)}) collective-permute-start(f32[4,32,1024]{2,1,0:T(8,128)S(1)} %get-tuple-element.64), channel_id=1, source_target_pairs={{0,4},{4,0},{8,12},{12,8},{16,20},{20,16},{24,28},{28,24},{1,5},{5... | collective-permute-start | bytes 1572872 | tf_op jit(solution)/shard_map/ppermute | solution.py:436
  35.6 14.5 %collective-permute-start.22 = (f32[4,32,1152]{2,1,0:T(8,128)S(1)}, f32[4,32,1152]{2,1,0:T(8,128)S(1)}, u32[]{:S(2)}, u32[]{:S(2)}) collective-permute-start(f32[4,32,1152]{2,1,0:T(8,128)S(1)} %get-tuple-element.53), channel_id=1, source_target_pairs={{0,4},{4,0},{8,12},{12,8},{16,20},{20,16},{24,28},{28,24},{1,5},{5... | collective-permute-start | bytes 1769480 | tf_op jit(solution)/shard_map/ppermute | solution.py:436
  35.7 13.4 %collective-permute-start.31 = (f32[4,32,1024]{2,1,0:T(8,128)S(1)}, f32[4,32,1024]{2,1,0:T(8,128)S(1)}, u32[]{:S(2)}, u32[]{:S(2)}) collective-permute-start(f32[4,32,1024]{2,1,0:T(8,128)S(1)} %get-tuple-element.66), channel_id=1, source_target_pairs={{0,4},{4,0},{8,12},{12,8},{16,20},{20,16},{24,28},{28,24},{1,5},{5... | collective-permute-start | bytes 1572872 | tf_op jit(solution)/shard_map/ppermute | solution.py:436
  36.2 15.5 %collective-permute-start.26 = (f32[2,32,1024]{2,1,0:T(8,128)S(1)}, f32[2,32,1024]{2,1,0:T(8,128)S(1)}, u32[]{:S(2)}, u32[]{:S(2)}) collective-permute-start(f32[2,32,1024]{2,1,0:T(8,128)S(1)} %slice.82), channel_id=1, source_target_pairs={{0,16},{4,20},{8,24},{12,28},{16,0},{20,4},{24,8},{28,12},{1,17},{... | collective-permute-start | bytes 786440 | tf_op jit(solution)/shard_map/ppermute | solution.py:251
  42.7 13.5 %collective-permute-start.29 = (f32[2,32,1024]{2,1,0:T(8,128)S(1)}, f32[2,32,1024]{2,1,0:T(8,128)S(1)}, u32[]{:S(2)}, u32[]{:S(2)}) collective-permute-start(f32[2,32,1024]{2,1,0:T(8,128)S(1)} %slice_bitcast_fusion.2), channel_id=1, source_target_pairs={{0,8},{4,12},{8,0},{12,4},{16,24},{20,28},{24,16},{28,20},{1,9},{5... | collective-permute-start | bytes 786440 | tf_op jit(solution)/shard_map/ppermute | solution.py:251
  49.2 19.3 %copy-start = (f32[2,32,2048]{2,1,0:T(8,128)S(1)}, f32[2,32,2048]{2,1,0:T(8,128)}, u32[]{:S(2)}) copy-start(f32[2,32,2048]{2,1,0:T(8,128)} %param.11) | copy-start | bytes 1572868
  49.2 9.1 %collective-permute-start.32 = (f32[2,32,1024]{2,1,0:T(8,128)S(1)}, f32[2,32,1024]{2,1,0:T(8,128)S(1)}, u32[]{:S(2)}, u32[]{:S(2)}) collective-permute-start(f32[2,32,1024]{2,1,0:T(8,128)S(1)} %slice.90), channel_id=1, source_target_pairs={{0,16},{4,20},{8,24},{12,28},{16,0},{20,4},{24,8},{28,12},{1,17},{... | collective-permute-start | bytes 786440 | tf_op jit(solution)/shard_map/ppermute | solution.py:251
  50.2 12.3 %collective-permute-start.23 = (f32[2,32,1152]{2,1,0:T(8,128)S(1)}, f32[2,32,1152]{2,1,0:T(8,128)S(1)}, u32[]{:S(2)}, u32[]{:S(2)}) collective-permute-start(f32[2,32,1152]{2,1,0:T(8,128)S(1)} %slice_bitcast_fusion), channel_id=1, source_target_pairs={{0,8},{4,12},{8,0},{12,4},{16,24},{20,28},{24,16},{28,20},{1,9},{5... | collective-permute-start | bytes 884744 | tf_op jit(solution)/shard_map/ppermute | solution.py:251
  51.7 13.6 %collective-permute-start.27 = (f32[32,1024]{1,0:T(8,128)S(1)}, f32[32,1024]{1,0:T(8,128)S(1)}, u32[]{:S(2)}, u32[]{:S(2)}) collective-permute-start(f32[32,1024]{1,0:T(8,128)S(1)} %slice_bitcast_fusion.10), channel_id=1, source_target_pairs={{0,8},{4,12},{8,0},{12,4},{16,24},{20,28},{24,16},{28,20},{1,9},{5... | collective-permute-start | bytes 393224 | tf_op jit(solution)/shard_map/ppermute | solution.py:251
  56.3 9.1 %collective-permute-start.30 = (f32[32,1024]{1,0:T(8,128)S(1)}, f32[32,1024]{1,0:T(8,128)S(1)}, u32[]{:S(2)}, u32[]{:S(2)}) collective-permute-start(f32[32,1024]{1,0:T(8,128)S(1)} %slice_bitcast_fusion.8), channel_id=1, source_target_pairs={{0,16},{4,20},{8,24},{12,28},{16,0},{20,4},{24,8},{28,12},{1,17},{... | collective-permute-start | bytes 393224 | tf_op jit(solution)/shard_map/ppermute | solution.py:251
  58.4 8.9 %collective-permute-start.33 = (f32[32,1024]{1,0:T(8,128)S(1)}, f32[32,1024]{1,0:T(8,128)S(1)}, u32[]{:S(2)}, u32[]{:S(2)}) collective-permute-start(f32[32,1024]{1,0:T(8,128)S(1)} %slice_bitcast_fusion.6), channel_id=1, source_target_pairs={{0,8},{4,12},{8,0},{12,4},{16,24},{20,28},{24,16},{28,20},{1,9},{5... | collective-permute-start | bytes 393224 | tf_op jit(solution)/shard_map/ppermute | solution.py:251
  62.6 5.2 %collective-permute-start.24 = (f32[32,1152]{1,0:T(8,128)S(1)}, f32[32,1152]{1,0:T(8,128)S(1)}, u32[]{:S(2)}, u32[]{:S(2)}) collective-permute-start(f32[32,1152]{1,0:T(8,128)S(1)} %slice_bitcast_fusion.4), channel_id=1, source_target_pairs={{0,16},{4,20},{8,24},{12,28},{16,0},{20,4},{24,8},{28,12},{1,17},{... | collective-permute-start | bytes 442376 | tf_op jit(solution)/shard_map/ppermute | solution.py:251
